TPU v7x, 128 devices: a whole 4x4x4 slice. The times are simulated.
128 devices in a mesh: cells: 32 (over y, z, core), tiles: 4 (over x).
Axes of the slice: x: 4, y: 4, z: 4, core: 2. Of those that a mesh axis runs over, the one named last changes fastest.
Arguments:
- embeddings: bfloat16 [3, 32768, 256], P(None, 'cells'), may hold values from -6 to 6
- log_mass: float32 [3, 32768], P(None, 'cells'), may hold values from -1 to 1
- signatures: bfloat16 [32768, 256], P('cells'), may hold values from -6 to 6
- tile_list: int32 [2, 2, 4096], P(None, None, ('cells', 'tiles')), may hold values from -1 to 255, as said below
Outputs:
- early_fates: bfloat16 [32768, 256], P('cells')
- late_fates: bfloat16 [32768, 256], P('cells')
Inputs may be any that keep to these rules, and one draw needn't show every extreme that they name: `tile_list`: for each coupling, slots c * 128 to c * 128 + 127 belong to owner c (an index of cells). A live slot holds a source block of owner c (blocks c * 8 to c * 8 + 7) and a target block of owner c - 1, c or c + 1; an empty slot holds -1 in both rows. Within the slots of each device the live ones come first. No pair of blocks appears twice in a coupling, every source block and every target block appears in some live slot, and one owner in each coupling has all 128 slots live.
All inputs are finite; a program needn't handle non-finite values.
Results may differ from a plain program's by a relative error of at most 0.006.
Values may be sent and summed in bfloat16 or wider, within the bound.
No kernel may reach another device: no remote copies, remote signals or barrier semaphores. Data moves between devices by JAX's collectives and lax.ppermute only.
A program may use at most 64 MiB of HBM per device.

v0:
```python
import jax
import jax.numpy as jnp
from jax import lax
from jax.experimental import pallas as pl
from jax.experimental.pallas import tpu as pltpu
from jax.sharding import PartitionSpec as P

EMB = 256
BLOCK = 128
NBLK = 8
WIN = 3 * NBLK
CELLS = NBLK * BLOCK
EPS = 0.01
RHO = 1.0
LAM = RHO / (RHO + EPS)
BIG = 1e30

LOG2E = 1.4426950408889634
SCALE = LOG2E / (EMB * EPS)

QUAD = 4
STRIDE = WIN + QUAD
GROUPS = 2 * NBLK * STRIDE
TABLE = 512

VMEM = pl.BlockSpec(memory_space=pltpu.VMEM)
SMEM = pl.BlockSpec(memory_space=pltpu.SMEM)


def sibling(value):
    return lax.ppermute(value, "cells", [(c, c ^ 1) for c in range(lax.axis_size("cells"))])


def outward(value):
    count = lax.axis_size("cells")
    pairs = [(c, (c + 1 if c % 2 else c - 1) % count) for c in range(count)]
    return lax.ppermute(value, "cells", pairs)


def mirrored(value):
    count = lax.axis_size("tiles")
    return lax.ppermute(value, "tiles", [(t, count - 1 - t) for t in range(count)])


def call(kernel, outs, out_specs, in_specs, scratch=(), flops=10**9, mib=16):
    return pl.pallas_call(
        kernel,
        out_shape=outs,
        in_specs=in_specs,
        out_specs=out_specs,
        scratch_shapes=list(scratch),
        compiler_params=pltpu.CompilerParams(vmem_limit_bytes=mib << 20),
        cost_estimate=pl.CostEstimate(flops=flops, bytes_accessed=4 << 20, transcendentals=1 << 21),
    )


def slot_codes(tile_list, owner):
    source, target = tile_list[:, 0], tile_list[:, 1]
    away = target >> 3
    region = jnp.where(away == owner, 0, jnp.where(away == (owner ^ 1), 1, 2))
    code = (source - owner * NBLK) * 32 + region * NBLK + (target & 7)
    return jnp.where(source >= 0, code, -1)


def table_kernel(*refs):
    *code_refs, table_ref = refs
    for coupling in range(2):
        for s in range(NBLK):
            table_ref[GROUPS + coupling * NBLK + s] = 0

        @pl.loop(0, code_refs[0].shape[1])
        def _(slot):
            for code_ref in code_refs:
                code = code_ref[coupling, slot]

                @pl.when(code >= 0)
                def _():
                    row = coupling * NBLK + (code >> 5)
                    count = table_ref[GROUPS + row]
                    table_ref[row * STRIDE + count] = code & 31
                    table_ref[GROUPS + row] = count + 1

        for s in range(NBLK):
            row = coupling * NBLK + s
            count = table_ref[GROUPS + row]
            for extra in range(QUAD - 1):
                table_ref[row * STRIDE + count + extra] = WIN
            table_ref[GROUPS + row] = (count + QUAD - 1) >> 2


def products(source_ref, target_refs, g_ref):
    for region, target_ref in enumerate(target_refs):

        @pl.loop(0, NBLK // 2)
        def _(pair):
            rows = target_ref[pl.ds(pl.multiple_of(pair * 256, 256), 256), :]
            g = lax.dot_general(
                source_ref[...], rows, (((1,), (1,)), ((), ())), preferred_element_type=jnp.float32
            ) * (2.0 * SCALE)
            g_ref[region * NBLK + 2 * pair] = g[:, :BLOCK]
            g_ref[region * NBLK + 2 * pair + 1] = g[:, BLOCK:]

    g_ref[WIN] = jnp.zeros((CELLS, BLOCK), jnp.float32)


def extended(hh_ref, terms_ref):
    terms_ref[:WIN, :] = hh_ref[...]
    terms_ref[WIN:, :] = jnp.full((8, BLOCK), -BIG, jnp.float32)


def row_parts(table_ref, coupling, s):
    row = coupling * NBLK + s
    base = row * STRIDE

    def targets(q):
        return [table_ref[base + q * QUAD + k] for k in range(QUAD)]

    rows = pl.ds(pl.multiple_of(s * BLOCK, BLOCK), BLOCK)
    return rows, table_ref[GROUPS + row], targets


def row_maximum(rows, groups, targets, terms_ref, g_ref):
    def step(q, highest):
        v = [g_ref[t, rows, :] + terms_ref[pl.ds(t, 1), :] for t in targets(q)]
        return jnp.maximum(highest, jnp.maximum(jnp.maximum(v[0], v[1]), jnp.maximum(v[2], v[3])))

    highest = lax.fori_loop(0, groups, step, jnp.full((BLOCK, BLOCK), -BIG, jnp.float32))
    return jnp.max(highest, axis=1, keepdims=True)


def scale_rows(table_ref, coupling, hh_ref, kc_ref, g_ref, part_ref, terms_ref, top_ref, mass_ref):
    extended(hh_ref, terms_ref)
    top_ref[...] = jnp.full(top_ref.shape, -BIG, jnp.float32)
    mass_ref[...] = jnp.zeros(mass_ref.shape, jnp.float32)

    @pl.loop(0, NBLK)
    def _(s):
        rows, groups, targets = row_parts(table_ref, coupling, s)
        m = row_maximum(rows, groups, targets, terms_ref, g_ref)

        def step(q, acc):
            v = [jnp.exp2(g_ref[t, rows, :] + terms_ref[pl.ds(t, 1), :] - m) for t in targets(q)]
            return acc + ((v[0] + v[1]) + (v[2] + v[3]))

        acc = lax.fori_loop(0, groups, step, jnp.zeros((BLOCK, BLOCK), jnp.float32))
        total = m + LOG2E * jnp.log(jnp.sum(acc, axis=1, keepdims=True))
        kc = jnp.broadcast_to(kc_ref[pl.ds(s, 1), :], (BLOCK, BLOCK)).T
        uu = kc - LAM * total

        @pl.loop(0, groups)
        def _(q):
            ts = targets(q)
            tops = [top_ref[t] for t in ts]
            masses = [mass_ref[t] for t in ts]
            for t, top, mass in zip(ts, tops, masses):
                v = (g_ref[t, rows, :] + uu).reshape(BLOCK // 8, 8, BLOCK)
                high = jnp.maximum(top, jnp.max(v, axis=0))
                mass_ref[t] = mass * jnp.exp2(top - high) + jnp.sum(jnp.exp2(v - high), axis=0)
                top_ref[t] = high

    top = top_ref[:WIN]
    high = jnp.max(top, axis=1, keepdims=True)
    part_ref[0] = high[:, 0, :]
    part_ref[1] = jnp.sum(mass_ref[:WIN] * jnp.exp2(top - high), axis=1)


def weigh(table_ref, coupling, hh_ref, g_ref, w_ref, sum_ref, terms_ref):
    extended(hh_ref, terms_ref)

    @pl.loop(0, NBLK)
    def _(s):
        rows, groups, targets = row_parts(table_ref, coupling, s)
        m = row_maximum(rows, groups, targets, terms_ref, g_ref)
        w_ref[rows, :] = jnp.zeros((BLOCK, (WIN + 1) * BLOCK), jnp.bfloat16)

        def step(q, acc):
            for t in targets(q):
                e = jnp.exp2(g_ref[t, rows, :] + terms_ref[pl.ds(t, 1), :] - m)
                w_ref[rows, pl.ds(pl.multiple_of(t * BLOCK, BLOCK), BLOCK)] = e.astype(jnp.bfloat16)
                acc = acc + e
            return acc

        acc = lax.fori_loop(0, groups, step, jnp.zeros((BLOCK, BLOCK), jnp.float32))
        sum_ref[rows, :] = jnp.broadcast_to(jnp.sum(acc, axis=1, keepdims=True), (BLOCK, BLOCK))


def pull(w_ref, sum_ref, fate_refs, out_ref):
    @pl.loop(0, 4)
    def _(chunk):
        rows = pl.ds(pl.multiple_of(chunk * 256, 256), 256)
        total = jnp.zeros((256, out_ref.shape[1]), jnp.float32)
        for region, fate_ref in enumerate(fate_refs):
            total += jnp.dot(
                w_ref[rows, region * CELLS : (region + 1) * CELLS],
                fate_ref[...],
                preferred_element_type=jnp.float32,
            )
        inverse = 1.0 / sum_ref[rows, :]
        out_ref[rows, :] = (total * jnp.concatenate([inverse, inverse], axis=1)).astype(jnp.bfloat16)


def first_kernel(group_ref, table_ref, source_ref, own_ref, sib_ref, out_ref, hh_ref, kc_ref, g_ref, part_ref, *scratch):
    products(source_ref, (own_ref, sib_ref, out_ref), g_ref)
    scale_rows(table_ref, group_ref[0], hh_ref, kc_ref, g_ref, part_ref, *scratch)


def second_kernel(group_ref, table_ref, hh_ref, kc_ref, g_ref, part_ref, *scratch):
    scale_rows(table_ref, group_ref[0], hh_ref, kc_ref, g_ref, part_ref, *scratch)


def products_kernel(source_ref, own_ref, sib_ref, out_ref, g_ref):
    products(source_ref, (own_ref, sib_ref, out_ref), g_ref)


def weigh_one(coupling, group_ref, table_ref, hh_ref, g_ref, other_ref, *outs):
    @pl.when(group_ref[0] == coupling)
    def _():
        weigh(table_ref, coupling, hh_ref, g_ref, *outs)

    @pl.when(group_ref[0] != coupling)
    def _():
        weigh(table_ref, coupling, hh_ref, other_ref, *outs)


def late_kernel(group_ref, table_ref, hh_ref, g_ref, other_ref, own_ref, sib_ref, out_ref, late_ref, w_ref, sum_ref, terms_ref):
    weigh_one(1, group_ref, table_ref, hh_ref, g_ref, other_ref, w_ref, sum_ref, terms_ref)
    pull(w_ref, sum_ref, (own_ref, sib_ref, out_ref), late_ref)


def early_weights_kernel(group_ref, table_ref, hh_ref, g_ref, other_ref, w_ref, sum_ref, terms_ref):
    weigh_one(0, group_ref, table_ref, hh_ref, g_ref, other_ref, w_ref, sum_ref, terms_ref)


def early_kernel(w_ref, sum_ref, own_ref, sib_ref, out_ref, early_ref):
    pull(w_ref, sum_ref, (own_ref, sib_ref, out_ref), early_ref)


G_SHAPE = jax.ShapeDtypeStruct((WIN + 1, CELLS, BLOCK), jnp.float32)
PART_SHAPE = jax.ShapeDtypeStruct((2, WIN, BLOCK), jnp.float32)
W_SHAPE = jax.ShapeDtypeStruct((CELLS, (WIN + 1) * BLOCK), jnp.bfloat16)
SUM_SHAPE = jax.ShapeDtypeStruct((CELLS, BLOCK), jnp.float32)
FATE_SHAPE = jax.ShapeDtypeStruct((CELLS, EMB), jnp.bfloat16)
TERMS = pltpu.VMEM((WIN + 8, BLOCK), jnp.float32)
SWEEP_SCRATCH = [TERMS] + [pltpu.VMEM((WIN + 1, 8, BLOCK), jnp.float32)] * 2
HOLD = [pltpu.VMEM(W_SHAPE.shape, W_SHAPE.dtype), pltpu.VMEM(SUM_SHAPE.shape, SUM_SHAPE.dtype)]


def build_table(codes):
    specs = [SMEM] * len(codes)
    return call(table_kernel, jax.ShapeDtypeStruct((TABLE,), jnp.int32), SMEM, specs)(*codes)


def first_sweep(*args):
    return call(first_kernel, (G_SHAPE, PART_SHAPE), (VMEM, VMEM), [SMEM, SMEM] + [VMEM] * 6, SWEEP_SCRATCH)(*args)


def next_sweep(*args):
    return call(second_kernel, PART_SHAPE, VMEM, [SMEM, SMEM] + [VMEM] * 3, SWEEP_SCRATCH)(*args)


def other_products(*args):
    return call(products_kernel, G_SHAPE, VMEM, [VMEM] * 4)(*args)


def late_fates(*args):
    return call(late_kernel, FATE_SHAPE, VMEM, [SMEM, SMEM] + [VMEM] * 6, HOLD + [TERMS])(*args)


def early_weights(*args):
    return call(
        early_weights_kernel, (W_SHAPE, SUM_SHAPE), (VMEM, VMEM), [SMEM, SMEM] + [VMEM] * 3, [TERMS]
    )(*args)


def early_fates(*args):
    return call(early_kernel, FATE_SHAPE, VMEM, [VMEM] * 5)(*args)


def merged(first, second):
    highest = jnp.maximum(first[0], second[0])
    return jnp.stack(
        [
            highest,
            first[1] * jnp.exp2(first[0] - highest) + second[1] * jnp.exp2(second[0] - highest),
        ]
    )


def folded(part):
    own = merged(part[:, :NBLK], sibling(part[:, NBLK : 2 * NBLK]))
    beyond = part[:, 2 * NBLK :]
    arrived = outward(jnp.concatenate([own, beyond], axis=1))
    own = merged(own, arrived[:, NBLK:])
    out = merged(arrived[:, :NBLK], beyond)
    own_total = own[0] + jnp.log2(own[1])
    out_total = out[0] + jnp.log2(out[1])
    return jnp.concatenate([own_total, sibling(own_total), out_total], axis=0)


def shifted(value, steps):
    count = lax.axis_size("tiles")
    return lax.ppermute(value, "tiles", [(t, (t + steps) % count) for t in range(count)])


def on_device(embeddings, log_mass, signatures, tile_list):
    owner = lax.axis_index("cells").astype(jnp.int32)
    group = (lax.axis_index("tiles") >= 2).astype(jnp.int32)
    group_arg = group.reshape(1)

    def moment(array, index):
        return lax.dynamic_index_in_dim(array, index, 0, keepdims=False)

    target = moment(embeddings, group + 1)
    target_out, target_sib = outward(target), sibling(target)
    codes = slot_codes(tile_list, owner)
    table = build_table([codes] + [shifted(codes, k) for k in range(1, lax.axis_size("tiles"))])

    widened = embeddings.astype(jnp.float32)
    norms = (jnp.sum(widened * widened, axis=2) * SCALE).reshape(3, NBLK, BLOCK)
    masses = log_mass.reshape(3, NBLK, BLOCK) * LOG2E
    small = jnp.stack([masses - norms, masses + (LAM - 1.0) * norms], axis=1)
    window = jnp.concatenate(
        [moment(part, group + 1) for part in (small, sibling(small), outward(small))], axis=1
    )
    kc = moment(small, group)[1]

    g, part = first_sweep(
        group_arg, table, moment(embeddings, group), target, target_sib, target_out, window[0], kc
    )

    other, _ = lax.optimization_barrier((moment(embeddings, 2 - group), target_out))
    other_out, other_sib = outward(other), sibling(other)

    hh = window[1] - LAM * folded(part)
    part = next_sweep(group_arg, table, hh, kc, g)
    fates, _ = lax.optimization_barrier((signatures, hh))
    fates_out, fates_sib = outward(fates), sibling(fates)

    g_other = other_products(moment(embeddings, 1 - group), other, other_sib, other_out)
    hh = window[1] - LAM * folded(part)
    hh_other = mirrored(hh)
    hh_late = jnp.where(group == 1, hh, hh_other)
    hh_early = jnp.where(group == 1, hh_other, hh)

    late = late_fates(group_arg, table, hh_late, g, g_other, signatures, fates_sib, fates_out)
    late_out, late_sib = outward(late), sibling(late)
    weights, sums = early_weights(group_arg, table, hh_early, g, g_other)
    early = early_fates(weights, sums, late, late_sib, late_out)
    return early, late


def solution(mesh):
    in_specs = (
        P(None, "cells", None),
        P(None, "cells"),
        P("cells", None),
        P(None, None, ("cells", "tiles")),
    )
    out_specs = (P("cells", None), P("cells", None))
    return jax.shard_map(
        on_device, mesh=mesh, in_specs=in_specs, out_specs=out_specs, check_vma=False
    )
```

profile of v0, /device:TPU:0, one launch (start us, length us, event | category | flops | bytes accessed | tf_op | source)
XLA Modules:
  0.0 94.2 jit_solution(3303571245928293282)
XLA Ops:
  0.6 0.8 compare_select_fusion.2
  1.5 2.9 %collective-permute-start.2 = (s32[2,32]{1,0:T(2,128)S(1)}, s32[2,32]{1,0:T(2,128)S(1)}, u32[]{:S(2)}, u32[]{:S(2)}) collective-permute-start(s32[2,32]{1,0:T(2,128)S(1)} %bitcast.233), channel_id=1, source_target_pairs={{0,3},{1,0},{2,1},{3,2},{4,7},{5,4},{6,5},{7,6},{8,11},{9,8},{10,9... | collective-permute-start | bytes 776 | tf_op jit(solution)/shard_map/ppermute | solution.py:302
  4.4 0.8 collective-permute-start.1
  5.2 0.9 collective-permute-start
  6.1 1.9 %multiply_reduce_fusion = f32[3,1024]{1,0:T(4,128)S(1)} fusion(bf16[3,1024,256]{2,1,0:T(8,128)(2,1)} %param.4), kind=kLoop, calls=%fused_computation | loop fusion | flops 2356224 | bytes 1585152 | tf_op jit(solution)/shard_map/reduce_sum | solution.py:319
  8.0 0.7 add_bitcast_fusion
  8.7 5.2 %collective-permute-start.4 = (f32[3,2,8,128]{3,2,1,0:T(8,128)S(1)}, f32[3,2,8,128]{3,2,1,0:T(8,128)S(1)}, u32[]{:S(2)}, u32[]{:S(2)}) collective-permute-start(f32[3,2,8,128]{3,2,1,0:T(8,128)S(1)} %bitcast_dynamic-update-slice_fusion), channel_id=1, source_target_pairs={{0,124},{4,8},{8,4},{12,16},{16,12},{20,24},{24,20},{28,32},{32,28... | collective-permute-start | bytes 73736 | tf_op jit(solution)/shard_map/ppermute | solution.py:37
  13.9 0.1 dynamic-slice_bitcast_fusion
  14.1 1.7 %collective-permute-start.6 = (bf16[1024,256]{1,0:T(8,128)(2,1)S(1)}, bf16[1024,256]{1,0:T(8,128)(2,1)S(1)}, u32[]{:S(2)}, u32[]{:S(2)}) collective-permute-start(bf16[1024,256]{1,0:T(8,128)(2,1)S(1)} %get-tuple-element.19.own_ref), channel_id=1, source_target_pairs={{0,124},{4,8},{8,4},{12,16},{16,12},{20,24},{24,20},{28,32},{32,28... | collective-permute-start | bytes 1572872 | tf_op jit(solution)/shard_map/ppermute | solution.py:37
  15.8 3.1 %shard_map.59.table_ref = s32[512]{0:T(512)S(1)} custom-call(s32[2,32]{1,0:T(2,128)S(1)} %bitcast.236, s32[2,32]{1,0:T(2,128)S(1)} %collective-permute-done.refs_1_, s32[2,32]{1,0:T(2,128)S(1)} %collective-permute-done.1.refs_2_, s32[2,32]{1,0:T(2,128)S(1)} %collective-permute-done.2.refs_3_), custom_call_target="tpu_custom_call" | custom-call | flops 1000000000 | bytes 4194304 | tf_op jit(solution)/shard_map/pallas_call | solution.py:250
  19.0 7.1 %collective-permute-done.6.out_ref = bf16[1024,256]{1,0:T(8,128)(2,1)S(1)} collective-permute-done((bf16[1024,256]{1,0:T(8,128)(2,1)S(1)}, bf16[1024,256]{1,0:T(8,128)(2,1)S(1)}, u32[]{:S(2)}, u32[]{:S(2)}) %collective-permute-start.6) | collective-permute-done | bytes 524320 | tf_op jit(solution)/shard_map/ppermute | solution.py:37
  26.1 8.5 %shard_map.60 = (f32[25,1024,128]{2,1,0:T(8,128)S(1)}, f32[2,24,128]{2,1,0:T(8,128)S(1)}) custom-call(s32[1]{0:T(128)} %bitcast.group_ref, s32[512]{0:T(512)S(1)} %shard_map.59.table_ref, bf16[1024,256]{1,0:T(8,128)(2,1)S(1)} %get-tuple-element.20.source_ref, bf16[1024,256]{1,0:T(8,128)(2,1)S(1)} %get-tuple-element.19.own_ref, ...), custom_call_target="tpu_custom_call" | custom-call | flops 1000000000 | bytes 4194304 | tf_op jit(solution)/shard_map/pallas_call | solution.py:254
  34.7 1.2 %collective-permute-done.7 = f32[2,8,128]{2,1,0:T(8,128)S(1)} collective-permute-done((f32[2,8,128]{2,1,0:T(8,128)S(1)}, f32[2,8,128]{2,1,0:T(8,128)S(1)}, u32[]{:S(2)}, u32[]{:S(2)}) %collective-permute-start.7) | collective-permute-done | bytes 8224 | tf_op jit(solution)/shard_map/ppermute | solution.py:31
  35.8 3.6 %collective-permute-start.8 = (f32[2,16,128]{2,1,0:T(8,128)S(1)}, f32[2,16,128]{2,1,0:T(8,128)S(1)}, u32[]{:S(2)}, u32[]{:S(2)}) collective-permute-start(f32[2,16,128]{2,1,0:T(8,128)S(1)} %pad_maximum_fusion.1), channel_id=1, source_target_pairs={{0,124},{4,8},{8,4},{12,16},{16,12},{20,24},{24,20},{28,32},{32,28... | collective-permute-start | bytes 49160 | tf_op jit(solution)/shard_map/ppermute | solution.py:37
  39.4 3.0 %collective-permute-done.8 = f32[2,16,128]{2,1,0:T(8,128)S(1)} collective-permute-done((f32[2,16,128]{2,1,0:T(8,128)S(1)}, f32[2,16,128]{2,1,0:T(8,128)S(1)}, u32[]{:S(2)}, u32[]{:S(2)}) %collective-permute-start.8) | collective-permute-done | bytes 16416 | tf_op jit(solution)/shard_map/ppermute | solution.py:37
  42.5 1.2 %collective-permute-done.9 = f32[8,128]{1,0:T(8,128)S(1)} collective-permute-done((f32[8,128]{1,0:T(8,128)S(1)}, f32[8,128]{1,0:T(8,128)S(1)}, u32[]{:S(2)}, u32[]{:S(2)}) %collective-permute-start.9) | collective-permute-done | bytes 4128 | tf_op jit(solution)/shard_map/ppermute | solution.py:31
  43.7 4.4 %shard_map.61 = f32[2,24,128]{2,1,0:T(8,128)S(1)} custom-call(s32[1]{0:T(128)} %bitcast.group_ref, s32[512]{0:T(512)S(1)} %shard_map.59.table_ref, f32[24,128]{1,0:T(8,128)S(1)} %fusion.hh_ref, f32[8,128]{1,0:T(8,128)S(1)} %dynamic-slice_bitcast_fusion.7.kc_ref, f32[25,1024,128]{2,1,0:T(8,128)S(1)} %get-tuple-element.9.g_ref), custom_call_target="tpu_custom_call" | custom-call | flops 1000000000 | bytes 4194304 | tf_op jit(solution)/shard_map/pallas_call | solution.py:258
  48.2 2.0 %collective-permute-start.10 = (f32[2,8,128]{2,1,0:T(8,128)S(1)}, f32[2,8,128]{2,1,0:T(8,128)S(1)}, u32[]{:S(2)}, u32[]{:S(2)}) collective-permute-start(f32[2,8,128]{2,1,0:T(8,128)S(1)} %get-tuple-element.30), channel_id=1, source_target_pairs={{0,4},{4,0},{8,12},{12,8},{16,20},{20,16},{24,28},{28,24},{32,36},... | collective-permute-start | bytes 24584 | tf_op jit(solution)/shard_map/ppermute | solution.py:31
  50.2 0.8 collective-permute-done.10
  51.0 3.9 %collective-permute-start.11 = (f32[2,16,128]{2,1,0:T(8,128)S(1)}, f32[2,16,128]{2,1,0:T(8,128)S(1)}, u32[]{:S(2)}, u32[]{:S(2)}) collective-permute-start(f32[2,16,128]{2,1,0:T(8,128)S(1)} %pad_maximum_fusion.2), channel_id=1, source_target_pairs={{0,124},{4,8},{8,4},{12,16},{16,12},{20,24},{24,20},{28,32},{32,28... | collective-permute-start | bytes 49160 | tf_op jit(solution)/shard_map/ppermute | solution.py:37
  54.9 1.2 %collective-permute-start.15 = (bf16[1024,256]{1,0:T(8,128)(2,1)S(1)}, bf16[1024,256]{1,0:T(8,128)(2,1)S(1)}, u32[]{:S(2)}, u32[]{:S(2)}) collective-permute-start(bf16[1024,256]{1,0:T(8,128)(2,1)S(1)} %get-tuple-element.10.own_ref), channel_id=1, source_target_pairs={{0,124},{4,8},{8,4},{12,16},{16,12},{20,24},{24,20},{28,32},{32,28... | collective-permute-start | bytes 1572872 | tf_op jit(solution)/shard_map/ppermute | solution.py:37
  56.2 1.4 %collective-permute-done.11 = f32[2,16,128]{2,1,0:T(8,128)S(1)} collective-permute-done((f32[2,16,128]{2,1,0:T(8,128)S(1)}, f32[2,16,128]{2,1,0:T(8,128)S(1)}, u32[]{:S(2)}, u32[]{:S(2)}) %collective-permute-start.11) | collective-permute-done | bytes 16416 | tf_op jit(solution)/shard_map/ppermute | solution.py:37
  57.7 3.9 %collective-permute-start.17 = (bf16[1024,256]{1,0:T(8,128)(2,1)S(1)}, bf16[1024,256]{1,0:T(8,128)(2,1)S(1)}, u32[]{:S(2)}, u32[]{:S(2)}) collective-permute-start(bf16[1024,256]{1,0:T(8,128)(2,1)S(1)} %copy-done.3), channel_id=1, source_target_pairs={{0,124},{4,8},{8,4},{12,16},{16,12},{20,24},{24,20},{28,32},{32,28... | collective-permute-start | bytes 1572872 | tf_op jit(solution)/shard_map/ppermute | solution.py:37
  61.7 4.9 %collective-permute-done.13 = f32[24,128]{1,0:T(8,128)S(1)} collective-permute-done((f32[24,128]{1,0:T(8,128)S(1)}, f32[24,128]{1,0:T(8,128)S(1)}, u32[]{:S(2)}, u32[]{:S(2)}) %collective-permute-start.13) | collective-permute-done | bytes 12320 | tf_op jit(solution)/shard_map/ppermute | solution.py:42
  66.6 0.2 collective-permute-done.15.out_ref
  66.8 5.2 %shard_map.62.other_ref = f32[25,1024,128]{2,1,0:T(8,128)S(1)} custom-call(bf16[1024,256]{1,0:T(8,128)(2,1)S(1)} %get-tuple-element.21.source_ref, bf16[1024,256]{1,0:T(8,128)(2,1)S(1)} %get-tuple-element.10.own_ref, bf16[1024,256]{1,0:T(8,128)(2,1)} %collective-permute-done.14.sib_ref, bf16[1024,256]{1,0:T(8,128)(2,1)S(1)} %collective-permute-done.15.out_ref), custom_call_target="tpu_custom_call" | custom-call | flops 1000000000 | bytes 4194304 | tf_op jit(solution)/shard_map/pallas_call | solution.py:262
  72.1 0.4 collective-permute-done.17.out_ref
  72.5 6.4 %shard_map.64.own_ref = bf16[1024,256]{1,0:T(8,128)(2,1)} custom-call(s32[1]{0:T(128)} %bitcast.group_ref, s32[512]{0:T(512)S(1)} %shard_map.59.table_ref, f32[24,128]{1,0:T(8,128)S(1)} %get-tuple-element.28.hh_ref, f32[25,1024,128]{2,1,0:T(8,128)S(1)} %copy-done.1, f32[25,1024,128]{2,1,0:T(8,128)S(1)} %shard_map.62.other_ref, ...), custom_call_target="tpu_custom_call" | custom-call | flops 1000000000 | bytes 4194304 | tf_op jit(solution)/shard_map/pallas_call | solution.py:266
  78.9 1.0 %collective-permute-start.19 = (bf16[1024,256]{1,0:T(8,128)(2,1)}, bf16[1024,256]{1,0:T(8,128)(2,1)S(1)}, u32[]{:S(2)}, u32[]{:S(2)}) collective-permute-start(bf16[1024,256]{1,0:T(8,128)(2,1)} %shard_map.64.own_ref), channel_id=1, source_target_pairs={{0,124},{4,8},{8,4},{12,16},{16,12},{20,24},{24,20},{28,32},{32,28... | collective-permute-start | bytes 1572872 | tf_op jit(solution)/shard_map/ppermute | solution.py:37
  79.8 3.3 %shard_map.63 = (bf16[1024,3200]{1,0:T(8,128)(2,1)S(1)}, f32[1024,128]{1,0:T(8,128)S(1)}) custom-call(s32[1]{0:T(128)} %bitcast.group_ref, s32[512]{0:T(512)S(1)} %shard_map.59.table_ref, f32[24,128]{1,0:T(8,128)S(1)} %get-tuple-element.29.hh_ref, f32[25,1024,128]{2,1,0:T(8,128)S(1)} %copy-done.1, f32[25,1024,128]{2,1,0:T(8,128)S(1)} %shard_map.62.other_ref), custom_call_target="tpu_custom_call" | custom-call | flops 1000000000 | bytes 4194304 | tf_op jit(solution)/shard_map/pallas_call | solution.py:270
  83.1 7.9 %collective-permute-done.19.out_ref = bf16[1024,256]{1,0:T(8,128)(2,1)S(1)} collective-permute-done((bf16[1024,256]{1,0:T(8,128)(2,1)}, bf16[1024,256]{1,0:T(8,128)(2,1)S(1)}, u32[]{:S(2)}, u32[]{:S(2)}) %collective-permute-start.19) | collective-permute-done | bytes 524320 | tf_op jit(solution)/shard_map/ppermute | solution.py:37
  91.0 3.1 %shard_map.65 = bf16[1024,256]{1,0:T(8,128)(2,1)} custom-call(bf16[1024,3200]{1,0:T(8,128)(2,1)S(1)} %get-tuple-element.11.w_ref, f32[1024,128]{1,0:T(8,128)S(1)} %get-tuple-element.12.sum_ref, bf16[1024,256]{1,0:T(8,128)(2,1)S(1)} %copy-done.2, bf16[1024,256]{1,0:T(8,128)(2,1)S(1)} %collective-permute-done.18.sib_ref, ...), custom_call_target="tpu_custom_call" | custom-call | flops 1000000000 | bytes 4194304 | tf_op jit(solution)/shard_map/pallas_call | solution.py:276
  (48 shorter events, 0.5 us)
Async XLA Ops:
  0.6 13.3 %copy-start.4 = (bf16[3,1024,256]{2,1,0:T(8,128)(2,1)S(1)}, bf16[3,1024,256]{2,1,0:T(8,128)(2,1)}, u32[]{:S(2)}) copy-start(bf16[3,1024,256]{2,1,0:T(8,128)(2,1)} %param.4) | copy-start | bytes 4718596
  1.5 12.6 %collective-permute-start.2 = (s32[2,32]{1,0:T(2,128)S(1)}, s32[2,32]{1,0:T(2,128)S(1)}, u32[]{:S(2)}, u32[]{:S(2)}) collective-permute-start(s32[2,32]{1,0:T(2,128)S(1)} %bitcast.233), channel_id=1, source_target_pairs={{0,3},{1,0},{2,1},{3,2},{4,7},{5,4},{6,5},{7,6},{8,11},{9,8},{10,9... | collective-permute-start | bytes 776 | tf_op jit(solution)/shard_map/ppermute | solution.py:302
  4.4 11.4 %collective-permute-start.1 = (s32[2,32]{1,0:T(2,128)S(1)}, s32[2,32]{1,0:T(2,128)S(1)}, u32[]{:S(2)}, u32[]{:S(2)}) collective-permute-start(s32[2,32]{1,0:T(2,128)S(1)} %bitcast.234), channel_id=1, source_target_pairs={{0,2},{1,3},{2,0},{3,1},{4,6},{5,7},{6,4},{7,5},{8,10},{9,11},{10,... | collective-permute-start | bytes 776 | tf_op jit(solution)/shard_map/ppermute | solution.py:302
  5.2 10.6 %collective-permute-start = (s32[2,32]{1,0:T(2,128)S(1)}, s32[2,32]{1,0:T(2,128)S(1)}, u32[]{:S(2)}, u32[]{:S(2)}) collective-permute-start(s32[2,32]{1,0:T(2,128)S(1)} %bitcast.235), channel_id=1, source_target_pairs={{0,1},{1,2},{2,3},{3,0},{4,5},{5,6},{6,7},{7,4},{8,9},{9,10},{10,1... | collective-permute-start | bytes 776 | tf_op jit(solution)/shard_map/ppermute | solution.py:302
  8.7 10.2 %collective-permute-start.4 = (f32[3,2,8,128]{3,2,1,0:T(8,128)S(1)}, f32[3,2,8,128]{3,2,1,0:T(8,128)S(1)}, u32[]{:S(2)}, u32[]{:S(2)}) collective-permute-start(f32[3,2,8,128]{3,2,1,0:T(8,128)S(1)} %bitcast_dynamic-update-slice_fusion), channel_id=1, source_target_pairs={{0,124},{4,8},{8,4},{12,16},{16,12},{20,24},{24,20},{28,32},{32,28... | collective-permute-start | bytes 73736 | tf_op jit(solution)/shard_map/ppermute | solution.py:37
  13.9 5.0 %collective-permute-start.3 = (f32[3,2,8,128]{3,2,1,0:T(8,128)S(1)}, f32[3,2,8,128]{3,2,1,0:T(8,128)S(1)}, u32[]{:S(2)}, u32[]{:S(2)}) collective-permute-start(f32[3,2,8,128]{3,2,1,0:T(8,128)S(1)} %bitcast_dynamic-update-slice_fusion), channel_id=1, source_target_pairs={{0,4},{4,0},{8,12},{12,8},{16,20},{20,16},{24,28},{28,24},{32,36},... | collective-permute-start | bytes 73736 | tf_op jit(solution)/shard_map/ppermute | solution.py:31
  14.1 12.0 %collective-permute-start.6 = (bf16[1024,256]{1,0:T(8,128)(2,1)S(1)}, bf16[1024,256]{1,0:T(8,128)(2,1)S(1)}, u32[]{:S(2)}, u32[]{:S(2)}) collective-permute-start(bf16[1024,256]{1,0:T(8,128)(2,1)S(1)} %get-tuple-element.19.own_ref), channel_id=1, source_target_pairs={{0,124},{4,8},{8,4},{12,16},{16,12},{20,24},{24,20},{28,32},{32,28... | collective-permute-start | bytes 1572872 | tf_op jit(solution)/shard_map/ppermute | solution.py:37
  15.8 10.3 %collective-permute-start.5 = (bf16[1024,256]{1,0:T(8,128)(2,1)S(1)}, bf16[1024,256]{1,0:T(8,128)(2,1)S(1)}, u32[]{:S(2)}, u32[]{:S(2)}) collective-permute-start(bf16[1024,256]{1,0:T(8,128)(2,1)S(1)} %get-tuple-element.19.own_ref), channel_id=1, source_target_pairs={{0,4},{4,0},{8,12},{12,8},{16,20},{20,16},{24,28},{28,24},{32,36},... | collective-permute-start | bytes 1572872 | tf_op jit(solution)/shard_map/ppermute | solution.py:31
  34.6 13.6 %copy-start = (f32[25,1024,128]{2,1,0:T(8,128)}, f32[25,1024,128]{2,1,0:T(8,128)S(1)}, u32[]{:S(2)}) copy-start(f32[25,1024,128]{2,1,0:T(8,128)S(1)} %get-tuple-element.9.g_ref) | copy-start | bytes 39321604
  34.6 1.3 %collective-permute-start.7 = (f32[2,8,128]{2,1,0:T(8,128)S(1)}, f32[2,8,128]{2,1,0:T(8,128)S(1)}, u32[]{:S(2)}, u32[]{:S(2)}) collective-permute-start(f32[2,8,128]{2,1,0:T(8,128)S(1)} %get-tuple-element.32), channel_id=1, source_target_pairs={{0,4},{4,0},{8,12},{12,8},{16,20},{20,16},{24,28},{28,24},{32,36},... | collective-permute-start | bytes 24584 | tf_op jit(solution)/shard_map/ppermute | solution.py:31
  35.8 6.6 %collective-permute-start.8 = (f32[2,16,128]{2,1,0:T(8,128)S(1)}, f32[2,16,128]{2,1,0:T(8,128)S(1)}, u32[]{:S(2)}, u32[]{:S(2)}) collective-permute-start(f32[2,16,128]{2,1,0:T(8,128)S(1)} %pad_maximum_fusion.1), channel_id=1, source_target_pairs={{0,124},{4,8},{8,4},{12,16},{16,12},{20,24},{24,20},{28,32},{32,28... | collective-permute-start | bytes 49160 | tf_op jit(solution)/shard_map/ppermute | solution.py:37
  42.4 1.2 %collective-permute-start.9 = (f32[8,128]{1,0:T(8,128)S(1)}, f32[8,128]{1,0:T(8,128)S(1)}, u32[]{:S(2)}, u32[]{:S(2)}) collective-permute-start(f32[8,128]{1,0:T(8,128)S(1)} %get-tuple-element.24), channel_id=1, source_target_pairs={{0,4},{4,0},{8,12},{12,8},{16,20},{20,16},{24,28},{28,24},{32,36},... | collective-permute-start | bytes 12296 | tf_op jit(solution)/shard_map/ppermute | solution.py:31
  43.7 14.0 %copy-start.3 = (bf16[1024,256]{1,0:T(8,128)(2,1)S(1)}, bf16[1024,256]{1,0:T(8,128)(2,1)}, u32[]{:S(2)}) copy-start(bf16[1024,256]{1,0:T(8,128)(2,1)} %own_ref.1) | copy-start | bytes 1572868
  48.2 2.8 %collective-permute-start.10 = (f32[2,8,128]{2,1,0:T(8,128)S(1)}, f32[2,8,128]{2,1,0:T(8,128)S(1)}, u32[]{:S(2)}, u32[]{:S(2)}) collective-permute-start(f32[2,8,128]{2,1,0:T(8,128)S(1)} %get-tuple-element.30), channel_id=1, source_target_pairs={{0,4},{4,0},{8,12},{12,8},{16,20},{20,16},{24,28},{28,24},{32,36},... | collective-permute-start | bytes 24584 | tf_op jit(solution)/shard_map/ppermute | solution.py:31
  51.0 6.6 %collective-permute-start.11 = (f32[2,16,128]{2,1,0:T(8,128)S(1)}, f32[2,16,128]{2,1,0:T(8,128)S(1)}, u32[]{:S(2)}, u32[]{:S(2)}) collective-permute-start(f32[2,16,128]{2,1,0:T(8,128)S(1)} %pad_maximum_fusion.2), channel_id=1, source_target_pairs={{0,124},{4,8},{8,4},{12,16},{16,12},{20,24},{24,20},{28,32},{32,28... | collective-permute-start | bytes 49160 | tf_op jit(solution)/shard_map/ppermute | solution.py:37
  54.9 11.9 %collective-permute-start.15 = (bf16[1024,256]{1,0:T(8,128)(2,1)S(1)}, bf16[1024,256]{1,0:T(8,128)(2,1)S(1)}, u32[]{:S(2)}, u32[]{:S(2)}) collective-permute-start(bf16[1024,256]{1,0:T(8,128)(2,1)S(1)} %get-tuple-element.10.own_ref), channel_id=1, source_target_pairs={{0,124},{4,8},{8,4},{12,16},{16,12},{20,24},{24,20},{28,32},{32,28... | collective-permute-start | bytes 1572872 | tf_op jit(solution)/shard_map/ppermute | solution.py:37
  56.2 10.7 %collective-permute-start.14 = (bf16[1024,256]{1,0:T(8,128)(2,1)S(1)}, bf16[1024,256]{1,0:T(8,128)(2,1)}, u32[]{:S(2)}, u32[]{:S(2)}) collective-permute-start(bf16[1024,256]{1,0:T(8,128)(2,1)S(1)} %get-tuple-element.10.own_ref), channel_id=1, source_target_pairs={{0,4},{4,0},{8,12},{12,8},{16,20},{20,16},{24,28},{28,24},{32,36},... | collective-permute-start | bytes 1572872 | tf_op jit(solution)/shard_map/ppermute | solution.py:31
  57.6 4.0 %collective-permute-start.12 = (f32[8,128]{1,0:T(8,128)S(1)}, f32[8,128]{1,0:T(8,128)S(1)}, u32[]{:S(2)}, u32[]{:S(2)}) collective-permute-start(f32[8,128]{1,0:T(8,128)S(1)} %get-tuple-element.22), channel_id=1, source_target_pairs={{0,4},{4,0},{8,12},{12,8},{16,20},{20,16},{24,28},{28,24},{32,36},... | collective-permute-start | bytes 12296 | tf_op jit(solution)/shard_map/ppermute | solution.py:31
  57.7 14.8 %collective-permute-start.17 = (bf16[1024,256]{1,0:T(8,128)(2,1)S(1)}, bf16[1024,256]{1,0:T(8,128)(2,1)S(1)}, u32[]{:S(2)}, u32[]{:S(2)}) collective-permute-start(bf16[1024,256]{1,0:T(8,128)(2,1)S(1)} %copy-done.3), channel_id=1, source_target_pairs={{0,124},{4,8},{8,4},{12,16},{16,12},{20,24},{24,20},{28,32},{32,28... | collective-permute-start | bytes 1572872 | tf_op jit(solution)/shard_map/ppermute | solution.py:37
  61.6 10.9 %collective-permute-start.16 = (bf16[1024,256]{1,0:T(8,128)(2,1)S(1)}, bf16[1024,256]{1,0:T(8,128)(2,1)S(1)}, u32[]{:S(2)}, u32[]{:S(2)}) collective-permute-start(bf16[1024,256]{1,0:T(8,128)(2,1)S(1)} %copy-done.3), channel_id=1, source_target_pairs={{0,4},{4,0},{8,12},{12,8},{16,20},{20,16},{24,28},{28,24},{32,36},... | collective-permute-start | bytes 1572872 | tf_op jit(solution)/shard_map/ppermute | solution.py:31
  61.6 5.0 %collective-permute-start.13 = (f32[24,128]{1,0:T(8,128)S(1)}, f32[24,128]{1,0:T(8,128)S(1)}, u32[]{:S(2)}, u32[]{:S(2)}) collective-permute-start(f32[24,128]{1,0:T(8,128)S(1)} %fusion.1), channel_id=1, source_target_pairs={{0,3},{1,2},{2,1},{3,0},{4,7},{5,6},{6,5},{7,4},{8,11},{9,10},{10,... | collective-permute-start | bytes 36872 | tf_op jit(solution)/shard_map/ppermute | solution.py:42
  66.8 5.6 %copy-start.1 = (f32[25,1024,128]{2,1,0:T(8,128)S(1)}, f32[25,1024,128]{2,1,0:T(8,128)}, u32[]{:S(2)}) copy-start(f32[25,1024,128]{2,1,0:T(8,128)} %copy-done) | copy-start | bytes 39321604
  78.9 12.1 %collective-permute-start.19 = (bf16[1024,256]{1,0:T(8,128)(2,1)}, bf16[1024,256]{1,0:T(8,128)(2,1)S(1)}, u32[]{:S(2)}, u32[]{:S(2)}) collective-permute-start(bf16[1024,256]{1,0:T(8,128)(2,1)} %shard_map.64.own_ref), channel_id=1, source_target_pairs={{0,124},{4,8},{8,4},{12,16},{16,12},{20,24},{24,20},{28,32},{32,28... | collective-permute-start | bytes 1572872 | tf_op jit(solution)/shard_map/ppermute | solution.py:37
  79.8 11.2 %collective-permute-start.18 = (bf16[1024,256]{1,0:T(8,128)(2,1)}, bf16[1024,256]{1,0:T(8,128)(2,1)S(1)}, u32[]{:S(2)}, u32[]{:S(2)}) collective-permute-start(bf16[1024,256]{1,0:T(8,128)(2,1)} %shard_map.64.own_ref), channel_id=1, source_target_pairs={{0,4},{4,0},{8,12},{12,8},{16,20},{20,16},{24,28},{28,24},{32,36},... | collective-permute-start | bytes 1572872 | tf_op jit(solution)/shard_map/ppermute | solution.py:31
  79.8 11.2 %copy-start.2 = (bf16[1024,256]{1,0:T(8,128)(2,1)S(1)}, bf16[1024,256]{1,0:T(8,128)(2,1)}, u32[]{:S(2)}) copy-start(bf16[1024,256]{1,0:T(8,128)(2,1)} %shard_map.64.own_ref) | copy-start | bytes 1572868
where the time goes:
time: 94.5 us; the launch traced here: 94.2 us
  Pallas kernels  34.1 us (36%)
  waiting for transfers between devices  28.1 us (30%)
  starting transfers between devices  27.4 us (29%)
  other arithmetic  3.54 us (4%)
    ppermute x7, starting transfers between devices, outward(): return lax.ppermute(value, 'cells', pairs)  20.4 us
    ppermute x7, waiting for transfers between devices, outward(): return lax.ppermute(value, 'cells', pairs)  20 us
    pallas_call x1, Pallas kernels, first_sweep(): call(first_kernel, (G_SHAPE, PART_SHAPE), (VMEM, VMEM), [SMEM, SMEM] + [V...  8.46 us
    pallas_call x1, Pallas kernels, late_fates(): call(late_kernel, FATE_SHAPE, VMEM, [SMEM, SMEM] + [VMEM] * 6, HOLD + [TE...  6.4 us
    pallas_call x1, Pallas kernels, other_products(): return call(products_kernel, G_SHAPE, VMEM, [VMEM] * 4)(*args)  5.21 us
    ppermute x1, waiting for transfers between devices, mirrored(): lax.ppermute(value, 'tiles', [(t, count - 1 - t) for t in range(count)])  4.89 us
    ppermute x3, starting transfers between devices, shifted(): lax.ppermute(value, 'tiles', [(t, (t + steps) % count) for t in range(cou...  4.59 us
    pallas_call x1, Pallas kernels, next_sweep(): call(second_kernel, PART_SHAPE, VMEM, [SMEM, SMEM] + [VMEM] * 3, SWEEP_SC...  4.44 us
  transfers between devices with their start and end apart: 20, of which 10 were waited for; matrix products, arithmetic and copies ran while one was open for 3% of the time, Pallas kernels for 12%

commit v1 on v0

v1 whole, which is shorter than its diff:
```python
import jax
import jax.numpy as jnp
from jax import lax
from jax.experimental import pallas as pl
from jax.experimental.pallas import tpu as pltpu
from jax.sharding import PartitionSpec as P

EMB = 256
BLOCK = 128
NBLK = 8
WIN = 3 * NBLK
CELLS = NBLK * BLOCK
EPS = 0.01
RHO = 1.0
LAM = RHO / (RHO + EPS)
BIG = 1e30

LOG2E = 1.4426950408889634
SCALE = LOG2E / (EMB * EPS)

QUAD = 4
STRIDE = WIN + QUAD
GROUPS = NBLK * STRIDE
TABLE = 256

FLOPS, BYTES, MIB = 3 * 10**9, 10**4, 6
VMEM = pl.BlockSpec(memory_space=pltpu.VMEM)
SMEM = pl.BlockSpec(memory_space=pltpu.SMEM)


def sibling(value):
    return lax.ppermute(value, "cells", [(c, c ^ 1) for c in range(lax.axis_size("cells"))])


def outward(value):
    count = lax.axis_size("cells")
    pairs = [(c, (c + 1 if c % 2 else c - 1) % count) for c in range(count)]
    return lax.ppermute(value, "cells", pairs)


def mirrored(value):
    count = lax.axis_size("tiles")
    return lax.ppermute(value, "tiles", [(t, count - 1 - t) for t in range(count)])


def call(kernel, outs, out_specs, in_specs, scratch=(), aliases=None, flops=FLOPS, mib=MIB):
    return pl.pallas_call(
        kernel,
        out_shape=outs,
        in_specs=in_specs,
        out_specs=out_specs,
        scratch_shapes=list(scratch),
        input_output_aliases=aliases or {},
        compiler_params=pltpu.CompilerParams(vmem_limit_bytes=mib << 20),
        cost_estimate=pl.CostEstimate(flops=flops, bytes_accessed=BYTES, transcendentals=0),
    )


def table_kernel(place_ref, *refs):
    *slot_refs, table_ref = refs
    owner, coupling = place_ref[0], place_ref[1]
    for s in range(NBLK):
        table_ref[GROUPS + s] = 0

    @pl.loop(0, slot_refs[0].shape[2])
    def _(slot):
        for slot_ref in slot_refs:
            source = slot_ref[coupling, 0, slot]

            @pl.when(source >= 0)
            def _():
                target = slot_ref[coupling, 1, slot]
                away = target >> 3
                region = jnp.where(away == owner, 0, jnp.where(away == (owner ^ 1), 1, 2))
                s = source & 7
                count = table_ref[GROUPS + s]
                table_ref[s * STRIDE + count] = region * NBLK + (target & 7)
                table_ref[GROUPS + s] = count + 1

    for s in range(NBLK):
        count = table_ref[GROUPS + s]
        for extra in range(QUAD - 1):
            table_ref[s * STRIDE + count + extra] = WIN
        table_ref[GROUPS + s] = (count + QUAD - 1) >> 2


def products(source_ref, target_refs, g_ref, first):
    for region, target_ref in enumerate(target_refs, first):

        @pl.loop(0, NBLK // 2)
        def _(pair):
            rows = target_ref[pl.ds(pl.multiple_of(pair * 256, 256), 256), :]
            g = lax.dot_general(
                source_ref[...], rows, (((1,), (1,)), ((), ())), preferred_element_type=jnp.float32
            ) * (2.0 * SCALE)
            g_ref[region * NBLK + 2 * pair] = g[:, :BLOCK]
            g_ref[region * NBLK + 2 * pair + 1] = g[:, BLOCK:]


def target_constants(target_ref, mass_row, window_ref, region):
    ones = jnp.ones((8, EMB), jnp.bfloat16)
    for pair in range(NBLK // 2):
        y = target_ref[pair * 256 : (pair + 1) * 256, :].astype(jnp.float32)
        square = y * y
        high = square.astype(jnp.bfloat16)
        low = (square - high.astype(jnp.float32)).astype(jnp.bfloat16)
        norm = sum(
            lax.dot_general(ones, part, (((1,), (1,)), ((), ())), preferred_element_type=jnp.float32)
            for part in (high, low)
        )
        for half in range(2):
            block = 2 * pair + half
            scaled = norm[:1, half * BLOCK : (half + 1) * BLOCK] * SCALE
            mass = mass_row(block) * LOG2E
            at = region * NBLK + block
            window_ref[0, at : at + 1, :] = mass - scaled
            window_ref[1, at : at + 1, :] = mass + (LAM - 1.0) * scaled


def mass_rows(mass_ref, group, first):
    def row(block):
        lanes = slice(block * BLOCK, (block + 1) * BLOCK)
        low, high = mass_ref[first : first + 1, lanes], mass_ref[first + 1 : first + 2, lanes]
        return jnp.where(group == 0, low, high)

    return row


def extended(hh_ref, terms_ref):
    terms_ref[:WIN, :] = hh_ref[...]
    terms_ref[WIN:, :] = jnp.full((8, BLOCK), -BIG, jnp.float32)


def row_parts(table_ref, s):
    base = s * STRIDE

    def targets(q):
        return [table_ref[base + q * QUAD + k] for k in range(QUAD)]

    rows = pl.ds(pl.multiple_of(s * BLOCK, BLOCK), BLOCK)
    return rows, table_ref[GROUPS + s], targets


def row_maximum(rows, groups, targets, terms_ref, g_ref):
    def step(q, highest):
        v = [g_ref[t, rows, :] + terms_ref[pl.ds(t, 1), :] for t in targets(q)]
        return jnp.maximum(highest, jnp.maximum(jnp.maximum(v[0], v[1]), jnp.maximum(v[2], v[3])))

    highest = lax.fori_loop(0, groups, step, jnp.full((BLOCK, BLOCK), -BIG, jnp.float32))
    return jnp.max(highest, axis=1, keepdims=True)


def sweep_kernel(table_ref, hh_ref, kc_ref, g_ref, part_ref, terms_ref, top_ref, mass_ref):
    extended(hh_ref, terms_ref)
    top_ref[...] = jnp.full(top_ref.shape, -BIG, jnp.float32)
    mass_ref[...] = jnp.zeros(mass_ref.shape, jnp.float32)

    @pl.loop(0, NBLK)
    def _(s):
        rows, groups, targets = row_parts(table_ref, s)
        m = row_maximum(rows, groups, targets, terms_ref, g_ref)

        def step(q, acc):
            v = [jnp.exp2(g_ref[t, rows, :] + terms_ref[pl.ds(t, 1), :] - m) for t in targets(q)]
            return acc + ((v[0] + v[1]) + (v[2] + v[3]))

        acc = lax.fori_loop(0, groups, step, jnp.zeros((BLOCK, BLOCK), jnp.float32))
        total = m + LOG2E * jnp.log(jnp.sum(acc, axis=1, keepdims=True))
        uu = kc_ref[rows, :] - LAM * total

        @pl.loop(0, groups)
        def _(q):
            ts = targets(q)
            tops = [top_ref[t] for t in ts]
            masses = [mass_ref[t] for t in ts]
            for t, top, mass in zip(ts, tops, masses):
                v = (g_ref[t, rows, :] + uu).reshape(BLOCK // 8, 8, BLOCK)
                high = jnp.maximum(top, jnp.max(v, axis=0))
                mass_ref[t] = mass * jnp.exp2(top - high) + jnp.sum(jnp.exp2(v - high), axis=0)
                top_ref[t] = high

    top = top_ref[:WIN]
    high = jnp.max(top, axis=1, keepdims=True)
    part_ref[0] = high[:, 0, :]
    part_ref[1] = jnp.sum(mass_ref[:WIN] * jnp.exp2(top - high), axis=1)


def weigh(table_ref, hh_ref, g_ref, w_ref, sum_ref, terms_ref):
    extended(hh_ref, terms_ref)

    @pl.loop(0, NBLK)
    def _(s):
        rows, groups, targets = row_parts(table_ref, s)
        m = row_maximum(rows, groups, targets, terms_ref, g_ref)
        w_ref[rows, :] = jnp.zeros((BLOCK, (WIN + 1) * BLOCK), jnp.bfloat16)

        def step(q, acc):
            for t in targets(q):
                e = jnp.exp2(g_ref[t, rows, :] + terms_ref[pl.ds(t, 1), :] - m)
                w_ref[rows, pl.ds(pl.multiple_of(t * BLOCK, BLOCK), BLOCK)] = e.astype(jnp.bfloat16)
                acc = acc + e
            return acc

        acc = lax.fori_loop(0, groups, step, jnp.zeros((BLOCK, BLOCK), jnp.float32))
        sum_ref[rows, :] = jnp.broadcast_to(jnp.sum(acc, axis=1, keepdims=True), (BLOCK, BLOCK))


def pulled(w_ref, rows, fate_refs, first):
    total = 0.0
    for region, fate_ref in enumerate(fate_refs, first):
        total += jnp.dot(
            w_ref[rows, region * CELLS : (region + 1) * CELLS],
            fate_ref[...],
            preferred_element_type=jnp.float32,
        )
    return total


def divided(total, sums):
    inverse = 1.0 / sums
    return (total * jnp.concatenate([inverse, inverse], axis=1)).astype(jnp.bfloat16)


def chunks(body):
    @pl.loop(0, 4)
    def _(chunk):
        body(pl.ds(pl.multiple_of(chunk * 256, 256), 256))


def near_kernel(place_ref, cells_ref, mass_ref, sib_mass_ref, sib_ref, g_ref, kc_ref, window_ref):
    group = place_ref[1]
    source_ref, own_ref = cells_ref.at[group], cells_ref.at[group + 1]
    products(source_ref, (own_ref, sib_ref), g_ref, 0)
    g_ref[WIN] = jnp.zeros((CELLS, BLOCK), jnp.float32)
    target_constants(own_ref, mass_rows(mass_ref, group, 1), window_ref, 0)
    target_constants(sib_ref, mass_rows(sib_mass_ref, group, 1), window_ref, 1)
    source_mass = mass_rows(mass_ref, group, 0)
    for s in range(NBLK):
        x = source_ref[s * BLOCK : (s + 1) * BLOCK, :].astype(jnp.float32)
        norm = jnp.sum(x * x, axis=1, keepdims=True) * SCALE
        mass = jnp.broadcast_to(source_mass(s), (BLOCK, BLOCK)).T
        kc_ref[s * BLOCK : (s + 1) * BLOCK, :] = mass * LOG2E + (LAM - 1.0) * norm


def far_kernel(place_ref, cells_ref, out_mass_ref, out_ref, near_ref, near_window_ref, g_ref, window_ref):
    del near_ref
    group = place_ref[1]
    window_ref[:, : 2 * NBLK, :] = near_window_ref[...]
    products(cells_ref.at[group], (out_ref,), g_ref, 2)
    target_constants(out_ref, mass_rows(out_mass_ref, group, 1), window_ref, 2)


def other_kernel(place_ref, cells_ref, sib_ref, out_ref, g_ref):
    group = place_ref[1]
    products(cells_ref.at[1 - group], (cells_ref.at[2 - group], sib_ref, out_ref), g_ref, 0)
    g_ref[WIN] = jnp.zeros((CELLS, BLOCK), jnp.float32)


def weigh_one(coupling, place_ref, mine, others, *outs):
    @pl.when(place_ref[1] == coupling)
    def _():
        weigh(*mine, *outs)

    @pl.when(place_ref[1] != coupling)
    def _():
        weigh(*others, *outs)


def late_kernel(place_ref, table_ref, hh_ref, g_ref, table2_ref, hh2_ref, g2_ref, own_ref, sib_ref, out_ref, late_ref, w_ref, sum_ref, terms_ref):
    weigh_one(1, place_ref, (table_ref, hh_ref, g_ref), (table2_ref, hh2_ref, g2_ref), w_ref, sum_ref, terms_ref)
    fates = (own_ref, sib_ref, out_ref)

    @chunks
    def _(rows):
        late_ref[rows, :] = divided(pulled(w_ref, rows, fates, 0), sum_ref[rows, :])


def early_weights_kernel(place_ref, table_ref, hh_ref, g_ref, table2_ref, hh2_ref, g2_ref, w_ref, sum_ref, terms_ref):
    weigh_one(0, place_ref, (table_ref, hh_ref, g_ref), (table2_ref, hh2_ref, g2_ref), w_ref, sum_ref, terms_ref)


def early_near_kernel(w_ref, own_ref, sib_ref, total_ref):
    @chunks
    def _(rows):
        total_ref[rows, :] = pulled(w_ref, rows, (own_ref, sib_ref), 0)


def early_kernel(w_ref, sum_ref, total_ref, out_ref, early_ref):
    @chunks
    def _(rows):
        total = total_ref[rows, :] + pulled(w_ref, rows, (out_ref,), 2)
        early_ref[rows, :] = divided(total, sum_ref[rows, :])


G_SHAPE = pltpu.VMEM((WIN + 1, CELLS, BLOCK), jnp.float32)
PART_SHAPE = jax.ShapeDtypeStruct((2, WIN, BLOCK), jnp.float32)
W_SHAPE = jax.ShapeDtypeStruct((CELLS, (WIN + 1) * BLOCK), jnp.bfloat16)
COLUMN_SHAPE = jax.ShapeDtypeStruct((CELLS, BLOCK), jnp.float32)
FATE_SHAPE = jax.ShapeDtypeStruct((CELLS, EMB), jnp.bfloat16)
TOTAL_SHAPE = jax.ShapeDtypeStruct((CELLS, EMB), jnp.float32)
TERMS = pltpu.VMEM((WIN + 8, BLOCK), jnp.float32)
SWEEP_SCRATCH = [TERMS] + [pltpu.VMEM((WIN + 1, 8, BLOCK), jnp.float32)] * 2
HOLD = [pltpu.VMEM(W_SHAPE.shape, W_SHAPE.dtype), pltpu.VMEM(COLUMN_SHAPE.shape, COLUMN_SHAPE.dtype)]


WINDOW_SHAPE = jax.ShapeDtypeStruct((2, WIN, BLOCK), jnp.float32)
NEAR_SHAPE = jax.ShapeDtypeStruct((2, 2 * NBLK, BLOCK), jnp.float32)


def build_table(place, slots):
    specs = [SMEM] * (1 + len(slots))
    return call(table_kernel, jax.ShapeDtypeStruct((TABLE,), jnp.int32), SMEM, specs)(place, *slots)


def near_products(*args):
    return call(near_kernel, (G_SHAPE, COLUMN_SHAPE, NEAR_SHAPE), (VMEM,) * 3, [SMEM] + [VMEM] * 4)(*args)


def far_products(*args):
    return call(far_kernel, (G_SHAPE, WINDOW_SHAPE), (VMEM,) * 2, [SMEM] + [VMEM] * 5, aliases={4: 0})(*args)


def sweep(*args):
    return call(sweep_kernel, PART_SHAPE, VMEM, [SMEM] + [VMEM] * 3, SWEEP_SCRATCH)(*args)


def other_products(*args):
    return call(other_kernel, G_SHAPE, VMEM, [SMEM] + [VMEM] * 3)(*args)


COUPLINGS = [SMEM, SMEM, VMEM, VMEM, SMEM, VMEM, VMEM]


def late_fates(*args):
    return call(late_kernel, FATE_SHAPE, VMEM, COUPLINGS + [VMEM] * 3, HOLD + [TERMS], mib=12)(*args)


def early_weights(*args):
    return call(early_weights_kernel, (W_SHAPE, COLUMN_SHAPE), (VMEM, VMEM), COUPLINGS, [TERMS])(*args)


def early_near(*args):
    return call(early_near_kernel, TOTAL_SHAPE, VMEM, [VMEM] * 3)(*args)


def early_fates(*args):
    return call(early_kernel, FATE_SHAPE, VMEM, [VMEM] * 4)(*args)


def merged(first, second):
    highest = jnp.maximum(first[0], second[0])
    return jnp.stack(
        [
            highest,
            first[1] * jnp.exp2(first[0] - highest) + second[1] * jnp.exp2(second[0] - highest),
        ]
    )


def folded(part, beside=lambda message: None):
    own = merged(part[:, :NBLK], sibling(part[:, NBLK : 2 * NBLK]))
    beyond = part[:, 2 * NBLK :]
    message = jnp.concatenate([own, beyond], axis=1)
    arrived, made = lax.optimization_barrier((outward(message), beside(message)))
    own = merged(own, arrived[:, NBLK:])
    out = merged(arrived[:, :NBLK], beyond)
    own_total = own[0] + jnp.log2(own[1])
    out_total = out[0] + jnp.log2(out[1])
    return jnp.concatenate([own_total, sibling(own_total), out_total], axis=0), made


def shifted(value, steps):
    count = lax.axis_size("tiles")
    return lax.ppermute(value, "tiles", [(t, (t + steps) % count) for t in range(count)])


def on_device(embeddings, log_mass, signatures, tile_list):
    owner = lax.axis_index("cells").astype(jnp.int32)
    group = (lax.axis_index("tiles") >= 2).astype(jnp.int32)
    place, place_other = jnp.stack([owner, group]), jnp.stack([owner, 1 - group])

    def moment(index):
        return lax.dynamic_index_in_dim(embeddings, index, 0, keepdims=False)

    def after(values, gate):
        return lax.optimization_barrier((values, gate))[0]

    target = moment(group + 1)
    target_out, target_sib = outward(target), sibling(target)
    masses, slots = after((log_mass, tile_list), target_sib)
    gathered = [slots] + [shifted(slots, k) for k in range(1, lax.axis_size("tiles"))]
    masses_out, masses_sib = outward(masses), sibling(masses)
    g, kc, near = near_products(place, embeddings, masses, masses_sib, target_sib)
    gathered, masses_out = lax.optimization_barrier((gathered, masses_out))
    table = build_table(place, gathered)

    other = after(moment(2 - group), near)
    other_out, other_sib = outward(other), sibling(other)
    g, window = far_products(place, embeddings, masses_out, target_out, g, near)
    part = sweep(table, window[0], kc, g)

    def beside(message):
        (sib, out), lists = after(((other_sib, other_out), gathered), message)
        return other_products(place, embeddings, sib, out), build_table(place_other, lists)

    totals, (g_other, table_other) = folded(part, beside)
    hh = window[1] - LAM * totals
    part = sweep(table, hh, kc, g)
    fates = after(signatures, hh)
    fates_out, fates_sib = outward(fates), sibling(fates)

    hh = window[1] - LAM * folded(part)[0]
    couplings = (place, table, hh, g, table_other, mirrored(hh), g_other)
    late = late_fates(*couplings, signatures, fates_sib, fates_out)
    late_out, late_sib = outward(late), sibling(late)
    weights, sums = early_weights(*couplings)
    total = early_near(weights, late, late_sib)
    early = early_fates(weights, sums, total, late_out)
    return early, late


def solution(mesh):
    in_specs = (
        P(None, "cells", None),
        P(None, "cells"),
        P("cells", None),
        P(None, None, ("cells", "tiles")),
    )
    out_specs = (P("cells", None), P("cells", None))
    return jax.shard_map(
        on_device, mesh=mesh, in_specs=in_specs, out_specs=out_specs, check_vma=False
    )
```

time: 94.5 us -> 91.1 us (0.964); the launches traced: 94.2 us -> 92.1 us
  waiting for transfers between devices: 28.1 us -> 17.5 us
  Pallas kernels: 34.1 us -> 39.7 us
  other arithmetic: 3.54 us -> 0.24 us
  local copies, waits for them, and re-layouts: 0.22 us -> 3.43 us
  starting transfers between devices: 27.4 us -> 30.4 us
    ppermute x7, waiting for transfers between devices: 20 us -> 12.1 us  [outward(): return lax.ppermute(value, 'cells', pairs)]
    pallas_call x6 -> x9, Pallas kernels: 30.9 us -> 34.6 us  [the longest x2 8.9 us: sweep(): call(sweep_kernel, PART_SHAPE, VMEM, [SMEM] + [VMEM] * 3, SWEEP_SCRATCH)]
    ppermute x9, starting transfers between devices: 2.27 us -> 4.85 us  [sibling(): lax.ppermute(value, 'cells', [(c, c ^ 1) for c in range(lax.axis_size('ce...]
    ppermute x1, waiting for transfers between devices: 4.89 us -> 2.64 us  [mirrored(): lax.ppermute(value, 'tiles', [(t, count - 1 - t) for t in range(count)])]
    ppermute x1, starting transfers between devices: 0.09 us -> 2.27 us  [mirrored(): lax.ppermute(value, 'tiles', [(t, count - 1 - t) for t in range(count)])]
    unnamed x11 -> x12, local copies, waits for them, and re-layouts: 0.02 us -> 2.14 us
    pallas_call x1 -> x2, Pallas kernels: 3.13 us -> 5.17 us  [build_table(): call(table_kernel, jax.ShapeDtypeStruct((TABLE,), jnp.int32), SMEM, specs)]
    reduce_sum x1 -> x0, other arithmetic: 1.89 us -> none  [on_device(): norms = (jnp.sum(widened * widened, axis=2) * SCALE).reshape(3, NBLK, BLOCK)]
  transfers between devices with their start and end apart: 20 -> 20, of which waited for: 10 -> 6; matrix products, arithmetic and copies ran while one was open for 3% -> 0% of each run, Pallas kernels for 12% -> 28%
where the time goes in v1:
time: 91.1 us; the launch traced here: 92.1 us
  Pallas kernels  39.7 us (44%)
  starting transfers between devices  30.4 us (33%)
  waiting for transfers between devices  17.5 us (19%)
  local copies, waits for them, and re-layouts  3.43 us (4%)
    ppermute x7, starting transfers between devices, outward(): return lax.ppermute(value, 'cells', pairs)  18.8 us
    ppermute x7, waiting for transfers between devices, outward(): return lax.ppermute(value, 'cells', pairs)  12.1 us
    pallas_call x2, Pallas kernels, sweep(): call(sweep_kernel, PART_SHAPE, VMEM, [SMEM] + [VMEM] * 3, SWEEP_SCRATCH)  8.9 us
    pallas_call x1, Pallas kernels, late_fates(): call(late_kernel, FATE_SHAPE, VMEM, COUPLINGS + [VMEM] * 3, HOLD + [TERMS...  7.68 us
    pallas_call x2, Pallas kernels, build_table(): call(table_kernel, jax.ShapeDtypeStruct((TABLE,), jnp.int32), SMEM, specs)  5.17 us
    ppermute x9, starting transfers between devices, sibling(): lax.ppermute(value, 'cells', [(c, c ^ 1) for c in range(lax.axis_size('ce...  4.85 us
    pallas_call x1, Pallas kernels, other_products(): return call(other_kernel, G_SHAPE, VMEM, [SMEM] + [VMEM] * 3)(*args)  4.57 us
    ppermute x3, starting transfers between devices, shifted(): lax.ppermute(value, 'tiles', [(t, (t + steps) % count) for t in range(cou...  4.45 us
  transfers between devices with their start and end apart: 20, of which 6 were waited for; matrix products, arithmetic and copies ran while one was open for 0% of the time, Pallas kernels for 28%

profile of v1, /device:TPU:0, one launch (start us, length us, event | category | flops | bytes accessed | tf_op | source)
XLA Modules:
  0.0 92.1 jit_solution(6492993698761676495)
XLA Ops:
  0.6 1.3 %dynamic-slice_bitcast_fusion = (bf16[1024,256]{1,0:T(8,128)(2,1)S(1)}, bf16[1024,256]{1,0:T(8,128)(2,1)S(1)}) fusion(bf16[3,1024,256]{2,1,0:T(8,128)(2,1)} %cells_ref.5, s32[]{:T(128)S(6)} %select_n.8, s32[]{:T(128)S(6)} %select_n.7), kind=kLoop, calls=%fused_computation | loop fusion | bytes 2097160 | tf_op jit(solution)/shard_map/jit(dynamic_index_in_dim)/squeeze | solution.py:383
  2.0 6.7 %collective-permute-start.5 = (bf16[1024,256]{1,0:T(8,128)(2,1)S(1)}, bf16[1024,256]{1,0:T(8,128)(2,1)S(1)}, u32[]{:S(2)}, u32[]{:S(2)}) collective-permute-start(bf16[1024,256]{1,0:T(8,128)(2,1)S(1)} %get-tuple-element.57), channel_id=1, source_target_pairs={{0,124},{4,8},{8,4},{12,16},{16,12},{20,24},{24,20},{28,32},{32,28... | collective-permute-start | bytes 1572872 | tf_op jit(solution)/shard_map/ppermute | solution.py:38
  8.8 2.8 %collective-permute-start.3 = (s32[2,2,32]{2,1,0:T(2,128)}, s32[2,2,32]{2,1,0:T(2,128)S(1)}, u32[]{:S(2)}, u32[]{:S(2)}) collective-permute-start(s32[2,2,32]{2,1,0:T(2,128)} %refs_0_.1), channel_id=1, source_target_pairs={{0,3},{1,0},{2,1},{3,2},{4,7},{5,4},{6,5},{7,6},{8,11},{9,8},{10,9... | collective-permute-start | bytes 1544 | tf_op jit(solution)/shard_map/ppermute | solution.py:374
  11.5 0.8 collective-permute-start.2
  12.3 0.9 collective-permute-start.1
  13.2 1.1 %collective-permute-start.4 = (f32[3,1024]{1,0:T(4,128)}, f32[3,1024]{1,0:T(4,128)S(1)}, u32[]{:S(2)}, u32[]{:S(2)}) collective-permute-start(f32[3,1024]{1,0:T(4,128)} %mass_ref), channel_id=1, source_target_pairs={{0,124},{4,8},{8,4},{12,16},{16,12},{20,24},{24,20},{28,32},{32,28... | collective-permute-start | bytes 36872 | tf_op jit(solution)/shard_map/ppermute | solution.py:38
  14.3 1.4 %copy-done = bf16[3,1024,256]{2,1,0:T(8,128)(2,1)S(1)} copy-done((bf16[3,1024,256]{2,1,0:T(8,128)(2,1)S(1)}, bf16[3,1024,256]{2,1,0:T(8,128)(2,1)}, u32[]{:S(2)}) %copy-start) | copy-done | bytes 1572888
  15.7 0.7 copy-done.4
  16.4 4.0 %shard_map.60 = (f32[25,1024,128]{2,1,0:T(8,128)S(1)}, f32[1024,128]{1,0:T(8,128)S(1)}, f32[2,16,128]{2,1,0:T(8,128)S(1)}) custom-call(s32[2]{0:T(128)S(1)} %pad_add_fusion.place_ref, bf16[3,1024,256]{2,1,0:T(8,128)(2,1)S(1)} %copy-done, f32[3,1024]{1,0:T(4,128)S(1)} %copy-done.4, f32[3,1024]{1,0:T(4,128)S(1)} %collective-permute-done.6.sib_mass_ref, ...), custom_call_target="tpu_custom_call" | custom-call | flops 3000000000 | bytes 10000 | tf_op jit(solution)/shard_map/pallas_call | solution.py:316
  20.4 4.1 %collective-permute-start.10 = (bf16[1024,256]{1,0:T(8,128)(2,1)S(1)}, bf16[1024,256]{1,0:T(8,128)(2,1)S(1)}, u32[]{:S(2)}, u32[]{:S(2)}) collective-permute-start(bf16[1024,256]{1,0:T(8,128)(2,1)S(1)} %get-tuple-element.39), channel_id=1, source_target_pairs={{0,124},{4,8},{8,4},{12,16},{16,12},{20,24},{24,20},{28,32},{32,28... | collective-permute-start | bytes 1572872 | tf_op jit(solution)/shard_map/ppermute | solution.py:38
  24.5 2.3 %shard_map.61 = (f32[25,1024,128]{2,1,0:T(8,128)S(1)}, f32[2,24,128]{2,1,0:T(8,128)S(1)}) custom-call(s32[2]{0:T(128)S(1)} %pad_add_fusion.place_ref, bf16[3,1024,256]{2,1,0:T(8,128)(2,1)S(1)} %copy-done, f32[3,1024]{1,0:T(4,128)S(1)} %collective-permute-done.4.out_mass_ref, ...), custom_call_target="tpu_custom_call", output_to_operand_aliasing={{0}: (4, {})} | custom-call | flops 3000000000 | bytes 10000 | tf_op jit(solution)/shard_map/pallas_call | solution.py:320
  26.8 2.6 %shard_map.59.table_ref = s32[256]{0:T(256)S(1)} custom-call(s32[2]{0:T(128)S(1)} %pad_add_fusion.place_ref, s32[2,2,32]{2,1,0:T(2,128)S(1)} %copy-done.5, s32[2,2,32]{2,1,0:T(2,128)S(1)} %collective-permute-done.1.refs_1_, s32[2,2,32]{2,1,0:T(2,128)S(1)} %collective-permute-done.2.refs_2_, s32[2,2,32]{2,1,0:T(2,128)S(1)} %collective-permute-done.3.refs_3_), custom_call_target="tpu_custom_call" | custom-call | flops 3000000000 | bytes 10000 | tf_op jit(solution)/shard_map/pallas_call | solution.py:312
  29.4 4.5 %shard_map.62 = f32[2,24,128]{2,1,0:T(8,128)S(1)} custom-call(s32[256]{0:T(256)S(1)} %shard_map.59.table_ref, f32[24,128]{1,0:T(8,128)S(1)} %slice_bitcast_fusion.hh_ref, f32[1024,128]{1,0:T(8,128)S(1)} %get-tuple-element.37.kc_ref, f32[25,1024,128]{2,1,0:T(8,128)S(1)} %get-tuple-element.38.g_ref), custom_call_target="tpu_custom_call" | custom-call | flops 3000000000 | bytes 10000 | tf_op jit(solution)/shard_map/pallas_call | solution.py:324
  33.8 2.2 %collective-permute-start.7 = (f32[2,8,128]{2,1,0:T(8,128)S(1)}, f32[2,8,128]{2,1,0:T(8,128)S(1)}, u32[]{:S(2)}, u32[]{:S(2)}) collective-permute-start(f32[2,8,128]{2,1,0:T(8,128)S(1)} %get-tuple-element.64), channel_id=1, source_target_pairs={{0,4},{4,0},{8,12},{12,8},{16,20},{20,16},{24,28},{28,24},{32,36},... | collective-permute-start | bytes 24584 | tf_op jit(solution)/shard_map/ppermute | solution.py:32
  36.1 0.8 collective-permute-done.7
  37.0 4.6 %shard_map.63.g2_ref = f32[25,1024,128]{2,1,0:T(8,128)S(1)} custom-call(s32[2]{0:T(128)S(1)} %pad_add_fusion.place_ref, bf16[3,1024,256]{2,1,0:T(8,128)(2,1)S(1)} %copy-done.1, bf16[1024,256]{1,0:T(8,128)(2,1)S(1)} %collective-permute-done.9.sib_ref, bf16[1024,256]{1,0:T(8,128)(2,1)S(1)} %collective-permute-done.10.out_ref), custom_call_target="tpu_custom_call" | custom-call | flops 3000000000 | bytes 10000 | tf_op jit(solution)/shard_map/pallas_call | solution.py:328
  41.6 2.6 %shard_map.64.table2_ref = s32[256]{0:T(256)S(1)} custom-call(s32[2]{0:T(128)S(1)} %pad_add_fusion.1.place_ref, s32[2,2,32]{2,1,0:T(2,128)S(1)} %copy-done.5, s32[2,2,32]{2,1,0:T(2,128)S(1)} %collective-permute-done.1.refs_1_, s32[2,2,32]{2,1,0:T(2,128)S(1)} %collective-permute-done.2.refs_2_, s32[2,2,32]{2,1,0:T(2,128)S(1)} %collective-permute-done.3.refs_3_), custom_call_target="tpu_custom_call" | custom-call | flops 3000000000 | bytes 10000 | tf_op jit(solution)/shard_map/pallas_call | solution.py:312
  44.7 0.8 collective-permute-done.11
  45.5 4.4 %shard_map.65 = f32[2,24,128]{2,1,0:T(8,128)S(1)} custom-call(s32[256]{0:T(256)S(1)} %shard_map.59.table_ref, f32[24,128]{1,0:T(8,128)S(1)} %fusion.hh_ref, f32[1024,128]{1,0:T(8,128)S(1)} %get-tuple-element.37.kc_ref, f32[25,1024,128]{2,1,0:T(8,128)S(1)} %get-tuple-element.38.g_ref), custom_call_target="tpu_custom_call" | custom-call | flops 3000000000 | bytes 10000 | tf_op jit(solution)/shard_map/pallas_call | solution.py:324
  50.0 2.0 %collective-permute-start.12 = (f32[2,8,128]{2,1,0:T(8,128)S(1)}, f32[2,8,128]{2,1,0:T(8,128)S(1)}, u32[]{:S(2)}, u32[]{:S(2)}) collective-permute-start(f32[2,8,128]{2,1,0:T(8,128)S(1)} %get-tuple-element.62), channel_id=1, source_target_pairs={{0,4},{4,0},{8,12},{12,8},{16,20},{20,16},{24,28},{28,24},{32,36},... | collective-permute-start | bytes 24584 | tf_op jit(solution)/shard_map/ppermute | solution.py:32
  52.0 3.3 %collective-permute-start.17 = (bf16[1024,256]{1,0:T(8,128)(2,1)S(1)}, bf16[1024,256]{1,0:T(8,128)(2,1)S(1)}, u32[]{:S(2)}, u32[]{:S(2)}) collective-permute-start(bf16[1024,256]{1,0:T(8,128)(2,1)S(1)} %copy-done.2), channel_id=1, source_target_pairs={{0,124},{4,8},{8,4},{12,16},{16,12},{20,24},{24,20},{28,32},{32,28... | collective-permute-start | bytes 1572872 | tf_op jit(solution)/shard_map/ppermute | solution.py:38
  55.3 1.9 %collective-permute-start.13 = (f32[2,16,128]{2,1,0:T(8,128)S(1)}, f32[2,16,128]{2,1,0:T(8,128)S(1)}, u32[]{:S(2)}, u32[]{:S(2)}) collective-permute-start(f32[2,16,128]{2,1,0:T(8,128)S(1)} %pad_maximum_fusion.1), channel_id=1, source_target_pairs={{0,124},{4,8},{8,4},{12,16},{16,12},{20,24},{24,20},{28,32},{32,28... | collective-permute-start | bytes 49160 | tf_op jit(solution)/shard_map/ppermute | solution.py:38
  57.2 6.9 %collective-permute-done.13 = f32[2,16,128]{2,1,0:T(8,128)S(1)} collective-permute-done((f32[2,16,128]{2,1,0:T(8,128)S(1)}, f32[2,16,128]{2,1,0:T(8,128)S(1)}, u32[]{:S(2)}, u32[]{:S(2)}) %collective-permute-start.13) | collective-permute-done | bytes 16416 | tf_op jit(solution)/shard_map/ppermute | solution.py:38
  64.2 1.2 %collective-permute-done.14 = f32[8,128]{1,0:T(8,128)S(1)} collective-permute-done((f32[8,128]{1,0:T(8,128)S(1)}, f32[8,128]{1,0:T(8,128)S(1)}, u32[]{:S(2)}, u32[]{:S(2)}) %collective-permute-start.14) | collective-permute-done | bytes 4128 | tf_op jit(solution)/shard_map/ppermute | solution.py:32
  65.4 2.3 %collective-permute-start.15 = (f32[24,128]{1,0:T(8,128)S(1)}, f32[24,128]{1,0:T(8,128)S(1)}, u32[]{:S(2)}, u32[]{:S(2)}) collective-permute-start(f32[24,128]{1,0:T(8,128)S(1)} %fusion.1.hh_ref), channel_id=1, source_target_pairs={{0,3},{1,2},{2,1},{3,0},{4,7},{5,6},{6,5},{7,4},{8,11},{9,10},{10,... | collective-permute-start | bytes 36872 | tf_op jit(solution)/shard_map/ppermute | solution.py:43
  67.7 2.6 %collective-permute-done.15.hh2_ref = f32[24,128]{1,0:T(8,128)S(1)} collective-permute-done((f32[24,128]{1,0:T(8,128)S(1)}, f32[24,128]{1,0:T(8,128)S(1)}, u32[]{:S(2)}, u32[]{:S(2)}) %collective-permute-start.15) | collective-permute-done | bytes 12320 | tf_op jit(solution)/shard_map/ppermute | solution.py:43
  70.3 7.7 %shard_map.67.own_ref = bf16[1024,256]{1,0:T(8,128)(2,1)} custom-call(s32[2]{0:T(128)S(1)} %pad_add_fusion.place_ref, s32[256]{0:T(256)S(1)} %shard_map.59.table_ref, f32[24,128]{1,0:T(8,128)S(1)} %fusion.1.hh_ref, f32[25,1024,128]{2,1,0:T(8,128)S(1)} %get-tuple-element.38.g_ref, s32[256]{0:T(256)S(1)} %shard_map.64.table2_ref, ...), custom_call_target="tpu_custom_call" | custom-call | flops 3000000000 | bytes 10000 | tf_op jit(solution)/shard_map/pallas_call | solution.py:335
  78.0 1.7 %collective-permute-start.19 = (bf16[1024,256]{1,0:T(8,128)(2,1)}, bf16[1024,256]{1,0:T(8,128)(2,1)S(1)}, u32[]{:S(2)}, u32[]{:S(2)}) collective-permute-start(bf16[1024,256]{1,0:T(8,128)(2,1)} %shard_map.67.own_ref), channel_id=1, source_target_pairs={{0,124},{4,8},{8,4},{12,16},{16,12},{20,24},{24,20},{28,32},{32,28... | collective-permute-start | bytes 1572872 | tf_op jit(solution)/shard_map/ppermute | solution.py:38
  79.7 3.4 %shard_map.66 = (bf16[1024,3200]{1,0:T(8,128)(2,1)S(1)}, f32[1024,128]{1,0:T(8,128)S(1)}) custom-call(s32[2]{0:T(128)S(1)} %pad_add_fusion.place_ref, s32[256]{0:T(256)S(1)} %shard_map.59.table_ref, f32[24,128]{1,0:T(8,128)S(1)} %fusion.1.hh_ref, f32[25,1024,128]{2,1,0:T(8,128)S(1)} %get-tuple-element.38.g_ref, s32[256]{0:T(256)S(1)} %shard_map.64.table2_ref, ...), custom_call_target="tpu_custom_call" | custom-call | flops 3000000000 | bytes 10000 | tf_op jit(solution)/shard_map/pallas_call | solution.py:339
  83.2 1.8 %shard_map.68.total_ref = f32[1024,256]{1,0:T(8,128)S(1)} custom-call(bf16[1024,3200]{1,0:T(8,128)(2,1)S(1)} %get-tuple-element.49.w_ref, bf16[1024,256]{1,0:T(8,128)(2,1)S(1)} %copy-done.3, bf16[1024,256]{1,0:T(8,128)(2,1)S(1)} %collective-permute-done.18.sib_ref), custom_call_target="tpu_custom_call" | custom-call | flops 3000000000 | bytes 10000 | tf_op jit(solution)/shard_map/pallas_call | solution.py:343
  84.9 5.2 %collective-permute-done.19.out_ref = bf16[1024,256]{1,0:T(8,128)(2,1)S(1)} collective-permute-done((bf16[1024,256]{1,0:T(8,128)(2,1)}, bf16[1024,256]{1,0:T(8,128)(2,1)S(1)}, u32[]{:S(2)}, u32[]{:S(2)}) %collective-permute-start.19) | collective-permute-done | bytes 524320 | tf_op jit(solution)/shard_map/ppermute | solution.py:38
  90.1 2.0 %shard_map.69 = bf16[1024,256]{1,0:T(8,128)(2,1)} custom-call(bf16[1024,3200]{1,0:T(8,128)(2,1)S(1)} %get-tuple-element.49.w_ref, f32[1024,128]{1,0:T(8,128)S(1)} %get-tuple-element.50.sum_ref, f32[1024,256]{1,0:T(8,128)S(1)} %shard_map.68.total_ref, bf16[1024,256]{1,0:T(8,128)(2,1)S(1)} %collective-permute-done.19.out_ref), custom_call_target="tpu_custom_call" | custom-call | flops 3000000000 | bytes 10000 | tf_op jit(solution)/shard_map/pallas_call | solution.py:347
  (45 shorter events, 1.1 us)
Async XLA Ops:
  1.9 6.8 %collective-permute-start = (bf16[1024,256]{1,0:T(8,128)(2,1)S(1)}, bf16[1024,256]{1,0:T(8,128)(2,1)S(1)}, u32[]{:S(2)}, u32[]{:S(2)}) collective-permute-start(bf16[1024,256]{1,0:T(8,128)(2,1)S(1)} %get-tuple-element.57), channel_id=1, source_target_pairs={{0,4},{4,0},{8,12},{12,8},{16,20},{20,16},{24,28},{28,24},{32,36},... | collective-permute-start | bytes 1572872 | tf_op jit(solution)/shard_map/ppermute | solution.py:32
  2.0 22.5 %collective-permute-start.5 = (bf16[1024,256]{1,0:T(8,128)(2,1)S(1)}, bf16[1024,256]{1,0:T(8,128)(2,1)S(1)}, u32[]{:S(2)}, u32[]{:S(2)}) collective-permute-start(bf16[1024,256]{1,0:T(8,128)(2,1)S(1)} %get-tuple-element.57), channel_id=1, source_target_pairs={{0,124},{4,8},{8,4},{12,16},{16,12},{20,24},{24,20},{28,32},{32,28... | collective-permute-start | bytes 1572872 | tf_op jit(solution)/shard_map/ppermute | solution.py:38
  8.7 4.5 %collective-permute-start.6 = (f32[3,1024]{1,0:T(4,128)}, f32[3,1024]{1,0:T(4,128)S(1)}, u32[]{:S(2)}, u32[]{:S(2)}) collective-permute-start(f32[3,1024]{1,0:T(4,128)} %mass_ref), channel_id=1, source_target_pairs={{0,4},{4,0},{8,12},{12,8},{16,20},{20,16},{24,28},{28,24},{32,36},... | collective-permute-start | bytes 36872 | tf_op jit(solution)/shard_map/ppermute | solution.py:32
  8.7 18.1 %copy-start.5 = (s32[2,2,32]{2,1,0:T(2,128)S(1)}, s32[2,2,32]{2,1,0:T(2,128)}, u32[]{:S(2)}) copy-start(s32[2,2,32]{2,1,0:T(2,128)} %refs_0_.1) | copy-start | bytes 1540
  8.8 11.6 %collective-permute-start.3 = (s32[2,2,32]{2,1,0:T(2,128)}, s32[2,2,32]{2,1,0:T(2,128)S(1)}, u32[]{:S(2)}, u32[]{:S(2)}) collective-permute-start(s32[2,2,32]{2,1,0:T(2,128)} %refs_0_.1), channel_id=1, source_target_pairs={{0,3},{1,0},{2,1},{3,2},{4,7},{5,4},{6,5},{7,6},{8,11},{9,8},{10,9... | collective-permute-start | bytes 1544 | tf_op jit(solution)/shard_map/ppermute | solution.py:374
  11.5 12.9 %collective-permute-start.2 = (s32[2,2,32]{2,1,0:T(2,128)}, s32[2,2,32]{2,1,0:T(2,128)S(1)}, u32[]{:S(2)}, u32[]{:S(2)}) collective-permute-start(s32[2,2,32]{2,1,0:T(2,128)} %refs_0_.1), channel_id=1, source_target_pairs={{0,2},{1,3},{2,0},{3,1},{4,6},{5,7},{6,4},{7,5},{8,10},{9,11},{10,... | collective-permute-start | bytes 1544 | tf_op jit(solution)/shard_map/ppermute | solution.py:374
  12.3 12.1 %collective-permute-start.1 = (s32[2,2,32]{2,1,0:T(2,128)}, s32[2,2,32]{2,1,0:T(2,128)S(1)}, u32[]{:S(2)}, u32[]{:S(2)}) collective-permute-start(s32[2,2,32]{2,1,0:T(2,128)} %refs_0_.1), channel_id=1, source_target_pairs={{0,1},{1,2},{2,3},{3,0},{4,5},{5,6},{6,7},{7,4},{8,9},{9,10},{10,1... | collective-permute-start | bytes 1544 | tf_op jit(solution)/shard_map/ppermute | solution.py:374
  13.2 11.3 %collective-permute-start.4 = (f32[3,1024]{1,0:T(4,128)}, f32[3,1024]{1,0:T(4,128)S(1)}, u32[]{:S(2)}, u32[]{:S(2)}) collective-permute-start(f32[3,1024]{1,0:T(4,128)} %mass_ref), channel_id=1, source_target_pairs={{0,124},{4,8},{8,4},{12,16},{16,12},{20,24},{24,20},{28,32},{32,28... | collective-permute-start | bytes 36872 | tf_op jit(solution)/shard_map/ppermute | solution.py:38
  14.3 1.4 %copy-start = (bf16[3,1024,256]{2,1,0:T(8,128)(2,1)S(1)}, bf16[3,1024,256]{2,1,0:T(8,128)(2,1)}, u32[]{:S(2)}) copy-start(bf16[3,1024,256]{2,1,0:T(8,128)(2,1)} %cells_ref.5) | copy-start | bytes 4718596
  15.7 0.7 copy-start.4
  20.4 16.6 %collective-permute-start.10 = (bf16[1024,256]{1,0:T(8,128)(2,1)S(1)}, bf16[1024,256]{1,0:T(8,128)(2,1)S(1)}, u32[]{:S(2)}, u32[]{:S(2)}) collective-permute-start(bf16[1024,256]{1,0:T(8,128)(2,1)S(1)} %get-tuple-element.39), channel_id=1, source_target_pairs={{0,124},{4,8},{8,4},{12,16},{16,12},{20,24},{24,20},{28,32},{32,28... | collective-permute-start | bytes 1572872 | tf_op jit(solution)/shard_map/ppermute | solution.py:38
  24.5 12.5 %collective-permute-start.9 = (bf16[1024,256]{1,0:T(8,128)(2,1)S(1)}, bf16[1024,256]{1,0:T(8,128)(2,1)S(1)}, u32[]{:S(2)}, u32[]{:S(2)}) collective-permute-start(bf16[1024,256]{1,0:T(8,128)(2,1)S(1)} %get-tuple-element.39), channel_id=1, source_target_pairs={{0,4},{4,0},{8,12},{12,8},{16,20},{20,16},{24,28},{28,24},{32,36},... | collective-permute-start | bytes 1572872 | tf_op jit(solution)/shard_map/ppermute | solution.py:32
  26.8 10.2 %copy-start.1 = (bf16[3,1024,256]{2,1,0:T(8,128)(2,1)S(1)}, bf16[3,1024,256]{2,1,0:T(8,128)(2,1)}, u32[]{:S(2)}) copy-start(bf16[3,1024,256]{2,1,0:T(8,128)(2,1)} %cells_ref.5) | copy-start | bytes 4718596
  33.8 3.0 %collective-permute-start.7 = (f32[2,8,128]{2,1,0:T(8,128)S(1)}, f32[2,8,128]{2,1,0:T(8,128)S(1)}, u32[]{:S(2)}, u32[]{:S(2)}) collective-permute-start(f32[2,8,128]{2,1,0:T(8,128)S(1)} %get-tuple-element.64), channel_id=1, source_target_pairs={{0,4},{4,0},{8,12},{12,8},{16,20},{20,16},{24,28},{28,24},{32,36},... | collective-permute-start | bytes 24584 | tf_op jit(solution)/shard_map/ppermute | solution.py:32
  36.9 7.3 %collective-permute-start.8 = (f32[2,16,128]{2,1,0:T(8,128)S(1)}, f32[2,16,128]{2,1,0:T(8,128)S(1)}, u32[]{:S(2)}, u32[]{:S(2)}) collective-permute-start(f32[2,16,128]{2,1,0:T(8,128)S(1)} %pad_maximum_fusion), channel_id=1, source_target_pairs={{0,124},{4,8},{8,4},{12,16},{16,12},{20,24},{24,20},{28,32},{32,28... | collective-permute-start | bytes 49160 | tf_op jit(solution)/shard_map/ppermute | solution.py:38
  41.6 10.4 %copy-start.2 = (bf16[1024,256]{1,0:T(8,128)(2,1)S(1)}, bf16[1024,256]{1,0:T(8,128)(2,1)}, u32[]{:S(2)}) copy-start(bf16[1024,256]{1,0:T(8,128)(2,1)} %own_ref.1) | copy-start | bytes 1572868
  44.2 1.3 %collective-permute-start.11 = (f32[8,128]{1,0:T(8,128)S(1)}, f32[8,128]{1,0:T(8,128)S(1)}, u32[]{:S(2)}, u32[]{:S(2)}) collective-permute-start(f32[8,128]{1,0:T(8,128)S(1)} %get-tuple-element.60), channel_id=1, source_target_pairs={{0,4},{4,0},{8,12},{12,8},{16,20},{20,16},{24,28},{28,24},{32,36},... | collective-permute-start | bytes 12296 | tf_op jit(solution)/shard_map/ppermute | solution.py:32
  50.0 5.3 %collective-permute-start.12 = (f32[2,8,128]{2,1,0:T(8,128)S(1)}, f32[2,8,128]{2,1,0:T(8,128)S(1)}, u32[]{:S(2)}, u32[]{:S(2)}) collective-permute-start(f32[2,8,128]{2,1,0:T(8,128)S(1)} %get-tuple-element.62), channel_id=1, source_target_pairs={{0,4},{4,0},{8,12},{12,8},{16,20},{20,16},{24,28},{28,24},{32,36},... | collective-permute-start | bytes 24584 | tf_op jit(solution)/shard_map/ppermute | solution.py:32
  52.0 18.3 %collective-permute-start.17 = (bf16[1024,256]{1,0:T(8,128)(2,1)S(1)}, bf16[1024,256]{1,0:T(8,128)(2,1)S(1)}, u32[]{:S(2)}, u32[]{:S(2)}) collective-permute-start(bf16[1024,256]{1,0:T(8,128)(2,1)S(1)} %copy-done.2), channel_id=1, source_target_pairs={{0,124},{4,8},{8,4},{12,16},{16,12},{20,24},{24,20},{28,32},{32,28... | collective-permute-start | bytes 1572872 | tf_op jit(solution)/shard_map/ppermute | solution.py:38
  55.3 15.0 %collective-permute-start.16 = (bf16[1024,256]{1,0:T(8,128)(2,1)S(1)}, bf16[1024,256]{1,0:T(8,128)(2,1)S(1)}, u32[]{:S(2)}, u32[]{:S(2)}) collective-permute-start(bf16[1024,256]{1,0:T(8,128)(2,1)S(1)} %copy-done.2), channel_id=1, source_target_pairs={{0,4},{4,0},{8,12},{12,8},{16,20},{20,16},{24,28},{28,24},{32,36},... | collective-permute-start | bytes 1572872 | tf_op jit(solution)/shard_map/ppermute | solution.py:32
  55.3 8.8 %collective-permute-start.13 = (f32[2,16,128]{2,1,0:T(8,128)S(1)}, f32[2,16,128]{2,1,0:T(8,128)S(1)}, u32[]{:S(2)}, u32[]{:S(2)}) collective-permute-start(f32[2,16,128]{2,1,0:T(8,128)S(1)} %pad_maximum_fusion.1), channel_id=1, source_target_pairs={{0,124},{4,8},{8,4},{12,16},{16,12},{20,24},{24,20},{28,32},{32,28... | collective-permute-start | bytes 49160 | tf_op jit(solution)/shard_map/ppermute | solution.py:38
  64.1 1.2 %collective-permute-start.14 = (f32[8,128]{1,0:T(8,128)S(1)}, f32[8,128]{1,0:T(8,128)S(1)}, u32[]{:S(2)}, u32[]{:S(2)}) collective-permute-start(f32[8,128]{1,0:T(8,128)S(1)} %get-tuple-element.58), channel_id=1, source_target_pairs={{0,4},{4,0},{8,12},{12,8},{16,20},{20,16},{24,28},{28,24},{32,36},... | collective-permute-start | bytes 12296 | tf_op jit(solution)/shard_map/ppermute | solution.py:32
  65.4 4.9 %collective-permute-start.15 = (f32[24,128]{1,0:T(8,128)S(1)}, f32[24,128]{1,0:T(8,128)S(1)}, u32[]{:S(2)}, u32[]{:S(2)}) collective-permute-start(f32[24,128]{1,0:T(8,128)S(1)} %fusion.1.hh_ref), channel_id=1, source_target_pairs={{0,3},{1,2},{2,1},{3,0},{4,7},{5,6},{6,5},{7,4},{8,11},{9,10},{10,... | collective-permute-start | bytes 36872 | tf_op jit(solution)/shard_map/ppermute | solution.py:43
  78.0 5.2 %copy-start.3 = (bf16[1024,256]{1,0:T(8,128)(2,1)S(1)}, bf16[1024,256]{1,0:T(8,128)(2,1)}, u32[]{:S(2)}) copy-start(bf16[1024,256]{1,0:T(8,128)(2,1)} %shard_map.67.own_ref) | copy-start | bytes 1572868
  78.0 5.2 %collective-permute-start.18 = (bf16[1024,256]{1,0:T(8,128)(2,1)}, bf16[1024,256]{1,0:T(8,128)(2,1)S(1)}, u32[]{:S(2)}, u32[]{:S(2)}) collective-permute-start(bf16[1024,256]{1,0:T(8,128)(2,1)} %shard_map.67.own_ref), channel_id=1, source_target_pairs={{0,4},{4,0},{8,12},{12,8},{16,20},{20,16},{24,28},{28,24},{32,36},... | collective-permute-start | bytes 1572872 | tf_op jit(solution)/shard_map/ppermute | solution.py:32
  78.0 12.1 %collective-permute-start.19 = (bf16[1024,256]{1,0:T(8,128)(2,1)}, bf16[1024,256]{1,0:T(8,128)(2,1)S(1)}, u32[]{:S(2)}, u32[]{:S(2)}) collective-permute-start(bf16[1024,256]{1,0:T(8,128)(2,1)} %shard_map.67.own_ref), channel_id=1, source_target_pairs={{0,124},{4,8},{8,4},{12,16},{16,12},{20,24},{24,20},{28,32},{32,28... | collective-permute-start | bytes 1572872 | tf_op jit(solution)/shard_map/ppermute | solution.py:38

commit v2 on v1

v2 whole, which is shorter than its diff:
```python
import jax
import jax.numpy as jnp
from jax import lax
from jax.experimental import pallas as pl
from jax.experimental.pallas import tpu as pltpu
from jax.sharding import PartitionSpec as P

EMB = 256
BLOCK = 128
NBLK = 8
WIN = 3 * NBLK
CELLS = NBLK * BLOCK
EPS = 0.01
RHO = 1.0
LAM = RHO / (RHO + EPS)
BIG = 1e30

LOG2E = 1.4426950408889634
SCALE = LOG2E / (EMB * EPS)

QUAD = 4
STRIDE = WIN + QUAD
GROUPS = 384
TABLE = 512

FLOPS, BYTES, MIB = 3 * 10**9, 10**4, 4
VMEM = pl.BlockSpec(memory_space=pltpu.VMEM)
SMEM = pl.BlockSpec(memory_space=pltpu.SMEM)
ANY = pl.BlockSpec(memory_space=pl.ANY)


def sibling(value):
    return lax.ppermute(value, "cells", [(c, c ^ 1) for c in range(lax.axis_size("cells"))])


def outward(value):
    count = lax.axis_size("cells")
    pairs = [(c, (c + 1 if c % 2 else c - 1) % count) for c in range(count)]
    return lax.ppermute(value, "cells", pairs)


def mirrored(value):
    count = lax.axis_size("tiles")
    return lax.ppermute(value, "tiles", [(t, count - 1 - t) for t in range(count)])


def call(kernel, outs, out_specs, in_specs, scratch=(), aliases=None, flops=FLOPS, mib=MIB):
    return pl.pallas_call(
        kernel,
        out_shape=outs,
        in_specs=in_specs,
        out_specs=out_specs,
        scratch_shapes=list(scratch),
        input_output_aliases=aliases or {},
        compiler_params=pltpu.CompilerParams(vmem_limit_bytes=mib << 20),
        cost_estimate=pl.CostEstimate(flops=flops, bytes_accessed=BYTES, transcendentals=0),
    )


def table_kernel(place_ref, behind_ref, *refs):
    del behind_ref
    *slot_refs, table_ref = refs
    owner, coupling = place_ref[0], place_ref[1]
    for s in range(NBLK + 1):
        table_ref[GROUPS + s] = 0

    @pl.loop(0, slot_refs[0].shape[2] // 2)
    def _(pair):
        for slot_ref in slot_refs:
            for half in range(2):
                source = slot_ref[coupling, 0, 2 * pair + half]
                target = slot_ref[coupling, 1, 2 * pair + half]
                away = target >> 3
                region = jnp.where(away == owner, 0, jnp.where(away == (owner ^ 1), NBLK, 2 * NBLK))
                s = jnp.where(source < 0, NBLK, source & 7)
                count = table_ref[GROUPS + s]
                table_ref[GROUPS + s] = count + 1
                table_ref[s * STRIDE + count] = region + (target & 7)

    for s in range(NBLK):
        count = table_ref[GROUPS + s]
        for extra in range(QUAD - 1):
            table_ref[s * STRIDE + count + extra] = WIN
        table_ref[GROUPS + s] = (count + QUAD - 1) >> 2


def products(source_ref, target_refs, g_ref, first):
    for region, target_ref in enumerate(target_refs, first):

        @pl.loop(0, NBLK // 2)
        def _(pair):
            rows = target_ref[pl.ds(pl.multiple_of(pair * 256, 256), 256), :]
            g = lax.dot_general(
                source_ref[...], rows, (((1,), (1,)), ((), ())), preferred_element_type=jnp.float32
            ) * (2.0 * SCALE)
            g_ref[region * NBLK + 2 * pair] = g[:, :BLOCK]
            g_ref[region * NBLK + 2 * pair + 1] = g[:, BLOCK:]


def target_constants(target_ref, mass_row, window_ref, region):
    ones = jnp.ones((8, EMB), jnp.bfloat16)
    for pair in range(NBLK // 2):
        y = target_ref[pair * 256 : (pair + 1) * 256, :].astype(jnp.float32)
        square = y * y
        high = square.astype(jnp.bfloat16)
        low = (square - high.astype(jnp.float32)).astype(jnp.bfloat16)
        norm = sum(
            lax.dot_general(ones, part, (((1,), (1,)), ((), ())), preferred_element_type=jnp.float32)
            for part in (high, low)
        )
        for half in range(2):
            block = 2 * pair + half
            scaled = norm[:1, half * BLOCK : (half + 1) * BLOCK] * SCALE
            mass = mass_row(block) * LOG2E
            at = region * NBLK + block
            window_ref[0, at : at + 1, :] = mass - scaled
            window_ref[1, at : at + 1, :] = mass + (LAM - 1.0) * scaled


def mass_rows(mass_ref, group, first):
    def row(block):
        lanes = slice(block * BLOCK, (block + 1) * BLOCK)
        low, high = mass_ref[first : first + 1, lanes], mass_ref[first + 1 : first + 2, lanes]
        return jnp.where(group == 0, low, high)

    return row


STRIPS = BLOCK // 8


def extended(hh_ref, terms_ref):
    for t in range(WIN):
        terms_ref[t] = jnp.broadcast_to(hh_ref[t : t + 1, :], (8, BLOCK))
    terms_ref[WIN] = jnp.full((8, BLOCK), -BIG, jnp.float32)


def source_rows(s):
    return pl.ds(pl.multiple_of(s * BLOCK, BLOCK), BLOCK)


def group_targets(table_ref, s, q):
    return [table_ref[s * STRIDE + q * QUAD + k] for k in range(QUAD)]


def strips(g_ref, t, s):
    return g_ref[jnp.minimum(t, WIN - 1), source_rows(s), :].reshape(STRIPS, 8, BLOCK)


def row_maxima(table_ref, terms_ref, g_ref, m_ref):
    @pl.loop(0, NBLK)
    def _(s):
        def step(q, highest):
            v = [strips(g_ref, t, s) + terms_ref[t] for t in group_targets(table_ref, s, q)]
            return jnp.maximum(highest, jnp.maximum(jnp.maximum(v[0], v[1]), jnp.maximum(v[2], v[3])))

        start = jnp.full((STRIPS, 8, BLOCK), -BIG, jnp.float32)
        highest = lax.fori_loop(0, table_ref[GROUPS + s], step, start)
        m_ref[source_rows(s), :] = highest.reshape(BLOCK, BLOCK)

    m_ref[...] = jnp.broadcast_to(jnp.max(m_ref[...], axis=1, keepdims=True), m_ref.shape)


def sweep_kernel(table_ref, hh_ref, kc_ref, g_ref, part_ref, terms_ref, top_ref, mass_ref, m_ref, acc_ref):
    extended(hh_ref, terms_ref)
    top_ref[...] = jnp.full(top_ref.shape, -BIG, jnp.float32)
    mass_ref[...] = jnp.zeros(mass_ref.shape, jnp.float32)
    row_maxima(table_ref, terms_ref, g_ref, m_ref)

    @pl.loop(0, NBLK)
    def _(s):
        m = m_ref[source_rows(s), :].reshape(STRIPS, 8, BLOCK)

        def step(q, acc):
            v = [
                jnp.exp2(strips(g_ref, t, s) + terms_ref[t] - m)
                for t in group_targets(table_ref, s, q)
            ]
            return acc + ((v[0] + v[1]) + (v[2] + v[3]))

        start = jnp.zeros((STRIPS, 8, BLOCK), jnp.float32)
        acc = lax.fori_loop(0, table_ref[GROUPS + s], step, start)
        acc_ref[source_rows(s), :] = acc.reshape(BLOCK, BLOCK)

    sums = jnp.broadcast_to(jnp.sum(acc_ref[...], axis=1, keepdims=True), acc_ref.shape)
    acc_ref[...] = kc_ref[...] - LAM * (m_ref[...] + LOG2E * jnp.log(sums))

    @pl.loop(0, NBLK)
    def _(s):
        uu = acc_ref[source_rows(s), :].reshape(STRIPS, 8, BLOCK)

        @pl.loop(0, table_ref[GROUPS + s])
        def _(q):
            ts = group_targets(table_ref, s, q)
            tops = [top_ref[t] for t in ts]
            masses = [mass_ref[t] for t in ts]
            made = []
            for t, top, mass in zip(ts, tops, masses):
                v = strips(g_ref, t, s) + uu
                high = jnp.maximum(top, jnp.max(v, axis=0))
                made.append((high, mass * jnp.exp2(top - high) + jnp.sum(jnp.exp2(v - high), axis=0)))
            for t, (high, mass) in zip(ts, made):
                top_ref[t] = high
                mass_ref[t] = mass

    top = top_ref[:WIN]
    high = jnp.max(top, axis=1, keepdims=True)
    part_ref[0] = high[:, 0, :]
    part_ref[1] = jnp.sum(mass_ref[:WIN] * jnp.exp2(top - high), axis=1)


def weigh(table_ref, hh_ref, g_ref, w_ref, sum_ref, terms_ref, m_ref):
    extended(hh_ref, terms_ref)
    row_maxima(table_ref, terms_ref, g_ref, m_ref)

    @pl.loop(0, NBLK)
    def _(s):
        rows = source_rows(s)
        m = m_ref[rows, :].reshape(STRIPS, 8, BLOCK)
        w_ref[rows, :] = jnp.zeros((BLOCK, (WIN + 1) * BLOCK), jnp.bfloat16)

        def step(q, acc):
            ts = group_targets(table_ref, s, q)
            v = [jnp.exp2(strips(g_ref, t, s) + terms_ref[t] - m) for t in ts]
            for t, e in zip(ts, v):
                lanes = pl.ds(pl.multiple_of(t * BLOCK, BLOCK), BLOCK)
                w_ref[rows, lanes] = e.reshape(BLOCK, BLOCK).astype(jnp.bfloat16)
            return acc + ((v[0] + v[1]) + (v[2] + v[3]))

        start = jnp.zeros((STRIPS, 8, BLOCK), jnp.float32)
        acc = lax.fori_loop(0, table_ref[GROUPS + s], step, start)
        sum_ref[rows, :] = acc.reshape(BLOCK, BLOCK)

    sum_ref[...] = jnp.broadcast_to(jnp.sum(sum_ref[...], axis=1, keepdims=True), sum_ref.shape)


def pulled(w_ref, rows, fate_refs, first):
    total = 0.0
    for region, fate_ref in enumerate(fate_refs, first):
        total += jnp.dot(
            w_ref[rows, region * CELLS : (region + 1) * CELLS],
            fate_ref[...],
            preferred_element_type=jnp.float32,
        )
    return total


def divided(total, sums):
    inverse = 1.0 / sums
    return (total * jnp.concatenate([inverse, inverse], axis=1)).astype(jnp.bfloat16)


def chunks(body):
    @pl.loop(0, 4)
    def _(chunk):
        body(pl.ds(pl.multiple_of(chunk * 256, 256), 256))


def near_kernel(place_ref, source_ref, own_ref, mass_hbm, sib_mass_ref, sib_ref, g_ref, kc_ref, window_ref, mass_ref, sem):
    group = place_ref[1]
    fetched = pltpu.make_async_copy(mass_hbm, mass_ref, sem)
    fetched.start()
    products(source_ref, (own_ref, sib_ref), g_ref, 0)
    target_constants(sib_ref, mass_rows(sib_mass_ref, group, 1), window_ref, 1)
    fetched.wait()
    target_constants(own_ref, mass_rows(mass_ref, group, 1), window_ref, 0)
    source_mass = mass_rows(mass_ref, group, 0)
    for s in range(NBLK):
        x = source_ref[s * BLOCK : (s + 1) * BLOCK, :].astype(jnp.float32)
        norm = jnp.sum(x * x, axis=1, keepdims=True) * SCALE
        mass = jnp.broadcast_to(source_mass(s), (BLOCK, BLOCK)).T
        kc_ref[s * BLOCK : (s + 1) * BLOCK, :] = mass * LOG2E + (LAM - 1.0) * norm


def far_kernel(place_ref, table_ref, source_ref, out_mass_ref, out_ref, near_ref, near_window_ref, g_ref, window_ref):
    del table_ref, near_ref
    window_ref[:, : 2 * NBLK, :] = near_window_ref[...]
    products(source_ref, (out_ref,), g_ref, 2)
    target_constants(out_ref, mass_rows(out_mass_ref, place_ref[1], 1), window_ref, 2)


def other_kernel(behind_ref, source_ref, own_ref, sib_ref, out_ref, g_ref):
    del behind_ref
    products(source_ref, [ref.at[:CELLS] for ref in (own_ref, sib_ref, out_ref)], g_ref, 0)


def weigh_one(coupling, place_ref, mine, others, *outs):
    @pl.when(place_ref[1] == coupling)
    def _():
        weigh(*mine, *outs)

    @pl.when(place_ref[1] != coupling)
    def _():
        weigh(*others, *outs)


def late_kernel(place_ref, table_ref, hh_ref, g_ref, table2_ref, hh2_ref, g2_ref, own_ref, sib_ref, out_ref, late_ref, w_ref, sum_ref, terms_ref, m_ref):
    weigh_one(1, place_ref, (table_ref, hh_ref, g_ref), (table2_ref, hh2_ref, g2_ref), w_ref, sum_ref, terms_ref, m_ref)
    fates = [ref.at[CELLS:] for ref in (own_ref, sib_ref, out_ref)]

    @chunks
    def _(rows):
        late_ref[rows, :] = divided(pulled(w_ref, rows, fates, 0), sum_ref[rows, :])


def early_weights_kernel(place_ref, table_ref, hh_ref, g_ref, table2_ref, hh2_ref, g2_ref, w_ref, sum_ref, terms_ref, m_ref):
    weigh_one(0, place_ref, (table_ref, hh_ref, g_ref), (table2_ref, hh2_ref, g2_ref), w_ref, sum_ref, terms_ref, m_ref)


def early_near_kernel(w_ref, own_ref, sib_ref, total_ref):
    @chunks
    def _(rows):
        total_ref[rows, :] = pulled(w_ref, rows, (own_ref, sib_ref), 0)


def early_kernel(w_ref, sum_ref, total_ref, out_ref, early_ref):
    @chunks
    def _(rows):
        total = total_ref[rows, :] + pulled(w_ref, rows, (out_ref,), 2)
        early_ref[rows, :] = divided(total, sum_ref[rows, :])


G_SHAPE = pltpu.VMEM((WIN, CELLS, BLOCK), jnp.float32)
PART_SHAPE = jax.ShapeDtypeStruct((2, WIN, BLOCK), jnp.float32)
W_SHAPE = jax.ShapeDtypeStruct((CELLS, (WIN + 1) * BLOCK), jnp.bfloat16)
COLUMN_SHAPE = jax.ShapeDtypeStruct((CELLS, BLOCK), jnp.float32)
FATE_SHAPE = jax.ShapeDtypeStruct((CELLS, EMB), jnp.bfloat16)
TOTAL_SHAPE = jax.ShapeDtypeStruct((CELLS, EMB), jnp.float32)
TERMS = pltpu.VMEM((WIN + 1, 8, BLOCK), jnp.float32)
COLUMN = pltpu.VMEM(COLUMN_SHAPE.shape, COLUMN_SHAPE.dtype)
SWEEP_SCRATCH = [TERMS] * 3 + [COLUMN] * 2
HOLD = [pltpu.VMEM(W_SHAPE.shape, W_SHAPE.dtype), COLUMN]


WINDOW_SHAPE = jax.ShapeDtypeStruct((2, WIN, BLOCK), jnp.float32)
NEAR_SHAPE = jax.ShapeDtypeStruct((2, 2 * NBLK, BLOCK), jnp.float32)


def build_table(place, behind, slots):
    specs = [SMEM, ANY] + [SMEM] * len(slots)
    return call(table_kernel, jax.ShapeDtypeStruct((TABLE,), jnp.int32), SMEM, specs)(place, behind, *slots)


def near_products(*args):
    specs = [SMEM, VMEM, VMEM, ANY, VMEM, VMEM]
    scratch = [pltpu.VMEM((3, CELLS), jnp.float32), pltpu.SemaphoreType.DMA]
    return call(near_kernel, (G_SHAPE, COLUMN_SHAPE, NEAR_SHAPE), (VMEM,) * 3, specs, scratch)(*args)


def far_products(*args):
    return call(far_kernel, (G_SHAPE, WINDOW_SHAPE), (VMEM,) * 2, [SMEM, SMEM] + [VMEM] * 5, aliases={5: 0})(*args)


def sweep(*args):
    return call(sweep_kernel, PART_SHAPE, VMEM, [SMEM] + [VMEM] * 3, SWEEP_SCRATCH)(*args)


def other_products(*args):
    return call(other_kernel, G_SHAPE, VMEM, [ANY] + [VMEM] * 4)(*args)


COUPLINGS = [SMEM, SMEM, VMEM, VMEM, SMEM, VMEM, VMEM]


def late_fates(*args):
    return call(late_kernel, FATE_SHAPE, VMEM, COUPLINGS + [VMEM] * 3, HOLD + [TERMS, COLUMN], mib=9)(*args)


def early_weights(*args):
    return call(early_weights_kernel, (W_SHAPE, COLUMN_SHAPE), (VMEM, VMEM), COUPLINGS, [TERMS, COLUMN])(*args)


def early_near(*args):
    return call(early_near_kernel, TOTAL_SHAPE, VMEM, [VMEM] * 3)(*args)


def early_fates(*args):
    return call(early_kernel, FATE_SHAPE, VMEM, [VMEM] * 4)(*args)


def merged(first, second):
    highest = jnp.maximum(first[0], second[0])
    return jnp.stack(
        [
            highest,
            first[1] * jnp.exp2(first[0] - highest) + second[1] * jnp.exp2(second[0] - highest),
        ]
    )


def folded(part, beside):
    own = merged(part[:, :NBLK], sibling(part[:, NBLK : 2 * NBLK]))
    beyond = part[:, 2 * NBLK :]
    message = jnp.concatenate([own, beyond], axis=1)
    arrived, made = lax.optimization_barrier((outward(message), beside(message)))
    own = merged(own, arrived[:, NBLK:])
    out = merged(arrived[:, :NBLK], beyond)
    own_total = own[0] + jnp.log2(own[1])
    out_total = out[0] + jnp.log2(out[1])
    return jnp.concatenate([own_total, sibling(own_total), out_total], axis=0), made


def shifted(value, steps):
    count = lax.axis_size("tiles")
    return lax.ppermute(value, "tiles", [(t, (t + steps) % count) for t in range(count)])


def on_device(embeddings, log_mass, signatures, tile_list):
    owner = lax.axis_index("cells").astype(jnp.int32)
    group = (lax.axis_index("tiles") >= 2).astype(jnp.int32)
    place, place_other = jnp.stack([owner, group]), jnp.stack([owner, 1 - group])

    def moment(array, index):
        return lax.dynamic_index_in_dim(array, index, 0, keepdims=False)

    target = moment(embeddings, group + 1)
    target_out, target_sib = outward(target), sibling(target)
    cells, masses, slots, target_sib = lax.optimization_barrier(
        (embeddings, log_mass, tile_list, target_sib)
    )
    gathered = [slots] + [shifted(slots, k) for k in range(1, lax.axis_size("tiles"))]
    masses_out, masses_sib = outward(masses), sibling(masses)
    source, other_source = moment(cells, group), moment(cells, 1 - group)
    rest = jnp.concatenate([moment(cells, 2 - group), signatures])
    g, kc, near = near_products(place, source, target, log_mass, masses_sib, target_sib)
    table = build_table(place, near, gathered)
    g, window = far_products(place, table, source, masses_out, target_out, g, near)
    part = sweep(table, window[0], kc, g)
    rest_out, rest_sib = outward(rest), sibling(rest)

    totals, g_other = folded(
        part, lambda message: other_products(message, other_source, rest, rest_sib, rest_out)
    )
    hh = window[1] - LAM * totals
    part = sweep(table, hh, kc, g)
    totals, table_other = folded(part, lambda message: build_table(place_other, message, gathered))
    hh = window[1] - LAM * totals
    couplings = (place, table, hh, g, table_other, mirrored(hh), g_other)
    late = late_fates(*couplings, rest, rest_sib, rest_out)
    late_out, late_sib = outward(late), sibling(late)
    weights, sums = early_weights(*couplings)
    total = early_near(weights, late, late_sib)
    early = early_fates(weights, sums, total, late_out)
    return early, late


def solution(mesh):
    in_specs = (
        P(None, "cells", None),
        P(None, "cells"),
        P("cells", None),
        P(None, None, ("cells", "tiles")),
    )
    out_specs = (P("cells", None), P("cells", None))
    return jax.shard_map(
        on_device, mesh=mesh, in_specs=in_specs, out_specs=out_specs, check_vma=False
    )
```

time: 91.1 us -> 83.5 us (0.917); the launches traced: 92.1 us -> 82.7 us
  starting transfers between devices: 30.4 us -> 24.1 us
  Pallas kernels: 39.7 us -> 38 us
    ppermute x9 -> x8, starting transfers between devices: 4.85 us -> 1.38 us  [sibling(): lax.ppermute(value, 'cells', [(c, c ^ 1) for c in range(lax.axis_size('ce...]
    ppermute x7 -> x6, starting transfers between devices: 18.8 us -> 16.2 us  [outward(): return lax.ppermute(value, 'cells', pairs)]
    ppermute x7 -> x6, waiting for transfers between devices: 12.1 us -> 9.74 us  [outward(): return lax.ppermute(value, 'cells', pairs)]
    unnamed x12 -> x8, local copies, waits for them, and re-layouts: 2.14 us -> 0.02 us
    pallas_call x1, Pallas kernels: 7.68 us -> 5.65 us  [late_fates(): call(late_kernel, FATE_SHAPE, VMEM, COUPLINGS + [VMEM] * 3, HOLD + [TERMS...]
    ppermute x9 -> x8, waiting for transfers between devices: 2.75 us -> 4.07 us  [sibling(): lax.ppermute(value, 'cells', [(c, c ^ 1) for c in range(lax.axis_size('ce...]
    squeeze x1 -> x2, local copies, waits for them, and re-layouts: 1.27 us -> 2.6 us  [moment(): return lax.dynamic_index_in_dim(array, index, 0, keepdims=False)]
  transfers between devices with their start and end apart: 20 -> 18, of which waited for: 6 -> 8; matrix products, arithmetic and copies ran while one was open for 0% -> 2% of each run, Pallas kernels for 28% -> 31%
where the time goes in v2:
time: 83.5 us; the launch traced here: 82.7 us
  Pallas kernels  38 us (46%)
  starting transfers between devices  24.1 us (29%)
  waiting for transfers between devices  16.7 us (20%)
  local copies, waits for them, and re-layouts  2.63 us (3%)
  between operations  0.88 us (1%)
    ppermute x6, starting transfers between devices, outward(): return lax.ppermute(value, 'cells', pairs)  16.2 us
    ppermute x6, waiting for transfers between devices, outward(): return lax.ppermute(value, 'cells', pairs)  9.74 us
    pallas_call x2, Pallas kernels, sweep(): call(sweep_kernel, PART_SHAPE, VMEM, [SMEM] + [VMEM] * 3, SWEEP_SCRATCH)  9.66 us
    pallas_call x1, Pallas kernels, late_fates(): call(late_kernel, FATE_SHAPE, VMEM, COUPLINGS + [VMEM] * 3, HOLD + [TERMS...  5.65 us
    pallas_call x2, Pallas kernels, build_table(): call(table_kernel, jax.ShapeDtypeStruct((TABLE,), jnp.int32), SMEM, specs)  4.55 us
    ppermute x3, starting transfers between devices, shifted(): lax.ppermute(value, 'tiles', [(t, (t + steps) % count) for t in range(cou...  4.46 us
    pallas_call x1, Pallas kernels, near_products(): call(near_kernel, (G_SHAPE, COLUMN_SHAPE, NEAR_SHAPE), (VMEM,) * 3, specs...  4.13 us
    ppermute x8, waiting for transfers between devices, sibling(): lax.ppermute(value, 'cells', [(c, c ^ 1) for c in range(lax.axis_size('ce...  4.07 us
  transfers between devices with their start and end apart: 18, of which 8 were waited for; matrix products, arithmetic and copies ran while one was open for 2% of the time, Pallas kernels for 31%

profile of v2, /device:TPU:0, one launch (start us, length us, event | category | flops | bytes accessed | tf_op | source)
XLA Modules:
  0.0 82.7 jit_solution(14710565158940622043)
XLA Ops:
  0.6 1.1 %dynamic-slice_bitcast_fusion.3.own_ref = bf16[1024,256]{1,0:T(8,128)(2,1)S(1)} fusion(bf16[3,1024,256]{2,1,0:T(8,128)(2,1)} %param.4, s32[]{:T(128)S(6)} %select_n.13), kind=kLoop, calls=%fused_computation.4 | loop fusion | bytes 1048580 | tf_op jit(solution)/shard_map/jit(dynamic_index_in_dim)/squeeze | solution.py:414
  1.9 6.7 %collective-permute-start.6 = (bf16[1024,256]{1,0:T(8,128)(2,1)S(1)}, bf16[1024,256]{1,0:T(8,128)(2,1)S(1)}, u32[]{:S(2)}, u32[]{:S(2)}) collective-permute-start(bf16[1024,256]{1,0:T(8,128)(2,1)S(1)} %dynamic-slice_bitcast_fusion.3.own_ref), channel_id=1, source_target_pairs={{0,124},{4,8},{8,4},{12,16},{16,12},{20,24},{24,20},{28,32},{32,28... | collective-permute-start | bytes 1572872 | tf_op jit(solution)/shard_map/ppermute | solution.py:39
  8.6 2.8 %collective-permute-start.4 = (s32[2,2,32]{2,1,0:T(2,128)}, s32[2,2,32]{2,1,0:T(2,128)S(1)}, u32[]{:S(2)}, u32[]{:S(2)}) collective-permute-start(s32[2,2,32]{2,1,0:T(2,128)} %refs_0_.1), channel_id=1, source_target_pairs={{0,3},{1,0},{2,1},{3,2},{4,7},{5,4},{6,5},{7,6},{8,11},{9,8},{10,9... | collective-permute-start | bytes 1544 | tf_op jit(solution)/shard_map/ppermute | solution.py:405
  11.4 0.8 collective-permute-start.3
  12.2 0.9 %collective-permute-start.2 = (s32[2,2,32]{2,1,0:T(2,128)}, s32[2,2,32]{2,1,0:T(2,128)S(1)}, u32[]{:S(2)}, u32[]{:S(2)}) collective-permute-start(s32[2,2,32]{2,1,0:T(2,128)} %refs_0_.1), channel_id=1, source_target_pairs={{0,1},{1,2},{2,3},{3,0},{4,5},{5,6},{6,7},{7,4},{8,9},{9,10},{10,1... | collective-permute-start | bytes 1544 | tf_op jit(solution)/shard_map/ppermute | solution.py:405
  13.1 1.5 %dynamic-slice_bitcast_fusion = (bf16[1024,256]{1,0:T(8,128)(2,1)S(1)}, bf16[1024,256]{1,0:T(8,128)(2,1)S(1)}, bf16[1024,256]{1,0:T(8,128)(2,1)S(1)}) fusion(bf16[3,1024,256]{2,1,0:T(8,128)(2,1)} %param.4, s32[]{:T(128)S(6)} %select_n.16, s32[]{:T(128)S(6)} %select_n.15, s32[]{:T(128)S(6)} %select_n.14), kind=kLoop, calls=%fused_computation.1 | loop fusion | bytes 3145740 | tf_op jit(solution)/shard_map/jit(dynamic_index_in_dim)/squeeze | solution.py:414
  14.7 1.9 %collective-permute-start.5 = (f32[3,1024]{1,0:T(4,128)S(1)}, f32[3,1024]{1,0:T(4,128)S(1)}, u32[]{:S(2)}, u32[]{:S(2)}) collective-permute-start(f32[3,1024]{1,0:T(4,128)S(1)} %copy-done.1), channel_id=1, source_target_pairs={{0,124},{4,8},{8,4},{12,16},{16,12},{20,24},{24,20},{28,32},{32,28... | collective-permute-start | bytes 36872 | tf_op jit(solution)/shard_map/ppermute | solution.py:39
  16.6 4.1 %shard_map.59 = (f32[24,1024,128]{2,1,0:T(8,128)S(1)}, f32[1024,128]{1,0:T(8,128)S(1)}, f32[2,16,128]{2,1,0:T(8,128)S(1)}) custom-call(s32[2]{0:T(128)S(1)} %pad_add_fusion.place_ref, bf16[1024,256]{1,0:T(8,128)(2,1)S(1)} %get-tuple-element.38.source_ref, bf16[1024,256]{1,0:T(8,128)(2,1)S(1)} %dynamic-slice_bitcast_fusion.3.own_ref, ...), custom_call_target="tpu_custom_call" | custom-call | flops 3000000000 | bytes 10000 | tf_op jit(solution)/shard_map/pallas_call | solution.py:347
  20.7 3.3 %collective-permute-start.10 = (bf16[2048,256]{1,0:T(8,128)(2,1)S(1)}, bf16[2048,256]{1,0:T(8,128)(2,1)S(1)}, u32[]{:S(2)}, u32[]{:S(2)}) collective-permute-start(bf16[2048,256]{1,0:T(8,128)(2,1)S(1)} %pad_maximum_fusion.own_ref), channel_id=1, source_target_pairs={{0,124},{4,8},{8,4},{12,16},{16,12},{20,24},{24,20},{28,32},{32,28... | collective-permute-start | bytes 3145736 | tf_op jit(solution)/shard_map/ppermute | solution.py:39
  24.1 2.3 %shard_map.60.table_ref = s32[512]{0:T(512)S(1)} custom-call(s32[2]{0:T(128)S(1)} %pad_add_fusion.place_ref, f32[2,16,128]{2,1,0:T(8,128)S(1)} %get-tuple-element.20.behind_ref.near_window_ref, s32[2,2,32]{2,1,0:T(2,128)S(1)} %copy-done.2, s32[2,2,32]{2,1,0:T(2,128)S(1)} %collective-permute-done.2.refs_1_, s32[2,2,32]{2,1,0:T(2,128)S(1)} %collective-permute-done.3.refs_2_, ...), custom_call_target="tpu_custom_call" | custom-call | flops 3000000000 | bytes 10000 | tf_op jit(solution)/shard_map/pallas_call | solution.py:341
  26.4 2.3 %shard_map.61 = (f32[24,1024,128]{2,1,0:T(8,128)S(1)}, f32[2,24,128]{2,1,0:T(8,128)S(1)}) custom-call(s32[2]{0:T(128)S(1)} %pad_add_fusion.place_ref, s32[512]{0:T(512)S(1)} %shard_map.60.table_ref, bf16[1024,256]{1,0:T(8,128)(2,1)S(1)} %get-tuple-element.38.source_ref, ...), custom_call_target="tpu_custom_call", output_to_operand_aliasing={{0}: (5, {})} | custom-call | flops 3000000000 | bytes 10000 | tf_op jit(solution)/shard_map/pallas_call | solution.py:351
  28.7 4.8 %shard_map.62 = f32[2,24,128]{2,1,0:T(8,128)S(1)} custom-call(s32[512]{0:T(512)S(1)} %shard_map.60.table_ref, f32[24,128]{1,0:T(8,128)S(1)} %slice_bitcast_fusion.hh_ref, f32[1024,128]{1,0:T(8,128)S(1)} %get-tuple-element.24.kc_ref, f32[24,1024,128]{2,1,0:T(8,128)S(1)} %get-tuple-element.25.g_ref), custom_call_target="tpu_custom_call" | custom-call | flops 3000000000 | bytes 10000 | tf_op jit(solution)/shard_map/pallas_call | solution.py:355
  33.6 0.6 collective-permute-start.7
  34.1 0.8 %collective-permute-done.7 = f32[2,8,128]{2,1,0:T(8,128)S(1)} collective-permute-done((f32[2,8,128]{2,1,0:T(8,128)S(1)}, f32[2,8,128]{2,1,0:T(8,128)S(1)}, u32[]{:S(2)}, u32[]{:S(2)}) %collective-permute-start.7) | collective-permute-done | bytes 8224 | tf_op jit(solution)/shard_map/ppermute | solution.py:33
  35.2 3.2 %collective-permute-done.10.out_ref = bf16[2048,256]{1,0:T(8,128)(2,1)S(1)} collective-permute-done((bf16[2048,256]{1,0:T(8,128)(2,1)S(1)}, bf16[2048,256]{1,0:T(8,128)(2,1)S(1)}, u32[]{:S(2)}, u32[]{:S(2)}) %collective-permute-start.10) | collective-permute-done | bytes 1048608 | tf_op jit(solution)/shard_map/ppermute | solution.py:39
  38.3 4.0 %shard_map.63.g2_ref = f32[24,1024,128]{2,1,0:T(8,128)S(1)} custom-call(f32[2,16,128]{2,1,0:T(8,128)S(1)} %pad_maximum_fusion.1.behind_ref, bf16[1024,256]{1,0:T(8,128)(2,1)S(1)} %get-tuple-element.37.source_ref, bf16[2048,256]{1,0:T(8,128)(2,1)S(1)} %pad_maximum_fusion.own_ref, bf16[2048,256]{1,0:T(8,128)(2,1)S(1)} %collective-permute-done.9.sib_ref, ...), custom_call_target="tpu_custom_call" | custom-call | flops 3000000000 | bytes 10000 | tf_op jit(solution)/shard_map/pallas_call | solution.py:359
  42.5 1.2 %collective-permute-done.11 = f32[8,128]{1,0:T(8,128)S(1)} collective-permute-done((f32[8,128]{1,0:T(8,128)S(1)}, f32[8,128]{1,0:T(8,128)S(1)}, u32[]{:S(2)}, u32[]{:S(2)}) %collective-permute-start.11) | collective-permute-done | bytes 4128 | tf_op jit(solution)/shard_map/ppermute | solution.py:33
  43.7 4.8 %shard_map.64 = f32[2,24,128]{2,1,0:T(8,128)S(1)} custom-call(s32[512]{0:T(512)S(1)} %shard_map.60.table_ref, f32[24,128]{1,0:T(8,128)S(1)} %fusion.hh_ref, f32[1024,128]{1,0:T(8,128)S(1)} %get-tuple-element.24.kc_ref, f32[24,1024,128]{2,1,0:T(8,128)S(1)} %get-tuple-element.25.g_ref), custom_call_target="tpu_custom_call" | custom-call | flops 3000000000 | bytes 10000 | tf_op jit(solution)/shard_map/pallas_call | solution.py:355
  48.8 0.9 %collective-permute-done.12 = f32[2,8,128]{2,1,0:T(8,128)S(1)} collective-permute-done((f32[2,8,128]{2,1,0:T(8,128)S(1)}, f32[2,8,128]{2,1,0:T(8,128)S(1)}, u32[]{:S(2)}, u32[]{:S(2)}) %collective-permute-start.12) | collective-permute-done | bytes 8224 | tf_op jit(solution)/shard_map/ppermute | solution.py:33
  49.8 1.8 %collective-permute-start.13 = (f32[2,16,128]{2,1,0:T(8,128)S(1)}, f32[2,16,128]{2,1,0:T(8,128)S(1)}, u32[]{:S(2)}, u32[]{:S(2)}) collective-permute-start(f32[2,16,128]{2,1,0:T(8,128)S(1)} %pad_maximum_fusion.2.behind_ref), channel_id=1, source_target_pairs={{0,124},{4,8},{8,4},{12,16},{16,12},{20,24},{24,20},{28,32},{32,28... | collective-permute-start | bytes 49160 | tf_op jit(solution)/shard_map/ppermute | solution.py:39
  51.6 2.3 %shard_map.65.table2_ref = s32[512]{0:T(512)S(1)} custom-call(s32[2]{0:T(128)S(1)} %pad_add_fusion.1.place_ref, f32[2,16,128]{2,1,0:T(8,128)S(1)} %pad_maximum_fusion.2.behind_ref, s32[2,2,32]{2,1,0:T(2,128)S(1)} %copy-done.2, s32[2,2,32]{2,1,0:T(2,128)S(1)} %collective-permute-done.2.refs_1_, s32[2,2,32]{2,1,0:T(2,128)S(1)} %collective-permute-done.3.refs_2_, ...), custom_call_target="tpu_custom_call" | custom-call | flops 3000000000 | bytes 10000 | tf_op jit(solution)/shard_map/pallas_call | solution.py:341
  53.9 2.5 %collective-permute-done.13 = f32[2,16,128]{2,1,0:T(8,128)S(1)} collective-permute-done((f32[2,16,128]{2,1,0:T(8,128)S(1)}, f32[2,16,128]{2,1,0:T(8,128)S(1)}, u32[]{:S(2)}, u32[]{:S(2)}) %collective-permute-start.13) | collective-permute-done | bytes 16416 | tf_op jit(solution)/shard_map/ppermute | solution.py:39
  56.5 1.2 %collective-permute-done.14 = f32[8,128]{1,0:T(8,128)S(1)} collective-permute-done((f32[8,128]{1,0:T(8,128)S(1)}, f32[8,128]{1,0:T(8,128)S(1)}, u32[]{:S(2)}, u32[]{:S(2)}) %collective-permute-start.14) | collective-permute-done | bytes 4128 | tf_op jit(solution)/shard_map/ppermute | solution.py:33
  57.6 2.0 %collective-permute-start.15 = (f32[24,128]{1,0:T(8,128)S(1)}, f32[24,128]{1,0:T(8,128)S(1)}, u32[]{:S(2)}, u32[]{:S(2)}) collective-permute-start(f32[24,128]{1,0:T(8,128)S(1)} %fusion.1.hh_ref), channel_id=1, source_target_pairs={{0,3},{1,2},{2,1},{3,0},{4,7},{5,6},{6,5},{7,4},{8,11},{9,10},{10,... | collective-permute-start | bytes 36872 | tf_op jit(solution)/shard_map/ppermute | solution.py:44
  59.7 2.9 %collective-permute-done.15.hh2_ref = f32[24,128]{1,0:T(8,128)S(1)} collective-permute-done((f32[24,128]{1,0:T(8,128)S(1)}, f32[24,128]{1,0:T(8,128)S(1)}, u32[]{:S(2)}, u32[]{:S(2)}) %collective-permute-start.15) | collective-permute-done | bytes 12320 | tf_op jit(solution)/shard_map/ppermute | solution.py:44
  62.5 5.7 %shard_map.67.own_ref = bf16[1024,256]{1,0:T(8,128)(2,1)} custom-call(s32[2]{0:T(128)S(1)} %pad_add_fusion.place_ref, s32[512]{0:T(512)S(1)} %shard_map.60.table_ref, f32[24,128]{1,0:T(8,128)S(1)} %fusion.1.hh_ref, f32[24,1024,128]{2,1,0:T(8,128)S(1)} %get-tuple-element.25.g_ref, s32[512]{0:T(512)S(1)} %shard_map.65.table2_ref, ...), custom_call_target="tpu_custom_call" | custom-call | flops 3000000000 | bytes 10000 | tf_op jit(solution)/shard_map/pallas_call | solution.py:366
  68.2 0.3 collective-permute-start.16
  68.5 2.3 %collective-permute-start.17 = (bf16[1024,256]{1,0:T(8,128)(2,1)}, bf16[1024,256]{1,0:T(8,128)(2,1)S(1)}, u32[]{:S(2)}, u32[]{:S(2)}) collective-permute-start(bf16[1024,256]{1,0:T(8,128)(2,1)} %shard_map.67.own_ref), channel_id=1, source_target_pairs={{0,124},{4,8},{8,4},{12,16},{16,12},{20,24},{24,20},{28,32},{32,28... | collective-permute-start | bytes 1572872 | tf_op jit(solution)/shard_map/ppermute | solution.py:39
  70.8 3.9 %shard_map.66 = (bf16[1024,3200]{1,0:T(8,128)(2,1)S(1)}, f32[1024,128]{1,0:T(8,128)S(1)}) custom-call(s32[2]{0:T(128)S(1)} %pad_add_fusion.place_ref, s32[512]{0:T(512)S(1)} %shard_map.60.table_ref, f32[24,128]{1,0:T(8,128)S(1)} %fusion.1.hh_ref, f32[24,1024,128]{2,1,0:T(8,128)S(1)} %get-tuple-element.25.g_ref, s32[512]{0:T(512)S(1)} %shard_map.65.table2_ref, ...), custom_call_target="tpu_custom_call" | custom-call | flops 3000000000 | bytes 10000 | tf_op jit(solution)/shard_map/pallas_call | solution.py:370
  74.7 1.8 %shard_map.68.total_ref = f32[1024,256]{1,0:T(8,128)S(1)} custom-call(bf16[1024,3200]{1,0:T(8,128)(2,1)S(1)} %get-tuple-element.30.w_ref, bf16[1024,256]{1,0:T(8,128)(2,1)S(1)} %copy-done, bf16[1024,256]{1,0:T(8,128)(2,1)S(1)} %collective-permute-done.16.sib_ref), custom_call_target="tpu_custom_call" | custom-call | flops 3000000000 | bytes 10000 | tf_op jit(solution)/shard_map/pallas_call | solution.py:374
  76.5 4.1 %collective-permute-done.17.out_ref = bf16[1024,256]{1,0:T(8,128)(2,1)S(1)} collective-permute-done((bf16[1024,256]{1,0:T(8,128)(2,1)}, bf16[1024,256]{1,0:T(8,128)(2,1)S(1)}, u32[]{:S(2)}, u32[]{:S(2)}) %collective-permute-start.17) | collective-permute-done | bytes 524320 | tf_op jit(solution)/shard_map/ppermute | solution.py:39
  80.6 2.0 %shard_map.69 = bf16[1024,256]{1,0:T(8,128)(2,1)} custom-call(bf16[1024,3200]{1,0:T(8,128)(2,1)S(1)} %get-tuple-element.30.w_ref, f32[1024,128]{1,0:T(8,128)S(1)} %get-tuple-element.31.sum_ref, f32[1024,256]{1,0:T(8,128)S(1)} %shard_map.68.total_ref, bf16[1024,256]{1,0:T(8,128)(2,1)S(1)} %collective-permute-done.17.out_ref), custom_call_target="tpu_custom_call" | custom-call | flops 3000000000 | bytes 10000 | tf_op jit(solution)/shard_map/pallas_call | solution.py:378
  (39 shorter events, 1.1 us)
Async XLA Ops:
  0.6 13.9 %copy-start.3 = (bf16[1024,256]{1,0:T(8,128)(2,1)S(1)}, bf16[1024,256]{1,0:T(8,128)(2,1)}, u32[]{:S(2)}) copy-start(bf16[1024,256]{1,0:T(8,128)(2,1)} %param.6) | copy-start | bytes 1572868
  1.8 6.8 %collective-permute-start = (bf16[1024,256]{1,0:T(8,128)(2,1)S(1)}, bf16[1024,256]{1,0:T(8,128)(2,1)S(1)}, u32[]{:S(2)}, u32[]{:S(2)}) collective-permute-start(bf16[1024,256]{1,0:T(8,128)(2,1)S(1)} %dynamic-slice_bitcast_fusion.3.own_ref), channel_id=1, source_target_pairs={{0,4},{4,0},{8,12},{12,8},{16,20},{20,16},{24,28},{28,24},{32,36},... | collective-permute-start | bytes 1572872 | tf_op jit(solution)/shard_map/ppermute | solution.py:33
  1.9 24.5 %collective-permute-start.6 = (bf16[1024,256]{1,0:T(8,128)(2,1)S(1)}, bf16[1024,256]{1,0:T(8,128)(2,1)S(1)}, u32[]{:S(2)}, u32[]{:S(2)}) collective-permute-start(bf16[1024,256]{1,0:T(8,128)(2,1)S(1)} %dynamic-slice_bitcast_fusion.3.own_ref), channel_id=1, source_target_pairs={{0,124},{4,8},{8,4},{12,16},{16,12},{20,24},{24,20},{28,32},{32,28... | collective-permute-start | bytes 1572872 | tf_op jit(solution)/shard_map/ppermute | solution.py:39
  8.6 6.0 %copy-start.1 = (f32[3,1024]{1,0:T(4,128)S(1)}, f32[3,1024]{1,0:T(4,128)}, u32[]{:S(2)}) copy-start(f32[3,1024]{1,0:T(4,128)} %mass_hbm.1) | copy-start | bytes 36868
  8.6 12.1 %collective-permute-start.4 = (s32[2,2,32]{2,1,0:T(2,128)}, s32[2,2,32]{2,1,0:T(2,128)S(1)}, u32[]{:S(2)}, u32[]{:S(2)}) collective-permute-start(s32[2,2,32]{2,1,0:T(2,128)} %refs_0_.1), channel_id=1, source_target_pairs={{0,3},{1,0},{2,1},{3,2},{4,7},{5,4},{6,5},{7,6},{8,11},{9,8},{10,9... | collective-permute-start | bytes 1544 | tf_op jit(solution)/shard_map/ppermute | solution.py:405
  11.4 12.7 %collective-permute-start.3 = (s32[2,2,32]{2,1,0:T(2,128)}, s32[2,2,32]{2,1,0:T(2,128)S(1)}, u32[]{:S(2)}, u32[]{:S(2)}) collective-permute-start(s32[2,2,32]{2,1,0:T(2,128)} %refs_0_.1), channel_id=1, source_target_pairs={{0,2},{1,3},{2,0},{3,1},{4,6},{5,7},{6,4},{7,5},{8,10},{9,11},{10,... | collective-permute-start | bytes 1544 | tf_op jit(solution)/shard_map/ppermute | solution.py:405
  12.2 11.9 %collective-permute-start.2 = (s32[2,2,32]{2,1,0:T(2,128)}, s32[2,2,32]{2,1,0:T(2,128)S(1)}, u32[]{:S(2)}, u32[]{:S(2)}) collective-permute-start(s32[2,2,32]{2,1,0:T(2,128)} %refs_0_.1), channel_id=1, source_target_pairs={{0,1},{1,2},{2,3},{3,0},{4,5},{5,6},{6,7},{7,4},{8,9},{9,10},{10,1... | collective-permute-start | bytes 1544 | tf_op jit(solution)/shard_map/ppermute | solution.py:405
  13.1 1.6 %collective-permute-start.1 = (f32[3,1024]{1,0:T(4,128)}, f32[3,1024]{1,0:T(4,128)S(1)}, u32[]{:S(2)}, u32[]{:S(2)}) collective-permute-start(f32[3,1024]{1,0:T(4,128)} %mass_hbm.1), channel_id=1, source_target_pairs={{0,4},{4,0},{8,12},{12,8},{16,20},{20,16},{24,28},{28,24},{32,36},... | collective-permute-start | bytes 36872 | tf_op jit(solution)/shard_map/ppermute | solution.py:33
  14.7 11.7 %collective-permute-start.5 = (f32[3,1024]{1,0:T(4,128)S(1)}, f32[3,1024]{1,0:T(4,128)S(1)}, u32[]{:S(2)}, u32[]{:S(2)}) collective-permute-start(f32[3,1024]{1,0:T(4,128)S(1)} %copy-done.1), channel_id=1, source_target_pairs={{0,124},{4,8},{8,4},{12,16},{16,12},{20,24},{24,20},{28,32},{32,28... | collective-permute-start | bytes 36872 | tf_op jit(solution)/shard_map/ppermute | solution.py:39
  16.6 7.5 %copy-start.2 = (s32[2,2,32]{2,1,0:T(2,128)S(1)}, s32[2,2,32]{2,1,0:T(2,128)}, u32[]{:S(2)}) copy-start(s32[2,2,32]{2,1,0:T(2,128)} %refs_0_.1) | copy-start | bytes 1540
  20.7 17.6 %collective-permute-start.10 = (bf16[2048,256]{1,0:T(8,128)(2,1)S(1)}, bf16[2048,256]{1,0:T(8,128)(2,1)S(1)}, u32[]{:S(2)}, u32[]{:S(2)}) collective-permute-start(bf16[2048,256]{1,0:T(8,128)(2,1)S(1)} %pad_maximum_fusion.own_ref), channel_id=1, source_target_pairs={{0,124},{4,8},{8,4},{12,16},{16,12},{20,24},{24,20},{28,32},{32,28... | collective-permute-start | bytes 3145736 | tf_op jit(solution)/shard_map/ppermute | solution.py:39
  24.1 14.3 %collective-permute-start.9 = (bf16[2048,256]{1,0:T(8,128)(2,1)S(1)}, bf16[2048,256]{1,0:T(8,128)(2,1)S(1)}, u32[]{:S(2)}, u32[]{:S(2)}) collective-permute-start(bf16[2048,256]{1,0:T(8,128)(2,1)S(1)} %pad_maximum_fusion.own_ref), channel_id=1, source_target_pairs={{0,4},{4,0},{8,12},{12,8},{16,20},{20,16},{24,28},{28,24},{32,36},... | collective-permute-start | bytes 3145736 | tf_op jit(solution)/shard_map/ppermute | solution.py:33
  33.6 1.4 %collective-permute-start.7 = (f32[2,8,128]{2,1,0:T(8,128)S(1)}, f32[2,8,128]{2,1,0:T(8,128)S(1)}, u32[]{:S(2)}, u32[]{:S(2)}) collective-permute-start(f32[2,8,128]{2,1,0:T(8,128)S(1)} %get-tuple-element.45), channel_id=1, source_target_pairs={{0,4},{4,0},{8,12},{12,8},{16,20},{20,16},{24,28},{28,24},{32,36},... | collective-permute-start | bytes 24584 | tf_op jit(solution)/shard_map/ppermute | solution.py:33
  35.0 7.4 %collective-permute-start.8 = (f32[2,16,128]{2,1,0:T(8,128)S(1)}, f32[2,16,128]{2,1,0:T(8,128)S(1)}, u32[]{:S(2)}, u32[]{:S(2)}) collective-permute-start(f32[2,16,128]{2,1,0:T(8,128)S(1)} %pad_maximum_fusion.1.behind_ref), channel_id=1, source_target_pairs={{0,124},{4,8},{8,4},{12,16},{16,12},{20,24},{24,20},{28,32},{32,28... | collective-permute-start | bytes 49160 | tf_op jit(solution)/shard_map/ppermute | solution.py:39
  42.4 1.2 %collective-permute-start.11 = (f32[8,128]{1,0:T(8,128)S(1)}, f32[8,128]{1,0:T(8,128)S(1)}, u32[]{:S(2)}, u32[]{:S(2)}) collective-permute-start(f32[8,128]{1,0:T(8,128)S(1)} %get-tuple-element.41), channel_id=1, source_target_pairs={{0,4},{4,0},{8,12},{12,8},{16,20},{20,16},{24,28},{28,24},{32,36},... | collective-permute-start | bytes 12296 | tf_op jit(solution)/shard_map/ppermute | solution.py:33
  48.5 1.3 %collective-permute-start.12 = (f32[2,8,128]{2,1,0:T(8,128)S(1)}, f32[2,8,128]{2,1,0:T(8,128)S(1)}, u32[]{:S(2)}, u32[]{:S(2)}) collective-permute-start(f32[2,8,128]{2,1,0:T(8,128)S(1)} %get-tuple-element.43), channel_id=1, source_target_pairs={{0,4},{4,0},{8,12},{12,8},{16,20},{20,16},{24,28},{28,24},{32,36},... | collective-permute-start | bytes 24584 | tf_op jit(solution)/shard_map/ppermute | solution.py:33
  49.8 6.6 %collective-permute-start.13 = (f32[2,16,128]{2,1,0:T(8,128)S(1)}, f32[2,16,128]{2,1,0:T(8,128)S(1)}, u32[]{:S(2)}, u32[]{:S(2)}) collective-permute-start(f32[2,16,128]{2,1,0:T(8,128)S(1)} %pad_maximum_fusion.2.behind_ref), channel_id=1, source_target_pairs={{0,124},{4,8},{8,4},{12,16},{16,12},{20,24},{24,20},{28,32},{32,28... | collective-permute-start | bytes 49160 | tf_op jit(solution)/shard_map/ppermute | solution.py:39
  56.4 1.2 %collective-permute-start.14 = (f32[8,128]{1,0:T(8,128)S(1)}, f32[8,128]{1,0:T(8,128)S(1)}, u32[]{:S(2)}, u32[]{:S(2)}) collective-permute-start(f32[8,128]{1,0:T(8,128)S(1)} %get-tuple-element.39), channel_id=1, source_target_pairs={{0,4},{4,0},{8,12},{12,8},{16,20},{20,16},{24,28},{28,24},{32,36},... | collective-permute-start | bytes 12296 | tf_op jit(solution)/shard_map/ppermute | solution.py:33
  57.6 4.9 %collective-permute-start.15 = (f32[24,128]{1,0:T(8,128)S(1)}, f32[24,128]{1,0:T(8,128)S(1)}, u32[]{:S(2)}, u32[]{:S(2)}) collective-permute-start(f32[24,128]{1,0:T(8,128)S(1)} %fusion.1.hh_ref), channel_id=1, source_target_pairs={{0,3},{1,2},{2,1},{3,0},{4,7},{5,6},{6,5},{7,4},{8,11},{9,10},{10,... | collective-permute-start | bytes 36872 | tf_op jit(solution)/shard_map/ppermute | solution.py:44
  68.2 6.5 %copy-start = (bf16[1024,256]{1,0:T(8,128)(2,1)S(1)}, bf16[1024,256]{1,0:T(8,128)(2,1)}, u32[]{:S(2)}) copy-start(bf16[1024,256]{1,0:T(8,128)(2,1)} %shard_map.67.own_ref) | copy-start | bytes 1572868
  68.2 6.5 %collective-permute-start.16 = (bf16[1024,256]{1,0:T(8,128)(2,1)}, bf16[1024,256]{1,0:T(8,128)(2,1)S(1)}, u32[]{:S(2)}, u32[]{:S(2)}) collective-permute-start(bf16[1024,256]{1,0:T(8,128)(2,1)} %shard_map.67.own_ref), channel_id=1, source_target_pairs={{0,4},{4,0},{8,12},{12,8},{16,20},{20,16},{24,28},{28,24},{32,36},... | collective-permute-start | bytes 1572872 | tf_op jit(solution)/shard_map/ppermute | solution.py:33
  68.5 12.1 %collective-permute-start.17 = (bf16[1024,256]{1,0:T(8,128)(2,1)}, bf16[1024,256]{1,0:T(8,128)(2,1)S(1)}, u32[]{:S(2)}, u32[]{:S(2)}) collective-permute-start(bf16[1024,256]{1,0:T(8,128)(2,1)} %shard_map.67.own_ref), channel_id=1, source_target_pairs={{0,124},{4,8},{8,4},{12,16},{16,12},{20,24},{24,20},{28,32},{32,28... | collective-permute-start | bytes 1572872 | tf_op jit(solution)/shard_map/ppermute | solution.py:39

commit v3 on v2

--- a/solution.py
+++ b/solution.py
@@ -27,6 +27,7 @@
 VMEM = pl.BlockSpec(memory_space=pltpu.VMEM)
 SMEM = pl.BlockSpec(memory_space=pltpu.SMEM)
 ANY = pl.BlockSpec(memory_space=pl.ANY)
+HBM = pl.BlockSpec(memory_space=pltpu.HBM)
 
 
 def sibling(value):
@@ -97,10 +98,40 @@
             g_ref[region * NBLK + 2 * pair + 1] = g[:, BLOCK:]
 
 
-def target_constants(target_ref, mass_row, window_ref, region):
+def block_masses(mass_ref, group, first):
+    rows = []
+    for block in range(NBLK):
+        lanes = slice(block * BLOCK, (block + 1) * BLOCK)
+        low, high = mass_ref[first : first + 1, lanes], mass_ref[first + 1 : first + 2, lanes]
+        rows.append(jnp.where(group == 0, low, high))
+    return jnp.concatenate(rows, axis=0)
+
+
+def pack_kernel(place_ref, cells_hbm, mass_hbm, message_ref, mass_ref, sems):
+    group = place_ref[1]
+    cells = pltpu.make_async_copy(cells_hbm.at[group + 1], message_ref.at[:CELLS], sems.at[0])
+    masses = pltpu.make_async_copy(mass_hbm, mass_ref, sems.at[1])
+    cells.start()
+    masses.start()
+    masses.wait()
+    left = block_masses(mass_ref, group, 1)
+    parts = []
+    for _ in range(3):
+        part = left.astype(jnp.bfloat16).astype(jnp.float32)
+        parts.append(part)
+        left = left - part
+    message_ref[CELLS:, :BLOCK] = jnp.concatenate(parts[:2], axis=0).astype(jnp.bfloat16)
+    tail = jnp.concatenate([parts[2], jnp.zeros_like(parts[2])], axis=0)
+    message_ref[CELLS:, BLOCK:] = tail.astype(jnp.bfloat16)
+    cells.wait()
+
+
+def target_constants(message_ref, window_ref, region):
+    parts = message_ref[CELLS:, :].astype(jnp.float32)
+    masses = (parts[:NBLK, :BLOCK] + parts[NBLK:, :BLOCK]) + parts[:NBLK, BLOCK:]
     ones = jnp.ones((8, EMB), jnp.bfloat16)
     for pair in range(NBLK // 2):
-        y = target_ref[pair * 256 : (pair + 1) * 256, :].astype(jnp.float32)
+        y = message_ref[pair * 256 : (pair + 1) * 256, :].astype(jnp.float32)
         square = y * y
         high = square.astype(jnp.bfloat16)
         low = (square - high.astype(jnp.float32)).astype(jnp.bfloat16)
@@ -111,19 +142,10 @@
         for half in range(2):
             block = 2 * pair + half
             scaled = norm[:1, half * BLOCK : (half + 1) * BLOCK] * SCALE
-            mass = mass_row(block) * LOG2E
+            mass = masses[block : block + 1, :] * LOG2E
             at = region * NBLK + block
             window_ref[0, at : at + 1, :] = mass - scaled
             window_ref[1, at : at + 1, :] = mass + (LAM - 1.0) * scaled
-
-
-def mass_rows(mass_ref, group, first):
-    def row(block):
-        lanes = slice(block * BLOCK, (block + 1) * BLOCK)
-        low, high = mass_ref[first : first + 1, lanes], mass_ref[first + 1 : first + 2, lanes]
-        return jnp.where(group == 0, low, high)
-
-    return row
 
 
 STRIPS = BLOCK // 8
@@ -256,27 +278,32 @@
         body(pl.ds(pl.multiple_of(chunk * 256, 256), 256))
 
 
-def near_kernel(place_ref, source_ref, own_ref, mass_hbm, sib_mass_ref, sib_ref, g_ref, kc_ref, window_ref, mass_ref, sem):
+def near_kernel(place_ref, cells_hbm, mass_hbm, own_ref, sib_ref, g_ref, kc_ref, window_ref, source_ref, mass_ref, sems):
     group = place_ref[1]
-    fetched = pltpu.make_async_copy(mass_hbm, mass_ref, sem)
-    fetched.start()
+    copies = (
+        pltpu.make_async_copy(cells_hbm.at[group], source_ref, sems.at[0]),
+        pltpu.make_async_copy(mass_hbm, mass_ref, sems.at[1]),
+    )
+    for copy in copies:
+        copy.start()
+    target_constants(own_ref, window_ref, 0)
+    target_constants(sib_ref, window_ref, 1)
+    copies[0].wait()
     products(source_ref, (own_ref, sib_ref), g_ref, 0)
-    target_constants(sib_ref, mass_rows(sib_mass_ref, group, 1), window_ref, 1)
-    fetched.wait()
-    target_constants(own_ref, mass_rows(mass_ref, group, 1), window_ref, 0)
-    source_mass = mass_rows(mass_ref, group, 0)
+    copies[1].wait()
+    masses = block_masses(mass_ref, group, 0)
     for s in range(NBLK):
         x = source_ref[s * BLOCK : (s + 1) * BLOCK, :].astype(jnp.float32)
         norm = jnp.sum(x * x, axis=1, keepdims=True) * SCALE
-        mass = jnp.broadcast_to(source_mass(s), (BLOCK, BLOCK)).T
+        mass = jnp.broadcast_to(masses[s : s + 1, :], (BLOCK, BLOCK)).T
         kc_ref[s * BLOCK : (s + 1) * BLOCK, :] = mass * LOG2E + (LAM - 1.0) * norm
 
 
-def far_kernel(place_ref, table_ref, source_ref, out_mass_ref, out_ref, near_ref, near_window_ref, g_ref, window_ref):
+def far_kernel(table_ref, source_ref, out_ref, near_ref, near_window_ref, g_ref, window_ref):
     del table_ref, near_ref
     window_ref[:, : 2 * NBLK, :] = near_window_ref[...]
     products(source_ref, (out_ref,), g_ref, 2)
-    target_constants(out_ref, mass_rows(out_mass_ref, place_ref[1], 1), window_ref, 2)
+    target_constants(out_ref, window_ref, 2)
 
 
 def other_kernel(behind_ref, source_ref, own_ref, sib_ref, out_ref, g_ref):
@@ -341,14 +368,23 @@
     return call(table_kernel, jax.ShapeDtypeStruct((TABLE,), jnp.int32), SMEM, specs)(place, behind, *slots)
 
 
+MESSAGE_SHAPE = jax.ShapeDtypeStruct((CELLS + 16, EMB), jnp.bfloat16)
+MASSES = pltpu.VMEM((3, CELLS), jnp.float32)
+
+
+def target_message(*args):
+    scratch = [MASSES, pltpu.SemaphoreType.DMA((2,))]
+    return call(pack_kernel, MESSAGE_SHAPE, VMEM, [SMEM, HBM, HBM], scratch)(*args)
+
+
 def near_products(*args):
-    specs = [SMEM, VMEM, VMEM, ANY, VMEM, VMEM]
-    scratch = [pltpu.VMEM((3, CELLS), jnp.float32), pltpu.SemaphoreType.DMA]
-    return call(near_kernel, (G_SHAPE, COLUMN_SHAPE, NEAR_SHAPE), (VMEM,) * 3, specs, scratch)(*args)
+    outs = (G_SHAPE, COLUMN_SHAPE, NEAR_SHAPE, FATE_SHAPE)
+    scratch = [MASSES, pltpu.SemaphoreType.DMA((2,))]
+    return call(near_kernel, outs, (VMEM,) * 4, [SMEM, HBM, HBM, VMEM, VMEM], scratch)(*args)
 
 
 def far_products(*args):
-    return call(far_kernel, (G_SHAPE, WINDOW_SHAPE), (VMEM,) * 2, [SMEM, SMEM] + [VMEM] * 5, aliases={5: 0})(*args)
+    return call(far_kernel, (G_SHAPE, WINDOW_SHAPE), (VMEM,) * 2, [SMEM] + [VMEM] * 4, aliases={3: 0})(*args)
 
 
 def sweep(*args):
@@ -413,18 +449,19 @@
     def moment(array, index):
         return lax.dynamic_index_in_dim(array, index, 0, keepdims=False)
 
-    target = moment(embeddings, group + 1)
+    cells, masses = (
+        pltpu.with_memory_space_constraint(array, pltpu.HBM) for array in (embeddings, log_mass)
+    )
+    target = target_message(place, cells, masses)
     target_out, target_sib = outward(target), sibling(target)
-    cells, masses, slots, target_sib = lax.optimization_barrier(
-        (embeddings, log_mass, tile_list, target_sib)
-    )
+    slots, target_sib = lax.optimization_barrier((tile_list, target_sib))
     gathered = [slots] + [shifted(slots, k) for k in range(1, lax.axis_size("tiles"))]
-    masses_out, masses_sib = outward(masses), sibling(masses)
-    source, other_source = moment(cells, group), moment(cells, 1 - group)
-    rest = jnp.concatenate([moment(cells, 2 - group), signatures])
-    g, kc, near = near_products(place, source, target, log_mass, masses_sib, target_sib)
+    g, kc, near, source = near_products(place, cells, masses, target, target_sib)
     table = build_table(place, near, gathered)
-    g, window = far_products(place, table, source, masses_out, target_out, g, near)
+    later, fates, near = lax.optimization_barrier((embeddings, signatures, near))
+    rest = jnp.concatenate([moment(later, 2 - group), fates])
+    other_source = moment(later, 1 - group)
+    g, window = far_products(table, source, target_out, g, near)
     part = sweep(table, window[0], kc, g)
     rest_out, rest_sib = outward(rest), sibling(rest)
 

time: 83.5 us -> 82.5 us (0.988)
  starting transfers between devices: 24.1 us -> 32.3 us
  waiting for transfers between devices: 16.7 us -> 11.8 us
  Pallas kernels: 38 us -> 36.1 us
  local copies, waits for them, and re-layouts: 2.63 us -> 1.05 us
    ppermute x6 -> x5, starting transfers between devices: 16.2 us -> 27.4 us  [outward(): return lax.ppermute(value, 'cells', pairs)]
    ppermute x6 -> x5, waiting for transfers between devices: 9.74 us -> 2.36 us  [outward(): return lax.ppermute(value, 'cells', pairs)]
    pallas_call x2, Pallas kernels: 9.66 us -> 6.55 us  [sweep(): call(sweep_kernel, PART_SHAPE, VMEM, [SMEM] + [VMEM] * 3, SWEEP_SCRATCH)]
    squeeze x2 -> x1, local copies, waits for them, and re-layouts: 2.6 us -> 0.08 us  [moment(): return lax.dynamic_index_in_dim(array, index, 0, keepdims=False)]
    pallas_call x2 -> x3, Pallas kernels: 6.45 us -> 8.57 us  [the longest x1 4.67 us: near_products(): call(near_kernel, outs, (VMEM,) * 4, [SMEM, HBM, HBM, VMEM, VMEM], scratch)]
    ppermute x1, starting transfers between devices: 2.03 us -> 0.01 us  [mirrored(): lax.ppermute(value, 'tiles', [(t, count - 1 - t) for t in range(count)])]
    ppermute x1, waiting for transfers between devices: 2.87 us -> 4.9 us  [mirrored(): lax.ppermute(value, 'tiles', [(t, count - 1 - t) for t in range(count)])]
    pallas_call x1, Pallas kernels: 3.87 us -> 2.88 us  [early_weights(): call(early_weights_kernel, (W_SHAPE, COLUMN_SHAPE), (VMEM, VMEM), COUPLIN...]
  transfers between devices with their start and end apart: 18 -> 16, of which waited for: 8 -> 6; matrix products, arithmetic and copies ran while one was open for 2% -> 0% of each run, Pallas kernels for 31% -> 28%
where the time goes in v3:
time: 82.5 us
  Pallas kernels  36.1 us (44%)
  starting transfers between devices  32.3 us (39%)
  waiting for transfers between devices  11.8 us (14%)
  local copies, waits for them, and re-layouts  1.05 us (1%)
  between operations  0.89 us (1%)
    ppermute x5, starting transfers between devices, outward(): return lax.ppermute(value, 'cells', pairs)  27.4 us
    pallas_call x2, Pallas kernels, sweep(): call(sweep_kernel, PART_SHAPE, VMEM, [SMEM] + [VMEM] * 3, SWEEP_SCRATCH)  6.55 us
    pallas_call x1, Pallas kernels, late_fates(): call(late_kernel, FATE_SHAPE, VMEM, COUPLINGS + [VMEM] * 3, HOLD + [TERMS...  5.66 us
    ppermute x1, waiting for transfers between devices, mirrored(): lax.ppermute(value, 'tiles', [(t, count - 1 - t) for t in range(count)])  4.9 us
    pallas_call x1, Pallas kernels, near_products(): call(near_kernel, outs, (VMEM,) * 4, [SMEM, HBM, HBM, VMEM, VMEM], scratch)  4.67 us
    ppermute x7, waiting for transfers between devices, sibling(): lax.ppermute(value, 'cells', [(c, c ^ 1) for c in range(lax.axis_size('ce...  4.55 us
    pallas_call x2, Pallas kernels, build_table(): call(table_kernel, jax.ShapeDtypeStruct((TABLE,), jnp.int32), SMEM, specs)  4.55 us
    ppermute x3, starting transfers between devices, shifted(): lax.ppermute(value, 'tiles', [(t, (t + steps) % count) for t in range(cou...  4.51 us
  transfers between devices with their start and end apart: 16, of which 6 were waited for; matrix products, arithmetic and copies ran while one was open for 0% of the time, Pallas kernels for 28%

profile of v3, /device:TPU:0, one launch (start us, length us, event | category | flops | bytes accessed | tf_op | source)
XLA Modules:
  0.0 82.5 jit_solution(2974491330754743119)
XLA Ops:
  0.7 1.6 %shard_map.59.own_ref = bf16[1040,256]{1,0:T(8,128)(2,1)S(1)} custom-call(s32[2]{0:T(128)S(1)} %pad_add_fusion.place_ref, bf16[3,1024,256]{2,1,0:T(8,128)(2,1)} %cells_hbm.3, f32[3,1024]{1,0:T(4,128)} %mass_hbm.3), custom_call_target="tpu_custom_call" | custom-call | flops 3000000000 | bytes 10000 | tf_op jit(solution)/shard_map/pallas_call | solution.py:377
  2.3 0.1 collective-permute-start
  2.4 6.7 %collective-permute-start.4 = (bf16[1040,256]{1,0:T(8,128)(2,1)S(1)}, bf16[1040,256]{1,0:T(8,128)(2,1)S(1)}, u32[]{:S(2)}, u32[]{:S(2)}) collective-permute-start(bf16[1040,256]{1,0:T(8,128)(2,1)S(1)} %shard_map.59.own_ref), channel_id=1, source_target_pairs={{0,124},{4,8},{8,4},{12,16},{16,12},{20,24},{24,20},{28,32},{32,28... | collective-permute-start | bytes 1597448 | tf_op jit(solution)/shard_map/ppermute | solution.py:40
  9.1 2.8 %collective-permute-start.3 = (s32[2,2,32]{2,1,0:T(2,128)S(1)}, s32[2,2,32]{2,1,0:T(2,128)S(1)}, u32[]{:S(2)}, u32[]{:S(2)}) collective-permute-start(s32[2,2,32]{2,1,0:T(2,128)S(1)} %copy-done.1), channel_id=1, source_target_pairs={{0,3},{1,0},{2,1},{3,2},{4,7},{5,4},{6,5},{7,6},{8,11},{9,8},{10,9... | collective-permute-start | bytes 1544 | tf_op jit(solution)/shard_map/ppermute | solution.py:441
  11.9 0.8 collective-permute-start.2
  12.7 0.9 %collective-permute-start.1 = (s32[2,2,32]{2,1,0:T(2,128)S(1)}, s32[2,2,32]{2,1,0:T(2,128)S(1)}, u32[]{:S(2)}, u32[]{:S(2)}) collective-permute-start(s32[2,2,32]{2,1,0:T(2,128)S(1)} %copy-done.1), channel_id=1, source_target_pairs={{0,1},{1,2},{2,3},{3,0},{4,5},{5,6},{6,7},{7,4},{8,9},{9,10},{10,1... | collective-permute-start | bytes 1544 | tf_op jit(solution)/shard_map/ppermute | solution.py:441
  13.6 4.7 %shard_map.60 = (f32[24,1024,128]{2,1,0:T(8,128)S(1)}, f32[1024,128]{1,0:T(8,128)S(1)}, f32[2,16,128]{2,1,0:T(8,128)S(1)}, bf16[1024,256]{1,0:T(8,128)(2,1)S(1)}) custom-call(s32[2]{0:T(128)S(1)} %pad_add_fusion.place_ref, bf16[3,1024,256]{2,1,0:T(8,128)(2,1)} %cells_hbm.3, f32[3,1024]{1,0:T(4,128)} %mass_hbm.3, bf16[1040,256]{1,0:T(8,128)(2,1)S(1)} %shard_map.59.own_ref, ...), custom_call_target="tpu_custom_call" | custom-call | flops 3000000000 | bytes 10000 | tf_op jit(solution)/shard_map/pallas_call | solution.py:383
  18.4 0.9 %copy-done.3 = bf16[1024,256]{1,0:T(8,128)(2,1)S(1)} copy-done((bf16[1024,256]{1,0:T(8,128)(2,1)S(1)}, bf16[1024,256]{1,0:T(8,128)(2,1)}, u32[]{:S(2)}) %copy-start.3) | copy-done | bytes 524312
  19.4 0.7 collective-permute-start.8
  20.1 2.3 %shard_map.61.table_ref = s32[512]{0:T(512)S(1)} custom-call(s32[2]{0:T(128)S(1)} %pad_add_fusion.place_ref, f32[2,16,128]{2,1,0:T(8,128)S(1)} %get-tuple-element.24.behind_ref.near_window_ref, s32[2,2,32]{2,1,0:T(2,128)S(1)} %copy-done.1, s32[2,2,32]{2,1,0:T(2,128)S(1)} %collective-permute-done.1.refs_1_, s32[2,2,32]{2,1,0:T(2,128)S(1)} %collective-permute-done.2.refs_2_, ...), custom_call_target="tpu_custom_call" | custom-call | flops 3000000000 | bytes 10000 | tf_op jit(solution)/shard_map/pallas_call | solution.py:368
  22.4 2.3 %shard_map.62 = (f32[24,1024,128]{2,1,0:T(8,128)S(1)}, f32[2,24,128]{2,1,0:T(8,128)S(1)}) custom-call(s32[512]{0:T(512)S(1)} %shard_map.61.table_ref, bf16[1024,256]{1,0:T(8,128)(2,1)S(1)} %get-tuple-element.22.source_ref, bf16[1040,256]{1,0:T(8,128)(2,1)S(1)} %collective-permute-done.4.out_ref, ...), custom_call_target="tpu_custom_call", output_to_operand_aliasing={{0}: (3, {})} | custom-call | flops 3000000000 | bytes 10000 | tf_op jit(solution)/shard_map/pallas_call | solution.py:387
  24.7 3.3 %shard_map.63 = f32[2,24,128]{2,1,0:T(8,128)S(1)} custom-call(s32[512]{0:T(512)S(1)} %shard_map.61.table_ref, f32[24,128]{1,0:T(8,128)S(1)} %slice_bitcast_fusion.hh_ref, f32[1024,128]{1,0:T(8,128)S(1)} %get-tuple-element.26.kc_ref, f32[24,1024,128]{2,1,0:T(8,128)S(1)} %get-tuple-element.27.g_ref), custom_call_target="tpu_custom_call" | custom-call | flops 3000000000 | bytes 10000 | tf_op jit(solution)/shard_map/pallas_call | solution.py:391
  28.0 0.1 collective-permute-start.5
  28.1 1.2 %collective-permute-done.5 = f32[2,8,128]{2,1,0:T(8,128)S(1)} collective-permute-done((f32[2,8,128]{2,1,0:T(8,128)S(1)}, f32[2,8,128]{2,1,0:T(8,128)S(1)}, u32[]{:S(2)}, u32[]{:S(2)}) %collective-permute-start.5) | collective-permute-done | bytes 8224 | tf_op jit(solution)/shard_map/ppermute | solution.py:34
  29.3 8.2 %collective-permute-start.6 = (f32[2,16,128]{2,1,0:T(8,128)S(1)}, f32[2,16,128]{2,1,0:T(8,128)S(1)}, u32[]{:S(2)}, u32[]{:S(2)}) collective-permute-start(f32[2,16,128]{2,1,0:T(8,128)S(1)} %pad_maximum_fusion.1.behind_ref), channel_id=1, source_target_pairs={{0,124},{4,8},{8,4},{12,16},{16,12},{20,24},{24,20},{28,32},{32,28... | collective-permute-start | bytes 49160 | tf_op jit(solution)/shard_map/ppermute | solution.py:40
  37.5 4.0 %shard_map.64.g2_ref = f32[24,1024,128]{2,1,0:T(8,128)S(1)} custom-call(f32[2,16,128]{2,1,0:T(8,128)S(1)} %pad_maximum_fusion.1.behind_ref, bf16[1024,256]{1,0:T(8,128)(2,1)S(1)} %get-tuple-element.41.source_ref, bf16[2048,256]{1,0:T(8,128)(2,1)S(1)} %pad_maximum_fusion.own_ref, bf16[2048,256]{1,0:T(8,128)(2,1)S(1)} %collective-permute-done.7.sib_ref, ...), custom_call_target="tpu_custom_call" | custom-call | flops 3000000000 | bytes 10000 | tf_op jit(solution)/shard_map/pallas_call | solution.py:395
  41.6 0.1 collective-permute-start.9
  41.7 1.2 %collective-permute-done.9 = f32[8,128]{1,0:T(8,128)S(1)} collective-permute-done((f32[8,128]{1,0:T(8,128)S(1)}, f32[8,128]{1,0:T(8,128)S(1)}, u32[]{:S(2)}, u32[]{:S(2)}) %collective-permute-start.9) | collective-permute-done | bytes 4128 | tf_op jit(solution)/shard_map/ppermute | solution.py:34
  42.9 3.3 %shard_map.65 = f32[2,24,128]{2,1,0:T(8,128)S(1)} custom-call(s32[512]{0:T(512)S(1)} %shard_map.61.table_ref, f32[24,128]{1,0:T(8,128)S(1)} %fusion.hh_ref, f32[1024,128]{1,0:T(8,128)S(1)} %get-tuple-element.26.kc_ref, f32[24,1024,128]{2,1,0:T(8,128)S(1)} %get-tuple-element.27.g_ref), custom_call_target="tpu_custom_call" | custom-call | flops 3000000000 | bytes 10000 | tf_op jit(solution)/shard_map/pallas_call | solution.py:391
  46.2 0.1 collective-permute-start.10
  46.3 1.1 %collective-permute-done.10 = f32[2,8,128]{2,1,0:T(8,128)S(1)} collective-permute-done((f32[2,8,128]{2,1,0:T(8,128)S(1)}, f32[2,8,128]{2,1,0:T(8,128)S(1)}, u32[]{:S(2)}, u32[]{:S(2)}) %collective-permute-start.10) | collective-permute-done | bytes 8224 | tf_op jit(solution)/shard_map/ppermute | solution.py:34
  47.4 5.9 %collective-permute-start.11 = (f32[2,16,128]{2,1,0:T(8,128)S(1)}, f32[2,16,128]{2,1,0:T(8,128)S(1)}, u32[]{:S(2)}, u32[]{:S(2)}) collective-permute-start(f32[2,16,128]{2,1,0:T(8,128)S(1)} %pad_maximum_fusion.2.behind_ref), channel_id=1, source_target_pairs={{0,124},{4,8},{8,4},{12,16},{16,12},{20,24},{24,20},{28,32},{32,28... | collective-permute-start | bytes 49160 | tf_op jit(solution)/shard_map/ppermute | solution.py:40
  53.3 2.3 %shard_map.66.table2_ref = s32[512]{0:T(512)S(1)} custom-call(s32[2]{0:T(128)S(1)} %pad_add_fusion.1.place_ref, f32[2,16,128]{2,1,0:T(8,128)S(1)} %pad_maximum_fusion.2.behind_ref, s32[2,2,32]{2,1,0:T(2,128)S(1)} %copy-done.1, s32[2,2,32]{2,1,0:T(2,128)S(1)} %collective-permute-done.1.refs_1_, s32[2,2,32]{2,1,0:T(2,128)S(1)} %collective-permute-done.2.refs_2_, ...), custom_call_target="tpu_custom_call" | custom-call | flops 3000000000 | bytes 10000 | tf_op jit(solution)/shard_map/pallas_call | solution.py:368
  55.6 0.1 collective-permute-start.12
  55.7 1.2 %collective-permute-done.12 = f32[8,128]{1,0:T(8,128)S(1)} collective-permute-done((f32[8,128]{1,0:T(8,128)S(1)}, f32[8,128]{1,0:T(8,128)S(1)}, u32[]{:S(2)}, u32[]{:S(2)}) %collective-permute-start.12) | collective-permute-done | bytes 4128 | tf_op jit(solution)/shard_map/ppermute | solution.py:34
  56.9 4.9 %collective-permute-done.13.hh2_ref = f32[24,128]{1,0:T(8,128)S(1)} collective-permute-done((f32[24,128]{1,0:T(8,128)S(1)}, f32[24,128]{1,0:T(8,128)S(1)}, u32[]{:S(2)}, u32[]{:S(2)}) %collective-permute-start.13) | collective-permute-done | bytes 12320 | tf_op jit(solution)/shard_map/ppermute | solution.py:45
  61.8 5.7 %shard_map.68.own_ref = bf16[1024,256]{1,0:T(8,128)(2,1)} custom-call(s32[2]{0:T(128)S(1)} %pad_add_fusion.place_ref, s32[512]{0:T(512)S(1)} %shard_map.61.table_ref, f32[24,128]{1,0:T(8,128)S(1)} %fusion.1.hh_ref, f32[24,1024,128]{2,1,0:T(8,128)S(1)} %get-tuple-element.27.g_ref, s32[512]{0:T(512)S(1)} %shard_map.66.table2_ref, ...), custom_call_target="tpu_custom_call" | custom-call | flops 3000000000 | bytes 10000 | tf_op jit(solution)/shard_map/pallas_call | solution.py:402
  67.4 5.9 %collective-permute-start.15 = (bf16[1024,256]{1,0:T(8,128)(2,1)}, bf16[1024,256]{1,0:T(8,128)(2,1)S(1)}, u32[]{:S(2)}, u32[]{:S(2)}) collective-permute-start(bf16[1024,256]{1,0:T(8,128)(2,1)} %shard_map.68.own_ref), channel_id=1, source_target_pairs={{0,124},{4,8},{8,4},{12,16},{16,12},{20,24},{24,20},{28,32},{32,28... | collective-permute-start | bytes 1572872 | tf_op jit(solution)/shard_map/ppermute | solution.py:40
  73.4 2.9 %shard_map.67 = (bf16[1024,3200]{1,0:T(8,128)(2,1)S(1)}, f32[1024,128]{1,0:T(8,128)S(1)}) custom-call(s32[2]{0:T(128)S(1)} %pad_add_fusion.place_ref, s32[512]{0:T(512)S(1)} %shard_map.61.table_ref, f32[24,128]{1,0:T(8,128)S(1)} %fusion.1.hh_ref, f32[24,1024,128]{2,1,0:T(8,128)S(1)} %get-tuple-element.27.g_ref, s32[512]{0:T(512)S(1)} %shard_map.66.table2_ref, ...), custom_call_target="tpu_custom_call" | custom-call | flops 3000000000 | bytes 10000 | tf_op jit(solution)/shard_map/pallas_call | solution.py:406
  76.3 1.8 %shard_map.69.total_ref = f32[1024,256]{1,0:T(8,128)S(1)} custom-call(bf16[1024,3200]{1,0:T(8,128)(2,1)S(1)} %get-tuple-element.34.w_ref, bf16[1024,256]{1,0:T(8,128)(2,1)S(1)} %copy-done, bf16[1024,256]{1,0:T(8,128)(2,1)S(1)} %collective-permute-done.14.sib_ref), custom_call_target="tpu_custom_call" | custom-call | flops 3000000000 | bytes 10000 | tf_op jit(solution)/shard_map/pallas_call | solution.py:410
  78.1 2.4 %collective-permute-done.15.out_ref = bf16[1024,256]{1,0:T(8,128)(2,1)S(1)} collective-permute-done((bf16[1024,256]{1,0:T(8,128)(2,1)}, bf16[1024,256]{1,0:T(8,128)(2,1)S(1)}, u32[]{:S(2)}, u32[]{:S(2)}) %collective-permute-start.15) | collective-permute-done | bytes 524320 | tf_op jit(solution)/shard_map/ppermute | solution.py:40
  80.5 2.0 %shard_map.70 = bf16[1024,256]{1,0:T(8,128)(2,1)} custom-call(bf16[1024,3200]{1,0:T(8,128)(2,1)S(1)} %get-tuple-element.34.w_ref, f32[1024,128]{1,0:T(8,128)S(1)} %get-tuple-element.35.sum_ref, f32[1024,256]{1,0:T(8,128)S(1)} %shard_map.69.total_ref, bf16[1024,256]{1,0:T(8,128)(2,1)S(1)} %collective-permute-done.15.out_ref), custom_call_target="tpu_custom_call" | custom-call | flops 3000000000 | bytes 10000 | tf_op jit(solution)/shard_map/pallas_call | solution.py:414
  (35 shorter events, 0.5 us)
Async XLA Ops:
  0.7 8.4 %copy-start.1 = (s32[2,2,32]{2,1,0:T(2,128)S(1)}, s32[2,2,32]{2,1,0:T(2,128)}, u32[]{:S(2)}) copy-start(s32[2,2,32]{2,1,0:T(2,128)} %refs_0_.1) | copy-start | bytes 1540
  2.3 6.8 %collective-permute-start = (bf16[1040,256]{1,0:T(8,128)(2,1)S(1)}, bf16[1040,256]{1,0:T(8,128)(2,1)S(1)}, u32[]{:S(2)}, u32[]{:S(2)}) collective-permute-start(bf16[1040,256]{1,0:T(8,128)(2,1)S(1)} %shard_map.59.own_ref), channel_id=1, source_target_pairs={{0,4},{4,0},{8,12},{12,8},{16,20},{20,16},{24,28},{28,24},{32,36},... | collective-permute-start | bytes 1597448 | tf_op jit(solution)/shard_map/ppermute | solution.py:34
  2.4 20.0 %collective-permute-start.4 = (bf16[1040,256]{1,0:T(8,128)(2,1)S(1)}, bf16[1040,256]{1,0:T(8,128)(2,1)S(1)}, u32[]{:S(2)}, u32[]{:S(2)}) collective-permute-start(bf16[1040,256]{1,0:T(8,128)(2,1)S(1)} %shard_map.59.own_ref), channel_id=1, source_target_pairs={{0,124},{4,8},{8,4},{12,16},{16,12},{20,24},{24,20},{28,32},{32,28... | collective-permute-start | bytes 1597448 | tf_op jit(solution)/shard_map/ppermute | solution.py:40
  9.1 9.2 %copy-start.2 = (bf16[3,1024,256]{2,1,0:T(8,128)(2,1)S(1)}, bf16[3,1024,256]{2,1,0:T(8,128)(2,1)}, u32[]{:S(2)}) copy-start(bf16[3,1024,256]{2,1,0:T(8,128)(2,1)} %cells_hbm.3) | copy-start | bytes 4718596
  9.1 11.0 %collective-permute-start.3 = (s32[2,2,32]{2,1,0:T(2,128)S(1)}, s32[2,2,32]{2,1,0:T(2,128)S(1)}, u32[]{:S(2)}, u32[]{:S(2)}) collective-permute-start(s32[2,2,32]{2,1,0:T(2,128)S(1)} %copy-done.1), channel_id=1, source_target_pairs={{0,3},{1,0},{2,1},{3,2},{4,7},{5,4},{6,5},{7,6},{8,11},{9,8},{10,9... | collective-permute-start | bytes 1544 | tf_op jit(solution)/shard_map/ppermute | solution.py:441
  11.9 8.2 %collective-permute-start.2 = (s32[2,2,32]{2,1,0:T(2,128)S(1)}, s32[2,2,32]{2,1,0:T(2,128)S(1)}, u32[]{:S(2)}, u32[]{:S(2)}) collective-permute-start(s32[2,2,32]{2,1,0:T(2,128)S(1)} %copy-done.1), channel_id=1, source_target_pairs={{0,2},{1,3},{2,0},{3,1},{4,6},{5,7},{6,4},{7,5},{8,10},{9,11},{10,... | collective-permute-start | bytes 1544 | tf_op jit(solution)/shard_map/ppermute | solution.py:441
  12.7 7.4 %collective-permute-start.1 = (s32[2,2,32]{2,1,0:T(2,128)S(1)}, s32[2,2,32]{2,1,0:T(2,128)S(1)}, u32[]{:S(2)}, u32[]{:S(2)}) collective-permute-start(s32[2,2,32]{2,1,0:T(2,128)S(1)} %copy-done.1), channel_id=1, source_target_pairs={{0,1},{1,2},{2,3},{3,0},{4,5},{5,6},{6,7},{7,4},{8,9},{9,10},{10,1... | collective-permute-start | bytes 1544 | tf_op jit(solution)/shard_map/ppermute | solution.py:441
  18.3 1.0 %copy-start.3 = (bf16[1024,256]{1,0:T(8,128)(2,1)S(1)}, bf16[1024,256]{1,0:T(8,128)(2,1)}, u32[]{:S(2)}) copy-start(bf16[1024,256]{1,0:T(8,128)(2,1)} %param.6) | copy-start | bytes 1572868
  19.4 18.1 %collective-permute-start.8 = (bf16[2048,256]{1,0:T(8,128)(2,1)S(1)}, bf16[2048,256]{1,0:T(8,128)(2,1)S(1)}, u32[]{:S(2)}, u32[]{:S(2)}) collective-permute-start(bf16[2048,256]{1,0:T(8,128)(2,1)S(1)} %pad_maximum_fusion.own_ref), channel_id=1, source_target_pairs={{0,124},{4,8},{8,4},{12,16},{16,12},{20,24},{24,20},{28,32},{32,28... | collective-permute-start | bytes 3145736 | tf_op jit(solution)/shard_map/ppermute | solution.py:40
  20.1 17.4 %collective-permute-start.7 = (bf16[2048,256]{1,0:T(8,128)(2,1)S(1)}, bf16[2048,256]{1,0:T(8,128)(2,1)S(1)}, u32[]{:S(2)}, u32[]{:S(2)}) collective-permute-start(bf16[2048,256]{1,0:T(8,128)(2,1)S(1)} %pad_maximum_fusion.own_ref), channel_id=1, source_target_pairs={{0,4},{4,0},{8,12},{12,8},{16,20},{20,16},{24,28},{28,24},{32,36},... | collective-permute-start | bytes 3145736 | tf_op jit(solution)/shard_map/ppermute | solution.py:34
  28.0 1.3 %collective-permute-start.5 = (f32[2,8,128]{2,1,0:T(8,128)S(1)}, f32[2,8,128]{2,1,0:T(8,128)S(1)}, u32[]{:S(2)}, u32[]{:S(2)}) collective-permute-start(f32[2,8,128]{2,1,0:T(8,128)S(1)} %get-tuple-element.48), channel_id=1, source_target_pairs={{0,4},{4,0},{8,12},{12,8},{16,20},{20,16},{24,28},{28,24},{32,36},... | collective-permute-start | bytes 24584 | tf_op jit(solution)/shard_map/ppermute | solution.py:34
  29.3 12.3 %collective-permute-start.6 = (f32[2,16,128]{2,1,0:T(8,128)S(1)}, f32[2,16,128]{2,1,0:T(8,128)S(1)}, u32[]{:S(2)}, u32[]{:S(2)}) collective-permute-start(f32[2,16,128]{2,1,0:T(8,128)S(1)} %pad_maximum_fusion.1.behind_ref), channel_id=1, source_target_pairs={{0,124},{4,8},{8,4},{12,16},{16,12},{20,24},{24,20},{28,32},{32,28... | collective-permute-start | bytes 49160 | tf_op jit(solution)/shard_map/ppermute | solution.py:40
  41.6 1.2 %collective-permute-start.9 = (f32[8,128]{1,0:T(8,128)S(1)}, f32[8,128]{1,0:T(8,128)S(1)}, u32[]{:S(2)}, u32[]{:S(2)}) collective-permute-start(f32[8,128]{1,0:T(8,128)S(1)} %get-tuple-element.44), channel_id=1, source_target_pairs={{0,4},{4,0},{8,12},{12,8},{16,20},{20,16},{24,28},{28,24},{32,36},... | collective-permute-start | bytes 12296 | tf_op jit(solution)/shard_map/ppermute | solution.py:34
  46.2 1.3 %collective-permute-start.10 = (f32[2,8,128]{2,1,0:T(8,128)S(1)}, f32[2,8,128]{2,1,0:T(8,128)S(1)}, u32[]{:S(2)}, u32[]{:S(2)}) collective-permute-start(f32[2,8,128]{2,1,0:T(8,128)S(1)} %get-tuple-element.46), channel_id=1, source_target_pairs={{0,4},{4,0},{8,12},{12,8},{16,20},{20,16},{24,28},{28,24},{32,36},... | collective-permute-start | bytes 24584 | tf_op jit(solution)/shard_map/ppermute | solution.py:34
  47.4 8.1 %collective-permute-start.11 = (f32[2,16,128]{2,1,0:T(8,128)S(1)}, f32[2,16,128]{2,1,0:T(8,128)S(1)}, u32[]{:S(2)}, u32[]{:S(2)}) collective-permute-start(f32[2,16,128]{2,1,0:T(8,128)S(1)} %pad_maximum_fusion.2.behind_ref), channel_id=1, source_target_pairs={{0,124},{4,8},{8,4},{12,16},{16,12},{20,24},{24,20},{28,32},{32,28... | collective-permute-start | bytes 49160 | tf_op jit(solution)/shard_map/ppermute | solution.py:40
  55.6 1.2 %collective-permute-start.12 = (f32[8,128]{1,0:T(8,128)S(1)}, f32[8,128]{1,0:T(8,128)S(1)}, u32[]{:S(2)}, u32[]{:S(2)}) collective-permute-start(f32[8,128]{1,0:T(8,128)S(1)} %get-tuple-element.42), channel_id=1, source_target_pairs={{0,4},{4,0},{8,12},{12,8},{16,20},{20,16},{24,28},{28,24},{32,36},... | collective-permute-start | bytes 12296 | tf_op jit(solution)/shard_map/ppermute | solution.py:34
  56.9 4.9 %collective-permute-start.13 = (f32[24,128]{1,0:T(8,128)S(1)}, f32[24,128]{1,0:T(8,128)S(1)}, u32[]{:S(2)}, u32[]{:S(2)}) collective-permute-start(f32[24,128]{1,0:T(8,128)S(1)} %fusion.1.hh_ref), channel_id=1, source_target_pairs={{0,3},{1,2},{2,1},{3,0},{4,7},{5,6},{6,5},{7,4},{8,11},{9,10},{10,... | collective-permute-start | bytes 36872 | tf_op jit(solution)/shard_map/ppermute | solution.py:45
  67.4 8.9 %copy-start = (bf16[1024,256]{1,0:T(8,128)(2,1)S(1)}, bf16[1024,256]{1,0:T(8,128)(2,1)}, u32[]{:S(2)}) copy-start(bf16[1024,256]{1,0:T(8,128)(2,1)} %shard_map.68.own_ref) | copy-start | bytes 1572868
  67.4 8.8 %collective-permute-start.14 = (bf16[1024,256]{1,0:T(8,128)(2,1)}, bf16[1024,256]{1,0:T(8,128)(2,1)S(1)}, u32[]{:S(2)}, u32[]{:S(2)}) collective-permute-start(bf16[1024,256]{1,0:T(8,128)(2,1)} %shard_map.68.own_ref), channel_id=1, source_target_pairs={{0,4},{4,0},{8,12},{12,8},{16,20},{20,16},{24,28},{28,24},{32,36},... | collective-permute-start | bytes 1572872 | tf_op jit(solution)/shard_map/ppermute | solution.py:34
  67.4 13.0 %collective-permute-start.15 = (bf16[1024,256]{1,0:T(8,128)(2,1)}, bf16[1024,256]{1,0:T(8,128)(2,1)S(1)}, u32[]{:S(2)}, u32[]{:S(2)}) collective-permute-start(bf16[1024,256]{1,0:T(8,128)(2,1)} %shard_map.68.own_ref), channel_id=1, source_target_pairs={{0,124},{4,8},{8,4},{12,16},{16,12},{20,24},{24,20},{28,32},{32,28... | collective-permute-start | bytes 1572872 | tf_op jit(solution)/shard_map/ppermute | solution.py:40

commit v4 on v3

--- a/solution.py
+++ b/solution.py
@@ -58,26 +58,27 @@
     )
 
 
-def table_kernel(place_ref, behind_ref, *refs):
-    del behind_ref
-    *slot_refs, table_ref = refs
-    owner, coupling = place_ref[0], place_ref[1]
+def start_table(table_ref):
     for s in range(NBLK + 1):
         table_ref[GROUPS + s] = 0
 
-    @pl.loop(0, slot_refs[0].shape[2] // 2)
-    def _(pair):
+
+def extend_table(place_ref, coupling, slot_refs, table_ref, step):
+    owner = place_ref[0]
+    share = slot_refs[0].shape[2] // 4
+    for index in range(share):
         for slot_ref in slot_refs:
-            for half in range(2):
-                source = slot_ref[coupling, 0, 2 * pair + half]
-                target = slot_ref[coupling, 1, 2 * pair + half]
-                away = target >> 3
-                region = jnp.where(away == owner, 0, jnp.where(away == (owner ^ 1), NBLK, 2 * NBLK))
-                s = jnp.where(source < 0, NBLK, source & 7)
-                count = table_ref[GROUPS + s]
-                table_ref[GROUPS + s] = count + 1
-                table_ref[s * STRIDE + count] = region + (target & 7)
-
+            source = slot_ref[coupling, 0, step * share + index]
+            target = slot_ref[coupling, 1, step * share + index]
+            away = target >> 3
+            region = jnp.where(away == owner, 0, jnp.where(away == (owner ^ 1), NBLK, 2 * NBLK))
+            s = jnp.where(source < 0, NBLK, source & 7)
+            count = table_ref[GROUPS + s]
+            table_ref[GROUPS + s] = count + 1
+            table_ref[s * STRIDE + count] = region + (target & 7)
+
+
+def close_table(table_ref):
     for s in range(NBLK):
         count = table_ref[GROUPS + s]
         for extra in range(QUAD - 1):
@@ -85,11 +86,13 @@
         table_ref[GROUPS + s] = (count + QUAD - 1) >> 2
 
 
-def products(source_ref, target_refs, g_ref, first):
+def products(source_ref, target_refs, g_ref, first, beside=None):
     for region, target_ref in enumerate(target_refs, first):
 
         @pl.loop(0, NBLK // 2)
         def _(pair):
+            if beside is not None and region == first:
+                beside(pair)
             rows = target_ref[pl.ds(pl.multiple_of(pair * 256, 256), 256), :]
             g = lax.dot_general(
                 source_ref[...], rows, (((1,), (1,)), ((), ())), preferred_element_type=jnp.float32
@@ -110,26 +113,14 @@
 def pack_kernel(place_ref, cells_hbm, mass_hbm, message_ref, mass_ref, sems):
     group = place_ref[1]
     cells = pltpu.make_async_copy(cells_hbm.at[group + 1], message_ref.at[:CELLS], sems.at[0])
-    masses = pltpu.make_async_copy(mass_hbm, mass_ref, sems.at[1])
+    fetched = pltpu.make_async_copy(mass_hbm, mass_ref, sems.at[1])
     cells.start()
-    masses.start()
-    masses.wait()
-    left = block_masses(mass_ref, group, 1)
-    parts = []
-    for _ in range(3):
-        part = left.astype(jnp.bfloat16).astype(jnp.float32)
-        parts.append(part)
-        left = left - part
-    message_ref[CELLS:, :BLOCK] = jnp.concatenate(parts[:2], axis=0).astype(jnp.bfloat16)
-    tail = jnp.concatenate([parts[2], jnp.zeros_like(parts[2])], axis=0)
-    message_ref[CELLS:, BLOCK:] = tail.astype(jnp.bfloat16)
+    fetched.start()
+    fetched.wait()
+    masses = block_masses(mass_ref, group, 1) * LOG2E
     cells.wait()
-
-
-def target_constants(message_ref, window_ref, region):
-    parts = message_ref[CELLS:, :].astype(jnp.float32)
-    masses = (parts[:NBLK, :BLOCK] + parts[NBLK:, :BLOCK]) + parts[:NBLK, BLOCK:]
     ones = jnp.ones((8, EMB), jnp.bfloat16)
+    norms = []
     for pair in range(NBLK // 2):
         y = message_ref[pair * 256 : (pair + 1) * 256, :].astype(jnp.float32)
         square = y * y
@@ -139,13 +130,25 @@
             lax.dot_general(ones, part, (((1,), (1,)), ((), ())), preferred_element_type=jnp.float32)
             for part in (high, low)
         )
-        for half in range(2):
-            block = 2 * pair + half
-            scaled = norm[:1, half * BLOCK : (half + 1) * BLOCK] * SCALE
-            mass = masses[block : block + 1, :] * LOG2E
-            at = region * NBLK + block
-            window_ref[0, at : at + 1, :] = mass - scaled
-            window_ref[1, at : at + 1, :] = mass + (LAM - 1.0) * scaled
+        norms += [norm[:1, :BLOCK], norm[:1, BLOCK:]]
+    norms = jnp.concatenate(norms, axis=0) * SCALE
+    for half, left in enumerate((masses - norms, masses + (LAM - 1.0) * norms)):
+        parts = []
+        for _ in range(3):
+            part = left.astype(jnp.bfloat16).astype(jnp.float32)
+            parts.append(part)
+            left = left - part
+        parts.append(jnp.zeros_like(left))
+        packed = jnp.concatenate(parts, axis=0).astype(jnp.bfloat16)
+        message_ref[CELLS:, half * BLOCK : (half + 1) * BLOCK] = packed
+
+
+def unpack(message_ref, window_ref, region):
+    parts = message_ref[CELLS:, :].astype(jnp.float32)
+    for half in range(2):
+        p = parts[:, half * BLOCK : (half + 1) * BLOCK]
+        total = (p[:NBLK] + p[NBLK : 2 * NBLK]) + p[2 * NBLK : 3 * NBLK]
+        window_ref[half, region * NBLK : (region + 1) * NBLK, :] = total
 
 
 STRIPS = BLOCK // 8
@@ -278,7 +281,9 @@
         body(pl.ds(pl.multiple_of(chunk * 256, 256), 256))
 
 
-def near_kernel(place_ref, cells_hbm, mass_hbm, own_ref, sib_ref, g_ref, kc_ref, window_ref, source_ref, mass_ref, sems):
+def near_kernel(place_ref, *refs):
+    *slot_refs, cells_hbm, mass_hbm, own_ref, sib_ref = refs[: len(refs) - 7]
+    g_ref, kc_ref, window_ref, source_ref, table_ref, mass_ref, sems = refs[len(refs) - 7 :]
     group = place_ref[1]
     copies = (
         pltpu.make_async_copy(cells_hbm.at[group], source_ref, sems.at[0]),
@@ -286,10 +291,18 @@
     )
     for copy in copies:
         copy.start()
-    target_constants(own_ref, window_ref, 0)
-    target_constants(sib_ref, window_ref, 1)
+    unpack(own_ref, window_ref, 0)
+    unpack(sib_ref, window_ref, 1)
     copies[0].wait()
-    products(source_ref, (own_ref, sib_ref), g_ref, 0)
+    start_table(table_ref)
+    products(
+        source_ref,
+        (own_ref, sib_ref),
+        g_ref,
+        0,
+        lambda step: extend_table(place_ref, place_ref[1], slot_refs, table_ref, step),
+    )
+    close_table(table_ref)
     copies[1].wait()
     masses = block_masses(mass_ref, group, 0)
     for s in range(NBLK):
@@ -299,16 +312,26 @@
         kc_ref[s * BLOCK : (s + 1) * BLOCK, :] = mass * LOG2E + (LAM - 1.0) * norm
 
 
-def far_kernel(table_ref, source_ref, out_ref, near_ref, near_window_ref, g_ref, window_ref):
-    del table_ref, near_ref
+def far_kernel(table_ref, source_ref, out_ref, near_ref, near_window_ref, kc_ref, g_ref, window_ref, part_ref, *scratch):
+    del near_ref
     window_ref[:, : 2 * NBLK, :] = near_window_ref[...]
+    unpack(out_ref, window_ref, 2)
     products(source_ref, (out_ref,), g_ref, 2)
-    target_constants(out_ref, window_ref, 2)
-
-
-def other_kernel(behind_ref, source_ref, own_ref, sib_ref, out_ref, g_ref):
+    sweep_kernel(table_ref, window_ref.at[0], kc_ref, g_ref, part_ref, *scratch)
+
+
+def other_kernel(place_ref, behind_ref, *refs):
+    *slot_refs, source_ref, own_ref, sib_ref, out_ref, g_ref, table_ref = refs
     del behind_ref
-    products(source_ref, [ref.at[:CELLS] for ref in (own_ref, sib_ref, out_ref)], g_ref, 0)
+    start_table(table_ref)
+    products(
+        source_ref,
+        [ref.at[:CELLS] for ref in (own_ref, sib_ref, out_ref)],
+        g_ref,
+        0,
+        lambda step: extend_table(place_ref, 1 - place_ref[1], slot_refs, table_ref, step),
+    )
+    close_table(table_ref)
 
 
 def weigh_one(coupling, place_ref, mine, others, *outs):
@@ -363,12 +386,8 @@
 NEAR_SHAPE = jax.ShapeDtypeStruct((2, 2 * NBLK, BLOCK), jnp.float32)
 
 
-def build_table(place, behind, slots):
-    specs = [SMEM, ANY] + [SMEM] * len(slots)
-    return call(table_kernel, jax.ShapeDtypeStruct((TABLE,), jnp.int32), SMEM, specs)(place, behind, *slots)
-
-
-MESSAGE_SHAPE = jax.ShapeDtypeStruct((CELLS + 16, EMB), jnp.bfloat16)
+TABLE_SHAPE = jax.ShapeDtypeStruct((TABLE,), jnp.int32)
+MESSAGE_SHAPE = jax.ShapeDtypeStruct((CELLS + 4 * NBLK, EMB), jnp.bfloat16)
 MASSES = pltpu.VMEM((3, CELLS), jnp.float32)
 
 
@@ -377,22 +396,25 @@
     return call(pack_kernel, MESSAGE_SHAPE, VMEM, [SMEM, HBM, HBM], scratch)(*args)
 
 
-def near_products(*args):
-    outs = (G_SHAPE, COLUMN_SHAPE, NEAR_SHAPE, FATE_SHAPE)
+def near_products(place, slots, *args):
+    outs = (G_SHAPE, COLUMN_SHAPE, NEAR_SHAPE, FATE_SHAPE, TABLE_SHAPE)
+    in_specs = [SMEM] * (1 + len(slots)) + [HBM, HBM, VMEM, VMEM]
     scratch = [MASSES, pltpu.SemaphoreType.DMA((2,))]
-    return call(near_kernel, outs, (VMEM,) * 4, [SMEM, HBM, HBM, VMEM, VMEM], scratch)(*args)
+    return call(near_kernel, outs, (VMEM,) * 4 + (SMEM,), in_specs, scratch)(place, *slots, *args)
 
 
 def far_products(*args):
-    return call(far_kernel, (G_SHAPE, WINDOW_SHAPE), (VMEM,) * 2, [SMEM] + [VMEM] * 4, aliases={3: 0})(*args)
+    outs = (G_SHAPE, WINDOW_SHAPE, PART_SHAPE)
+    return call(far_kernel, outs, (VMEM,) * 3, [SMEM] + [VMEM] * 5, SWEEP_SCRATCH, {3: 0})(*args)
 
 
 def sweep(*args):
     return call(sweep_kernel, PART_SHAPE, VMEM, [SMEM] + [VMEM] * 3, SWEEP_SCRATCH)(*args)
 
 
-def other_products(*args):
-    return call(other_kernel, G_SHAPE, VMEM, [ANY] + [VMEM] * 4)(*args)
+def other_products(place, behind, slots, *args):
+    in_specs = [SMEM, ANY] + [SMEM] * len(slots) + [VMEM] * 4
+    return call(other_kernel, (G_SHAPE, TABLE_SHAPE), (VMEM, SMEM), in_specs)(place, behind, *slots, *args)
 
 
 COUPLINGS = [SMEM, SMEM, VMEM, VMEM, SMEM, VMEM, VMEM]
@@ -424,7 +446,7 @@
     )
 
 
-def folded(part, beside):
+def folded(part, beside=lambda message: None):
     own = merged(part[:, :NBLK], sibling(part[:, NBLK : 2 * NBLK]))
     beyond = part[:, 2 * NBLK :]
     message = jnp.concatenate([own, beyond], axis=1)
@@ -444,7 +466,7 @@
 def on_device(embeddings, log_mass, signatures, tile_list):
     owner = lax.axis_index("cells").astype(jnp.int32)
     group = (lax.axis_index("tiles") >= 2).astype(jnp.int32)
-    place, place_other = jnp.stack([owner, group]), jnp.stack([owner, 1 - group])
+    place = jnp.stack([owner, group])
 
     def moment(array, index):
         return lax.dynamic_index_in_dim(array, index, 0, keepdims=False)
@@ -456,22 +478,22 @@
     target_out, target_sib = outward(target), sibling(target)
     slots, target_sib = lax.optimization_barrier((tile_list, target_sib))
     gathered = [slots] + [shifted(slots, k) for k in range(1, lax.axis_size("tiles"))]
-    g, kc, near, source = near_products(place, cells, masses, target, target_sib)
-    table = build_table(place, near, gathered)
+    g, kc, near, source, table = near_products(place, gathered, cells, masses, target, target_sib)
     later, fates, near = lax.optimization_barrier((embeddings, signatures, near))
     rest = jnp.concatenate([moment(later, 2 - group), fates])
     other_source = moment(later, 1 - group)
-    g, window = far_products(table, source, target_out, g, near)
-    part = sweep(table, window[0], kc, g)
+    g, window, part = far_products(table, source, target_out, g, near, kc)
     rest_out, rest_sib = outward(rest), sibling(rest)
 
-    totals, g_other = folded(
-        part, lambda message: other_products(message, other_source, rest, rest_sib, rest_out)
+    totals, (g_other, table_other) = folded(
+        part,
+        lambda message: other_products(
+            place, message, gathered, other_source, rest, rest_sib, rest_out
+        ),
     )
     hh = window[1] - LAM * totals
     part = sweep(table, hh, kc, g)
-    totals, table_other = folded(part, lambda message: build_table(place_other, message, gathered))
-    hh = window[1] - LAM * totals
+    hh = window[1] - LAM * folded(part)[0]
     couplings = (place, table, hh, g, table_other, mirrored(hh), g_other)
     late = late_fates(*couplings, rest, rest_sib, rest_out)
     late_out, late_sib = outward(late), sibling(late)

time: 82.5 us -> 89 us (1.079)
  waiting for transfers between devices: 11.8 us -> 32.8 us
  starting transfers between devices: 32.3 us -> 15.9 us
  Pallas kernels: 36.1 us -> 38.1 us
    ppermute x5, waiting for transfers between devices: 2.36 us -> 20 us  [outward(): return lax.ppermute(value, 'cells', pairs)]
    ppermute x5, starting transfers between devices: 27.4 us -> 9.95 us  [outward(): return lax.ppermute(value, 'cells', pairs)]
    ppermute x3, waiting for transfers between devices: 0.01 us -> 3.91 us  [shifted(): lax.ppermute(value, 'tiles', [(t, (t + steps) % count) for t in range(cou...]
    pallas_call x5 -> x3, Pallas kernels: 15.5 us -> 17.7 us  [the longest x1 6.14 us: other_products(): call(other_kernel, (G_SHAPE, TABLE_SHAPE), (VMEM, SMEM), in_specs)]
    pallas_call x2 -> x1, Pallas kernels: 6.55 us -> 4.52 us  [sweep(): call(sweep_kernel, PART_SHAPE, VMEM, [SMEM] + [VMEM] * 3, SWEEP_SCRATCH)]
    ppermute x7, starting transfers between devices: 0.43 us -> 1.48 us  [sibling(): lax.ppermute(value, 'cells', [(c, c ^ 1) for c in range(lax.axis_size('ce...]
  transfers between devices with their start and end apart: 16 -> 16, of which waited for: 6 -> 10; matrix products, arithmetic and copies ran while one was open for 0% -> 0% of each run, Pallas kernels for 28% -> 26%
where the time goes in v4:
time: 89 us; the launch traced here: 88.9 us
  Pallas kernels  38.1 us (43%)
  waiting for transfers between devices  32.8 us (37%)
  starting transfers between devices  15.9 us (18%)
  local copies, waits for them, and re-layouts  1.04 us (1%)
    ppermute x5, waiting for transfers between devices, outward(): return lax.ppermute(value, 'cells', pairs)  20 us
    ppermute x5, starting transfers between devices, outward(): return lax.ppermute(value, 'cells', pairs)  9.95 us
    pallas_call x1, Pallas kernels, late_fates(): call(late_kernel, FATE_SHAPE, VMEM, COUPLINGS + [VMEM] * 3, HOLD + [TERMS...  6.38 us
    pallas_call x1, Pallas kernels, other_products(): call(other_kernel, (G_SHAPE, TABLE_SHAPE), (VMEM, SMEM), in_specs)  6.14 us
    pallas_call x1, Pallas kernels, far_products(): call(far_kernel, outs, (VMEM,) * 3, [SMEM] + [VMEM] * 5, SWEEP_SCRATCH, {...  5.85 us
    pallas_call x1, Pallas kernels, near_products(): call(near_kernel, outs, (VMEM,) * 4 + (SMEM,), in_specs, scratch)  5.7 us
    ppermute x1, waiting for transfers between devices, mirrored(): lax.ppermute(value, 'tiles', [(t, count - 1 - t) for t in range(count)])  4.9 us
    pallas_call x1, Pallas kernels, sweep(): call(sweep_kernel, PART_SHAPE, VMEM, [SMEM] + [VMEM] * 3, SWEEP_SCRATCH)  4.52 us
  transfers between devices with their start and end apart: 16, of which 10 were waited for; matrix products, arithmetic and copies ran while one was open for 0% of the time, Pallas kernels for 26%

profile of v4, /device:TPU:0, one launch (start us, length us, event | category | flops | bytes accessed | tf_op | source)
XLA Modules:
  0.0 88.9 jit_solution(1423127417068070303)
XLA Ops:
  0.7 2.0 %shard_map.59.refs_6_ = bf16[1056,256]{1,0:T(8,128)(2,1)S(1)} custom-call(s32[2]{0:T(128)S(1)} %pad_add_fusion.place_ref, bf16[3,1024,256]{2,1,0:T(8,128)(2,1)} %refs_4_.1, f32[3,1024]{1,0:T(4,128)} %refs_5_.1), custom_call_target="tpu_custom_call" | custom-call | flops 3000000000 | bytes 10000 | tf_op jit(solution)/shard_map/pallas_call | solution.py:396
  2.7 0.1 collective-permute-start
  2.8 6.7 %collective-permute-start.4 = (bf16[1056,256]{1,0:T(8,128)(2,1)S(1)}, bf16[1056,256]{1,0:T(8,128)(2,1)S(1)}, u32[]{:S(2)}, u32[]{:S(2)}) collective-permute-start(bf16[1056,256]{1,0:T(8,128)(2,1)S(1)} %shard_map.59.refs_6_), channel_id=1, source_target_pairs={{0,124},{4,8},{8,4},{12,16},{16,12},{20,24},{24,20},{28,32},{32,28... | collective-permute-start | bytes 1622024 | tf_op jit(solution)/shard_map/ppermute | solution.py:40
  9.5 2.8 %collective-permute-start.3 = (s32[2,2,32]{2,1,0:T(2,128)S(1)}, s32[2,2,32]{2,1,0:T(2,128)S(1)}, u32[]{:S(2)}, u32[]{:S(2)}) collective-permute-start(s32[2,2,32]{2,1,0:T(2,128)S(1)} %copy-done.1), channel_id=1, source_target_pairs={{0,3},{1,0},{2,1},{3,2},{4,7},{5,4},{6,5},{7,6},{8,11},{9,8},{10,9... | collective-permute-start | bytes 1544 | tf_op jit(solution)/shard_map/ppermute | solution.py:463
  12.3 0.8 collective-permute-start.2
  13.1 0.9 collective-permute-start.1
  14.0 3.4 %collective-permute-done.2.refs_2_ = s32[2,2,32]{2,1,0:T(2,128)S(1)} collective-permute-done((s32[2,2,32]{2,1,0:T(2,128)S(1)}, s32[2,2,32]{2,1,0:T(2,128)S(1)}, u32[]{:S(2)}, u32[]{:S(2)}) %collective-permute-start.2) | collective-permute-done | bytes 544 | tf_op jit(solution)/shard_map/ppermute | solution.py:463
  17.4 0.5 collective-permute-done.1.refs_1_
  17.9 5.7 %shard_map.60 = (f32[24,1024,128]{2,1,0:T(8,128)S(1)}, f32[1024,128]{1,0:T(8,128)S(1)}, f32[2,16,128]{2,1,0:T(8,128)S(1)}, bf16[1024,256]{1,0:T(8,128)(2,1)S(1)}, s32[512]{0:T(512)S(1)}) custom-call(s32[2]{0:T(128)S(1)} %pad_add_fusion.place_ref, s32[2,2,32]{2,1,0:T(2,128)S(1)} %copy-done.1, s32[2,2,32]{2,1,0:T(2,128)S(1)} %collective-permute-done.1.refs_1_, ...), custom_call_target="tpu_custom_call" | custom-call | flops 3000000000 | bytes 10000 | tf_op jit(solution)/shard_map/pallas_call | solution.py:403
  23.7 0.9 %copy-done.3 = bf16[1024,256]{1,0:T(8,128)(2,1)S(1)} copy-done((bf16[1024,256]{1,0:T(8,128)(2,1)S(1)}, bf16[1024,256]{1,0:T(8,128)(2,1)}, u32[]{:S(2)}) %copy-start.3) | copy-done | bytes 524312
  24.7 0.1 collective-permute-start.8
  24.8 0.1 collective-permute-start.7
  24.9 5.8 %shard_map.61 = (f32[24,1024,128]{2,1,0:T(8,128)S(1)}, f32[2,24,128]{2,1,0:T(8,128)S(1)}, f32[2,24,128]{2,1,0:T(8,128)S(1)}) custom-call(s32[512]{0:T(512)S(1)} %get-tuple-element.24.table_ref, bf16[1024,256]{1,0:T(8,128)(2,1)S(1)} %get-tuple-element.25.source_ref, ...), custom_call_target="tpu_custom_call", output_to_operand_aliasing={{0}: (3, {})} | custom-call | flops 3000000000 | bytes 10000 | tf_op jit(solution)/shard_map/pallas_call | solution.py:408
  30.8 0.7 collective-permute-start.5
  31.5 0.8 collective-permute-done.5
  32.4 3.0 %collective-permute-start.6 = (f32[2,16,128]{2,1,0:T(8,128)S(1)}, f32[2,16,128]{2,1,0:T(8,128)S(1)}, u32[]{:S(2)}, u32[]{:S(2)}) collective-permute-start(f32[2,16,128]{2,1,0:T(8,128)S(1)} %pad_maximum_fusion.1.behind_ref), channel_id=1, source_target_pairs={{0,124},{4,8},{8,4},{12,16},{16,12},{20,24},{24,20},{28,32},{32,28... | collective-permute-start | bytes 49160 | tf_op jit(solution)/shard_map/ppermute | solution.py:40
  35.4 6.9 %collective-permute-done.8.refs_7_.out_ref = bf16[2048,256]{1,0:T(8,128)(2,1)S(1)} collective-permute-done((bf16[2048,256]{1,0:T(8,128)(2,1)S(1)}, bf16[2048,256]{1,0:T(8,128)(2,1)S(1)}, u32[]{:S(2)}, u32[]{:S(2)}) %collective-permute-start.8) | collective-permute-done | bytes 1048608 | tf_op jit(solution)/shard_map/ppermute | solution.py:40
  42.3 6.1 %shard_map.62 = (f32[24,1024,128]{2,1,0:T(8,128)S(1)}, s32[512]{0:T(512)S(1)}) custom-call(s32[2]{0:T(128)S(1)} %pad_add_fusion.place_ref, f32[2,16,128]{2,1,0:T(8,128)S(1)} %pad_maximum_fusion.1.behind_ref, s32[2,2,32]{2,1,0:T(2,128)S(1)} %copy-done.1, s32[2,2,32]{2,1,0:T(2,128)S(1)} %collective-permute-done.1.refs_1_, ...), custom_call_target="tpu_custom_call" | custom-call | flops 3000000000 | bytes 10000 | tf_op jit(solution)/shard_map/pallas_call | solution.py:417
  48.5 0.1 collective-permute-start.9
  48.6 1.2 %collective-permute-done.9 = f32[8,128]{1,0:T(8,128)S(1)} collective-permute-done((f32[8,128]{1,0:T(8,128)S(1)}, f32[8,128]{1,0:T(8,128)S(1)}, u32[]{:S(2)}, u32[]{:S(2)}) %collective-permute-start.9) | collective-permute-done | bytes 4128 | tf_op jit(solution)/shard_map/ppermute | solution.py:34
  49.8 4.5 %shard_map.63 = f32[2,24,128]{2,1,0:T(8,128)S(1)} custom-call(s32[512]{0:T(512)S(1)} %get-tuple-element.24.table_ref, f32[24,128]{1,0:T(8,128)S(1)} %fusion.hh_ref, f32[1024,128]{1,0:T(8,128)S(1)} %get-tuple-element.29.kc_ref, f32[24,1024,128]{2,1,0:T(8,128)S(1)} %get-tuple-element.37.g_ref), custom_call_target="tpu_custom_call" | custom-call | flops 3000000000 | bytes 10000 | tf_op jit(solution)/shard_map/pallas_call | solution.py:412
  54.3 0.4 collective-permute-start.10
  54.7 0.9 collective-permute-done.10
  55.6 0.1 collective-permute-start.11
  55.7 6.5 %collective-permute-done.11 = f32[2,16,128]{2,1,0:T(8,128)S(1)} collective-permute-done((f32[2,16,128]{2,1,0:T(8,128)S(1)}, f32[2,16,128]{2,1,0:T(8,128)S(1)}, u32[]{:S(2)}, u32[]{:S(2)}) %collective-permute-start.11) | collective-permute-done | bytes 16416 | tf_op jit(solution)/shard_map/ppermute | solution.py:40
  62.3 1.2 %collective-permute-done.12 = f32[8,128]{1,0:T(8,128)S(1)} collective-permute-done((f32[8,128]{1,0:T(8,128)S(1)}, f32[8,128]{1,0:T(8,128)S(1)}, u32[]{:S(2)}, u32[]{:S(2)}) %collective-permute-start.12) | collective-permute-done | bytes 4128 | tf_op jit(solution)/shard_map/ppermute | solution.py:34
  63.4 4.9 %collective-permute-done.13.hh2_ref = f32[24,128]{1,0:T(8,128)S(1)} collective-permute-done((f32[24,128]{1,0:T(8,128)S(1)}, f32[24,128]{1,0:T(8,128)S(1)}, u32[]{:S(2)}, u32[]{:S(2)}) %collective-permute-start.13) | collective-permute-done | bytes 12320 | tf_op jit(solution)/shard_map/ppermute | solution.py:45
  68.3 6.4 %shard_map.65.own_ref = bf16[1024,256]{1,0:T(8,128)(2,1)} custom-call(s32[2]{0:T(128)S(1)} %pad_add_fusion.place_ref, s32[512]{0:T(512)S(1)} %get-tuple-element.24.table_ref, f32[24,128]{1,0:T(8,128)S(1)} %fusion.1.hh_ref, f32[24,1024,128]{2,1,0:T(8,128)S(1)} %get-tuple-element.37.g_ref, s32[512]{0:T(512)S(1)} %get-tuple-element.38.table2_ref, ...), custom_call_target="tpu_custom_call" | custom-call | flops 3000000000 | bytes 10000 | tf_op jit(solution)/shard_map/pallas_call | solution.py:424
  74.8 3.7 %shard_map.64 = (bf16[1024,3200]{1,0:T(8,128)(2,1)S(1)}, f32[1024,128]{1,0:T(8,128)S(1)}) custom-call(s32[2]{0:T(128)S(1)} %pad_add_fusion.place_ref, s32[512]{0:T(512)S(1)} %get-tuple-element.24.table_ref, f32[24,128]{1,0:T(8,128)S(1)} %fusion.1.hh_ref, f32[24,1024,128]{2,1,0:T(8,128)S(1)} %get-tuple-element.37.g_ref, s32[512]{0:T(512)S(1)} %get-tuple-element.38.table2_ref, ...), custom_call_target="tpu_custom_call" | custom-call | flops 3000000000 | bytes 10000 | tf_op jit(solution)/shard_map/pallas_call | solution.py:428
  78.5 1.8 %shard_map.66.total_ref = f32[1024,256]{1,0:T(8,128)S(1)} custom-call(bf16[1024,3200]{1,0:T(8,128)(2,1)S(1)} %get-tuple-element.40.w_ref, bf16[1024,256]{1,0:T(8,128)(2,1)S(1)} %copy-done, bf16[1024,256]{1,0:T(8,128)(2,1)S(1)} %collective-permute-done.14.sib_ref), custom_call_target="tpu_custom_call" | custom-call | flops 3000000000 | bytes 10000 | tf_op jit(solution)/shard_map/pallas_call | solution.py:432
  80.3 6.6 %collective-permute-done.15.out_ref = bf16[1024,256]{1,0:T(8,128)(2,1)S(1)} collective-permute-done((bf16[1024,256]{1,0:T(8,128)(2,1)}, bf16[1024,256]{1,0:T(8,128)(2,1)S(1)}, u32[]{:S(2)}, u32[]{:S(2)}) %collective-permute-start.15) | collective-permute-done | bytes 524320 | tf_op jit(solution)/shard_map/ppermute | solution.py:40
  86.9 2.0 %shard_map.67 = bf16[1024,256]{1,0:T(8,128)(2,1)} custom-call(bf16[1024,3200]{1,0:T(8,128)(2,1)S(1)} %get-tuple-element.40.w_ref, f32[1024,128]{1,0:T(8,128)S(1)} %get-tuple-element.41.sum_ref, f32[1024,256]{1,0:T(8,128)S(1)} %shard_map.66.total_ref, bf16[1024,256]{1,0:T(8,128)(2,1)S(1)} %collective-permute-done.15.out_ref), custom_call_target="tpu_custom_call" | custom-call | flops 3000000000 | bytes 10000 | tf_op jit(solution)/shard_map/pallas_call | solution.py:436
  (30 shorter events, 0.5 us)
Async XLA Ops:
  0.7 8.8 %copy-start.1 = (s32[2,2,32]{2,1,0:T(2,128)S(1)}, s32[2,2,32]{2,1,0:T(2,128)}, u32[]{:S(2)}) copy-start(s32[2,2,32]{2,1,0:T(2,128)} %refs_0_.1) | copy-start | bytes 1540
  2.7 6.8 %collective-permute-start = (bf16[1056,256]{1,0:T(8,128)(2,1)S(1)}, bf16[1056,256]{1,0:T(8,128)(2,1)S(1)}, u32[]{:S(2)}, u32[]{:S(2)}) collective-permute-start(bf16[1056,256]{1,0:T(8,128)(2,1)S(1)} %shard_map.59.refs_6_), channel_id=1, source_target_pairs={{0,4},{4,0},{8,12},{12,8},{16,20},{20,16},{24,28},{28,24},{32,36},... | collective-permute-start | bytes 1622024 | tf_op jit(solution)/shard_map/ppermute | solution.py:34
  2.8 22.1 %collective-permute-start.4 = (bf16[1056,256]{1,0:T(8,128)(2,1)S(1)}, bf16[1056,256]{1,0:T(8,128)(2,1)S(1)}, u32[]{:S(2)}, u32[]{:S(2)}) collective-permute-start(bf16[1056,256]{1,0:T(8,128)(2,1)S(1)} %shard_map.59.refs_6_), channel_id=1, source_target_pairs={{0,124},{4,8},{8,4},{12,16},{16,12},{20,24},{24,20},{28,32},{32,28... | collective-permute-start | bytes 1622024 | tf_op jit(solution)/shard_map/ppermute | solution.py:40
  9.5 4.5 %collective-permute-start.3 = (s32[2,2,32]{2,1,0:T(2,128)S(1)}, s32[2,2,32]{2,1,0:T(2,128)S(1)}, u32[]{:S(2)}, u32[]{:S(2)}) collective-permute-start(s32[2,2,32]{2,1,0:T(2,128)S(1)} %copy-done.1), channel_id=1, source_target_pairs={{0,3},{1,0},{2,1},{3,2},{4,7},{5,4},{6,5},{7,6},{8,11},{9,8},{10,9... | collective-permute-start | bytes 1544 | tf_op jit(solution)/shard_map/ppermute | solution.py:463
  12.3 5.1 %collective-permute-start.2 = (s32[2,2,32]{2,1,0:T(2,128)S(1)}, s32[2,2,32]{2,1,0:T(2,128)S(1)}, u32[]{:S(2)}, u32[]{:S(2)}) collective-permute-start(s32[2,2,32]{2,1,0:T(2,128)S(1)} %copy-done.1), channel_id=1, source_target_pairs={{0,2},{1,3},{2,0},{3,1},{4,6},{5,7},{6,4},{7,5},{8,10},{9,11},{10,... | collective-permute-start | bytes 1544 | tf_op jit(solution)/shard_map/ppermute | solution.py:463
  13.1 4.8 %collective-permute-start.1 = (s32[2,2,32]{2,1,0:T(2,128)S(1)}, s32[2,2,32]{2,1,0:T(2,128)S(1)}, u32[]{:S(2)}, u32[]{:S(2)}) collective-permute-start(s32[2,2,32]{2,1,0:T(2,128)S(1)} %copy-done.1), channel_id=1, source_target_pairs={{0,1},{1,2},{2,3},{3,0},{4,5},{5,6},{6,7},{7,4},{8,9},{9,10},{10,1... | collective-permute-start | bytes 1544 | tf_op jit(solution)/shard_map/ppermute | solution.py:463
  14.0 9.6 %copy-start.2 = (bf16[3,1024,256]{2,1,0:T(8,128)(2,1)S(1)}, bf16[3,1024,256]{2,1,0:T(8,128)(2,1)}, u32[]{:S(2)}) copy-start(bf16[3,1024,256]{2,1,0:T(8,128)(2,1)} %refs_4_.1) | copy-start | bytes 4718596
  23.6 1.0 %copy-start.3 = (bf16[1024,256]{1,0:T(8,128)(2,1)S(1)}, bf16[1024,256]{1,0:T(8,128)(2,1)}, u32[]{:S(2)}) copy-start(bf16[1024,256]{1,0:T(8,128)(2,1)} %param.6) | copy-start | bytes 1572868
  24.7 17.6 %collective-permute-start.8 = (bf16[2048,256]{1,0:T(8,128)(2,1)S(1)}, bf16[2048,256]{1,0:T(8,128)(2,1)S(1)}, u32[]{:S(2)}, u32[]{:S(2)}) collective-permute-start(bf16[2048,256]{1,0:T(8,128)(2,1)S(1)} %pad_maximum_fusion.refs_5_.own_ref), channel_id=1, source_target_pairs={{0,124},{4,8},{8,4},{12,16},{16,12},{20,24},{24,20},{28,32},{32,28... | collective-permute-start | bytes 3145736 | tf_op jit(solution)/shard_map/ppermute | solution.py:40
  24.8 17.5 %collective-permute-start.7 = (bf16[2048,256]{1,0:T(8,128)(2,1)S(1)}, bf16[2048,256]{1,0:T(8,128)(2,1)S(1)}, u32[]{:S(2)}, u32[]{:S(2)}) collective-permute-start(bf16[2048,256]{1,0:T(8,128)(2,1)S(1)} %pad_maximum_fusion.refs_5_.own_ref), channel_id=1, source_target_pairs={{0,4},{4,0},{8,12},{12,8},{16,20},{20,16},{24,28},{28,24},{32,36},... | collective-permute-start | bytes 3145736 | tf_op jit(solution)/shard_map/ppermute | solution.py:34
  30.8 1.6 %collective-permute-start.5 = (f32[2,8,128]{2,1,0:T(8,128)S(1)}, f32[2,8,128]{2,1,0:T(8,128)S(1)}, u32[]{:S(2)}, u32[]{:S(2)}) collective-permute-start(f32[2,8,128]{2,1,0:T(8,128)S(1)} %get-tuple-element.54), channel_id=1, source_target_pairs={{0,4},{4,0},{8,12},{12,8},{16,20},{20,16},{24,28},{28,24},{32,36},... | collective-permute-start | bytes 24584 | tf_op jit(solution)/shard_map/ppermute | solution.py:34
  32.4 16.1 %collective-permute-start.6 = (f32[2,16,128]{2,1,0:T(8,128)S(1)}, f32[2,16,128]{2,1,0:T(8,128)S(1)}, u32[]{:S(2)}, u32[]{:S(2)}) collective-permute-start(f32[2,16,128]{2,1,0:T(8,128)S(1)} %pad_maximum_fusion.1.behind_ref), channel_id=1, source_target_pairs={{0,124},{4,8},{8,4},{12,16},{16,12},{20,24},{24,20},{28,32},{32,28... | collective-permute-start | bytes 49160 | tf_op jit(solution)/shard_map/ppermute | solution.py:40
  48.5 1.2 %collective-permute-start.9 = (f32[8,128]{1,0:T(8,128)S(1)}, f32[8,128]{1,0:T(8,128)S(1)}, u32[]{:S(2)}, u32[]{:S(2)}) collective-permute-start(f32[8,128]{1,0:T(8,128)S(1)} %get-tuple-element.50), channel_id=1, source_target_pairs={{0,4},{4,0},{8,12},{12,8},{16,20},{20,16},{24,28},{28,24},{32,36},... | collective-permute-start | bytes 12296 | tf_op jit(solution)/shard_map/ppermute | solution.py:34
  54.3 1.3 %collective-permute-start.10 = (f32[2,8,128]{2,1,0:T(8,128)S(1)}, f32[2,8,128]{2,1,0:T(8,128)S(1)}, u32[]{:S(2)}, u32[]{:S(2)}) collective-permute-start(f32[2,8,128]{2,1,0:T(8,128)S(1)} %get-tuple-element.52), channel_id=1, source_target_pairs={{0,4},{4,0},{8,12},{12,8},{16,20},{20,16},{24,28},{28,24},{32,36},... | collective-permute-start | bytes 24584 | tf_op jit(solution)/shard_map/ppermute | solution.py:34
  55.6 6.6 %collective-permute-start.11 = (f32[2,16,128]{2,1,0:T(8,128)S(1)}, f32[2,16,128]{2,1,0:T(8,128)S(1)}, u32[]{:S(2)}, u32[]{:S(2)}) collective-permute-start(f32[2,16,128]{2,1,0:T(8,128)S(1)} %pad_maximum_fusion.2), channel_id=1, source_target_pairs={{0,124},{4,8},{8,4},{12,16},{16,12},{20,24},{24,20},{28,32},{32,28... | collective-permute-start | bytes 49160 | tf_op jit(solution)/shard_map/ppermute | solution.py:40
  62.2 1.2 %collective-permute-start.12 = (f32[8,128]{1,0:T(8,128)S(1)}, f32[8,128]{1,0:T(8,128)S(1)}, u32[]{:S(2)}, u32[]{:S(2)}) collective-permute-start(f32[8,128]{1,0:T(8,128)S(1)} %get-tuple-element.48), channel_id=1, source_target_pairs={{0,4},{4,0},{8,12},{12,8},{16,20},{20,16},{24,28},{28,24},{32,36},... | collective-permute-start | bytes 12296 | tf_op jit(solution)/shard_map/ppermute | solution.py:34
  63.4 4.9 %collective-permute-start.13 = (f32[24,128]{1,0:T(8,128)S(1)}, f32[24,128]{1,0:T(8,128)S(1)}, u32[]{:S(2)}, u32[]{:S(2)}) collective-permute-start(f32[24,128]{1,0:T(8,128)S(1)} %fusion.1.hh_ref), channel_id=1, source_target_pairs={{0,3},{1,2},{2,1},{3,0},{4,7},{5,6},{6,5},{7,4},{8,11},{9,10},{10,... | collective-permute-start | bytes 36872 | tf_op jit(solution)/shard_map/ppermute | solution.py:45
  74.7 3.8 %copy-start = (bf16[1024,256]{1,0:T(8,128)(2,1)S(1)}, bf16[1024,256]{1,0:T(8,128)(2,1)}, u32[]{:S(2)}) copy-start(bf16[1024,256]{1,0:T(8,128)(2,1)} %shard_map.65.own_ref) | copy-start | bytes 1572868
  74.7 3.7 %collective-permute-start.14 = (bf16[1024,256]{1,0:T(8,128)(2,1)}, bf16[1024,256]{1,0:T(8,128)(2,1)S(1)}, u32[]{:S(2)}, u32[]{:S(2)}) collective-permute-start(bf16[1024,256]{1,0:T(8,128)(2,1)} %shard_map.65.own_ref), channel_id=1, source_target_pairs={{0,4},{4,0},{8,12},{12,8},{16,20},{20,16},{24,28},{28,24},{32,36},... | collective-permute-start | bytes 1572872 | tf_op jit(solution)/shard_map/ppermute | solution.py:34
  74.7 12.1 %collective-permute-start.15 = (bf16[1024,256]{1,0:T(8,128)(2,1)}, bf16[1024,256]{1,0:T(8,128)(2,1)S(1)}, u32[]{:S(2)}, u32[]{:S(2)}) collective-permute-start(bf16[1024,256]{1,0:T(8,128)(2,1)} %shard_map.65.own_ref), channel_id=1, source_target_pairs={{0,124},{4,8},{8,4},{12,16},{16,12},{20,24},{24,20},{28,32},{32,28... | collective-permute-start | bytes 1572872 | tf_op jit(solution)/shard_map/ppermute | solution.py:40

commit v5 on v4

--- a/solution.py
+++ b/solution.py
@@ -19,9 +19,10 @@
 SCALE = LOG2E / (EMB * EPS)
 
 QUAD = 4
-STRIDE = WIN + QUAD
-GROUPS = 384
-TABLE = 512
+STRIDE = 32
+GROUPS = NBLK * STRIDE
+UNREAD = GROUPS + NBLK
+TABLE = 384
 
 FLOPS, BYTES, MIB = 3 * 10**9, 10**4, 4
 VMEM = pl.BlockSpec(memory_space=pltpu.VMEM)
@@ -58,41 +59,42 @@
     )
 
 
-def start_table(table_ref):
-    for s in range(NBLK + 1):
-        table_ref[GROUPS + s] = 0
-
-
-def extend_table(place_ref, coupling, slot_refs, table_ref, step):
+def build_table(place_ref, coupling, slot_refs, table_ref):
     owner = place_ref[0]
-    share = slot_refs[0].shape[2] // 4
-    for index in range(share):
-        for slot_ref in slot_refs:
-            source = slot_ref[coupling, 0, step * share + index]
-            target = slot_ref[coupling, 1, step * share + index]
-            away = target >> 3
-            region = jnp.where(away == owner, 0, jnp.where(away == (owner ^ 1), NBLK, 2 * NBLK))
-            s = jnp.where(source < 0, NBLK, source & 7)
-            count = table_ref[GROUPS + s]
-            table_ref[GROUPS + s] = count + 1
-            table_ref[s * STRIDE + count] = region + (target & 7)
-
-
-def close_table(table_ref):
+    unroll = 4
+
+    def step(index, counts):
+        low, high = counts
+        for inner in range(unroll):
+            for slot_ref in slot_refs:
+                source = slot_ref[coupling, 0, index * unroll + inner]
+                target = slot_ref[coupling, 1, index * unroll + inner]
+                away = target >> 3
+                region = jnp.where(away == owner, 0, jnp.where(away == (owner ^ 1), NBLK, 2 * NBLK))
+                empty = source < 0
+                s = source & 7
+                shift = (s & 3) << 3
+                lower = s < 4
+                count = (jnp.where(lower, low, high) >> shift) & 255
+                table_ref[jnp.where(empty, UNREAD, s * STRIDE + count)] = region + (target & 7)
+                one = jnp.where(empty, 0, 1 << shift)
+                low, high = low + jnp.where(lower, one, 0), high + jnp.where(lower, 0, one)
+        return low, high
+
+    zero = jnp.int32(0)
+    counts = lax.fori_loop(0, slot_refs[0].shape[2] // unroll, step, (zero, zero))
     for s in range(NBLK):
-        count = table_ref[GROUPS + s]
+        count = (counts[s // 4] >> (8 * (s % 4))) & 255
         for extra in range(QUAD - 1):
             table_ref[s * STRIDE + count + extra] = WIN
         table_ref[GROUPS + s] = (count + QUAD - 1) >> 2
 
 
-def products(source_ref, target_refs, g_ref, first, beside=None):
+def products(source_ref, target_refs, g_ref, first):
     for region, target_ref in enumerate(target_refs, first):
 
         @pl.loop(0, NBLK // 2)
         def _(pair):
-            if beside is not None and region == first:
-                beside(pair)
             rows = target_ref[pl.ds(pl.multiple_of(pair * 256, 256), 256), :]
             g = lax.dot_general(
                 source_ref[...], rows, (((1,), (1,)), ((), ())), preferred_element_type=jnp.float32
@@ -293,16 +295,9 @@
         copy.start()
     unpack(own_ref, window_ref, 0)
     unpack(sib_ref, window_ref, 1)
+    build_table(place_ref, place_ref[1], slot_refs, table_ref)
     copies[0].wait()
-    start_table(table_ref)
-    products(
-        source_ref,
-        (own_ref, sib_ref),
-        g_ref,
-        0,
-        lambda step: extend_table(place_ref, place_ref[1], slot_refs, table_ref, step),
-    )
-    close_table(table_ref)
+    products(source_ref, (own_ref, sib_ref), g_ref, 0)
     copies[1].wait()
     masses = block_masses(mass_ref, group, 0)
     for s in range(NBLK):
@@ -320,18 +315,24 @@
     sweep_kernel(table_ref, window_ref.at[0], kc_ref, g_ref, part_ref, *scratch)
 
 
-def other_kernel(place_ref, behind_ref, *refs):
-    *slot_refs, source_ref, own_ref, sib_ref, out_ref, g_ref, table_ref = refs
+def other_kernel(behind_ref, source_ref, own_ref, sib_ref, out_ref, g_ref):
     del behind_ref
-    start_table(table_ref)
-    products(
-        source_ref,
-        [ref.at[:CELLS] for ref in (own_ref, sib_ref, out_ref)],
-        g_ref,
-        0,
-        lambda step: extend_table(place_ref, 1 - place_ref[1], slot_refs, table_ref, step),
-    )
-    close_table(table_ref)
+    products(source_ref, (own_ref, sib_ref, out_ref), g_ref, 0)
+
+
+def rest_kernel(place_ref, behind_ref, *refs):
+    del behind_ref
+    *slot_refs, cells_hbm, table_ref, source_ref, target_ref, sems = refs
+    group = place_ref[1]
+    copies = (
+        pltpu.make_async_copy(cells_hbm.at[2 - group], target_ref, sems.at[0]),
+        pltpu.make_async_copy(cells_hbm.at[1 - group], source_ref, sems.at[1]),
+    )
+    for copy in copies:
+        copy.start()
+    build_table(place_ref, 1 - group, slot_refs, table_ref)
+    for copy in copies:
+        copy.wait()
 
 
 def weigh_one(coupling, place_ref, mine, others, *outs):
@@ -346,7 +347,7 @@
 
 def late_kernel(place_ref, table_ref, hh_ref, g_ref, table2_ref, hh2_ref, g2_ref, own_ref, sib_ref, out_ref, late_ref, w_ref, sum_ref, terms_ref, m_ref):
     weigh_one(1, place_ref, (table_ref, hh_ref, g_ref), (table2_ref, hh2_ref, g2_ref), w_ref, sum_ref, terms_ref, m_ref)
-    fates = [ref.at[CELLS:] for ref in (own_ref, sib_ref, out_ref)]
+    fates = (own_ref, sib_ref, out_ref)
 
     @chunks
     def _(rows):
@@ -412,9 +413,15 @@
     return call(sweep_kernel, PART_SHAPE, VMEM, [SMEM] + [VMEM] * 3, SWEEP_SCRATCH)(*args)
 
 
-def other_products(place, behind, slots, *args):
-    in_specs = [SMEM, ANY] + [SMEM] * len(slots) + [VMEM] * 4
-    return call(other_kernel, (G_SHAPE, TABLE_SHAPE), (VMEM, SMEM), in_specs)(place, behind, *slots, *args)
+def other_products(*args):
+    return call(other_kernel, G_SHAPE, VMEM, [ANY] + [VMEM] * 4)(*args)
+
+
+def other_inputs(place, behind, slots, *args):
+    outs = (TABLE_SHAPE, FATE_SHAPE, FATE_SHAPE)
+    in_specs = [SMEM, ANY] + [SMEM] * len(slots) + [HBM]
+    scratch = [pltpu.SemaphoreType.DMA((2,))]
+    return call(rest_kernel, outs, (SMEM, VMEM, VMEM), in_specs, scratch)(place, behind, *slots, *args)
 
 
 COUPLINGS = [SMEM, SMEM, VMEM, VMEM, SMEM, VMEM, VMEM]
@@ -446,7 +453,7 @@
     )
 
 
-def folded(part, beside=lambda message: None):
+def folded(part, beside):
     own = merged(part[:, :NBLK], sibling(part[:, NBLK : 2 * NBLK]))
     beyond = part[:, 2 * NBLK :]
     message = jnp.concatenate([own, beyond], axis=1)
@@ -468,9 +475,6 @@
     group = (lax.axis_index("tiles") >= 2).astype(jnp.int32)
     place = jnp.stack([owner, group])
 
-    def moment(array, index):
-        return lax.dynamic_index_in_dim(array, index, 0, keepdims=False)
-
     cells, masses = (
         pltpu.with_memory_space_constraint(array, pltpu.HBM) for array in (embeddings, log_mass)
     )
@@ -479,23 +483,22 @@
     slots, target_sib = lax.optimization_barrier((tile_list, target_sib))
     gathered = [slots] + [shifted(slots, k) for k in range(1, lax.axis_size("tiles"))]
     g, kc, near, source, table = near_products(place, gathered, cells, masses, target, target_sib)
-    later, fates, near = lax.optimization_barrier((embeddings, signatures, near))
-    rest = jnp.concatenate([moment(later, 2 - group), fates])
-    other_source = moment(later, 1 - group)
     g, window, part = far_products(table, source, target_out, g, near, kc)
-    rest_out, rest_sib = outward(rest), sibling(rest)
-
-    totals, (g_other, table_other) = folded(
-        part,
-        lambda message: other_products(
-            place, message, gathered, other_source, rest, rest_sib, rest_out
-        ),
-    )
+
+    totals, (table_other, other_source, other) = folded(
+        part, lambda message: other_inputs(place, message, gathered, cells)
+    )
+    other_out, other_sib = outward(other), sibling(other)
+    fates, other = lax.optimization_barrier((signatures, other))
+    fates_out, fates_sib = outward(fates), sibling(fates)
     hh = window[1] - LAM * totals
     part = sweep(table, hh, kc, g)
-    hh = window[1] - LAM * folded(part)[0]
+    totals, g_other = folded(
+        part, lambda message: other_products(message, other_source, other, other_sib, other_out)
+    )
+    hh = window[1] - LAM * totals
     couplings = (place, table, hh, g, table_other, mirrored(hh), g_other)
-    late = late_fates(*couplings, rest, rest_sib, rest_out)
+    late = late_fates(*couplings, signatures, fates_sib, fates_out)
     late_out, late_sib = outward(late), sibling(late)
     weights, sums = early_weights(*couplings)
     total = early_near(weights, late, late_sib)

time: 89 us -> 83.4 us (0.937)
  waiting for transfers between devices: 32.8 us -> 18.7 us
  starting transfers between devices: 15.9 us -> 29.4 us
  Pallas kernels: 38.1 us -> 34 us
    ppermute x5 -> x6, starting transfers between devices: 9.95 us -> 22.6 us  [outward(): return lax.ppermute(value, 'cells', pairs)]
    ppermute x5 -> x6, waiting for transfers between devices: 20 us -> 7.97 us  [outward(): return lax.ppermute(value, 'cells', pairs)]
    pallas_call x1, Pallas kernels: 4.52 us -> 2.8 us  [sweep(): call(sweep_kernel, PART_SHAPE, VMEM, [SMEM] + [VMEM] * 3, SWEEP_SCRATCH)]
    pallas_call x1, Pallas kernels: 5.85 us -> 4.15 us  [far_products(): call(far_kernel, outs, (VMEM,) * 3, [SMEM] + [VMEM] * 5, SWEEP_SCRATCH, {...]
    ppermute x7 -> x8, waiting for transfers between devices: 3.99 us -> 2.33 us  [sibling(): lax.ppermute(value, 'cells', [(c, c ^ 1) for c in range(lax.axis_size('ce...]
    pallas_call x1, Pallas kernels: 3.67 us -> 2.56 us  [early_weights(): call(early_weights_kernel, (W_SHAPE, COLUMN_SHAPE), (VMEM, VMEM), COUPLIN...]
    pallas_call x1 -> x2, Pallas kernels: 6.14 us -> 6.51 us  [the longest x1 3.99 us: other_products(): return call(other_kernel, G_SHAPE, VMEM, [ANY] + [VMEM] * 4)(*args)]
  transfers between devices with their start and end apart: 16 -> 18, of which waited for: 10 -> 7; matrix products, arithmetic and copies ran while one was open for 0% -> 0% of each run, Pallas kernels for 26% -> 23%
where the time goes in v5:
time: 83.4 us; the launch traced here: 83.8 us
  Pallas kernels  34 us (41%)
  starting transfers between devices  29.4 us (35%)
  waiting for transfers between devices  18.7 us (22%)
    ppermute x6, starting transfers between devices, outward(): return lax.ppermute(value, 'cells', pairs)  22.6 us
    ppermute x6, waiting for transfers between devices, outward(): return lax.ppermute(value, 'cells', pairs)  7.97 us
    pallas_call x1, Pallas kernels, late_fates(): call(late_kernel, FATE_SHAPE, VMEM, COUPLINGS + [VMEM] * 3, HOLD + [TERMS...  6.88 us
    pallas_call x1, Pallas kernels, near_products(): call(near_kernel, outs, (VMEM,) * 4 + (SMEM,), in_specs, scratch)  5.21 us
    ppermute x3, starting transfers between devices, shifted(): lax.ppermute(value, 'tiles', [(t, (t + steps) % count) for t in range(cou...  4.44 us
    ppermute x1, waiting for transfers between devices, mirrored(): lax.ppermute(value, 'tiles', [(t, count - 1 - t) for t in range(count)])  4.24 us
    pallas_call x1, Pallas kernels, far_products(): call(far_kernel, outs, (VMEM,) * 3, [SMEM] + [VMEM] * 5, SWEEP_SCRATCH, {...  4.15 us
    ppermute x3, waiting for transfers between devices, shifted(): lax.ppermute(value, 'tiles', [(t, (t + steps) % count) for t in range(cou...  4.12 us
  transfers between devices with their start and end apart: 18, of which 7 were waited for; matrix products, arithmetic and copies ran while one was open for 0% of the time, Pallas kernels for 23%

profile of v5, /device:TPU:0, one launch (start us, length us, event | category | flops | bytes accessed | tf_op | source)
XLA Modules:
  0.0 83.8 jit_solution(186435082558938163)
XLA Ops:
  0.7 2.0 %shard_map.59.refs_6_ = bf16[1056,256]{1,0:T(8,128)(2,1)S(1)} custom-call(s32[2]{0:T(128)S(1)} %pad_add_fusion.place_ref, bf16[3,1024,256]{2,1,0:T(8,128)(2,1)} %refs_4_.3, f32[3,1024]{1,0:T(4,128)} %refs_5_.1), custom_call_target="tpu_custom_call" | custom-call | flops 3000000000 | bytes 10000 | tf_op jit(solution)/shard_map/pallas_call | solution.py:397
  2.7 0.1 collective-permute-start
  2.8 6.7 %collective-permute-start.4 = (bf16[1056,256]{1,0:T(8,128)(2,1)S(1)}, bf16[1056,256]{1,0:T(8,128)(2,1)S(1)}, u32[]{:S(2)}, u32[]{:S(2)}) collective-permute-start(bf16[1056,256]{1,0:T(8,128)(2,1)S(1)} %shard_map.59.refs_6_), channel_id=1, source_target_pairs={{0,124},{4,8},{8,4},{12,16},{16,12},{20,24},{24,20},{28,32},{32,28... | collective-permute-start | bytes 1622024 | tf_op jit(solution)/shard_map/ppermute | solution.py:41
  9.5 2.8 %collective-permute-start.3 = (s32[2,2,32]{2,1,0:T(2,128)}, s32[2,2,32]{2,1,0:T(2,128)S(1)}, u32[]{:S(2)}, u32[]{:S(2)}) collective-permute-start(s32[2,2,32]{2,1,0:T(2,128)} %refs_0_.1), channel_id=1, source_target_pairs={{0,3},{1,0},{2,1},{3,2},{4,7},{5,4},{6,5},{7,6},{8,11},{9,8},{10,9... | collective-permute-start | bytes 1544 | tf_op jit(solution)/shard_map/ppermute | solution.py:470
  12.3 0.8 collective-permute-start.2
  13.1 0.9 %collective-permute-start.1 = (s32[2,2,32]{2,1,0:T(2,128)}, s32[2,2,32]{2,1,0:T(2,128)S(1)}, u32[]{:S(2)}, u32[]{:S(2)}) collective-permute-start(s32[2,2,32]{2,1,0:T(2,128)} %refs_0_.1), channel_id=1, source_target_pairs={{0,1},{1,2},{2,3},{3,0},{4,5},{5,6},{6,7},{7,4},{8,9},{9,10},{10,1... | collective-permute-start | bytes 1544 | tf_op jit(solution)/shard_map/ppermute | solution.py:470
  14.0 3.6 %collective-permute-done.2.refs_2_ = s32[2,2,32]{2,1,0:T(2,128)S(1)} collective-permute-done((s32[2,2,32]{2,1,0:T(2,128)}, s32[2,2,32]{2,1,0:T(2,128)S(1)}, u32[]{:S(2)}, u32[]{:S(2)}) %collective-permute-start.2) | collective-permute-done | bytes 544 | tf_op jit(solution)/shard_map/ppermute | solution.py:470
  17.6 0.5 collective-permute-done.1.refs_1_
  18.1 0.7 copy-done.2
  18.8 5.2 %shard_map.60 = (f32[24,1024,128]{2,1,0:T(8,128)S(1)}, f32[1024,128]{1,0:T(8,128)S(1)}, f32[2,16,128]{2,1,0:T(8,128)S(1)}, bf16[1024,256]{1,0:T(8,128)(2,1)S(1)}, s32[384]{0:T(512)S(1)}) custom-call(s32[2]{0:T(128)S(1)} %pad_add_fusion.place_ref, s32[2,2,32]{2,1,0:T(2,128)S(1)} %copy-done.2, s32[2,2,32]{2,1,0:T(2,128)S(1)} %collective-permute-done.1.refs_1_, ...), custom_call_target="tpu_custom_call" | custom-call | flops 3000000000 | bytes 10000 | tf_op jit(solution)/shard_map/pallas_call | solution.py:404
  24.0 4.1 %shard_map.61 = (f32[24,1024,128]{2,1,0:T(8,128)S(1)}, f32[2,24,128]{2,1,0:T(8,128)S(1)}, f32[2,24,128]{2,1,0:T(8,128)S(1)}) custom-call(s32[384]{0:T(512)S(1)} %get-tuple-element.27.table_ref, bf16[1024,256]{1,0:T(8,128)(2,1)S(1)} %get-tuple-element.28.source_ref, ...), custom_call_target="tpu_custom_call", output_to_operand_aliasing={{0}: (3, {})} | custom-call | flops 3000000000 | bytes 10000 | tf_op jit(solution)/shard_map/pallas_call | solution.py:409
  28.2 0.1 collective-permute-start.5
  28.3 1.2 %collective-permute-done.5 = f32[2,8,128]{2,1,0:T(8,128)S(1)} collective-permute-done((f32[2,8,128]{2,1,0:T(8,128)S(1)}, f32[2,8,128]{2,1,0:T(8,128)S(1)}, u32[]{:S(2)}, u32[]{:S(2)}) %collective-permute-start.5) | collective-permute-done | bytes 8224 | tf_op jit(solution)/shard_map/ppermute | solution.py:35
  29.4 4.1 %collective-permute-start.6 = (f32[2,16,128]{2,1,0:T(8,128)S(1)}, f32[2,16,128]{2,1,0:T(8,128)S(1)}, u32[]{:S(2)}, u32[]{:S(2)}) collective-permute-start(f32[2,16,128]{2,1,0:T(8,128)S(1)} %pad_maximum_fusion.behind_ref), channel_id=1, source_target_pairs={{0,124},{4,8},{8,4},{12,16},{16,12},{20,24},{24,20},{28,32},{32,28... | collective-permute-start | bytes 49160 | tf_op jit(solution)/shard_map/ppermute | solution.py:41
  33.5 2.5 %shard_map.62 = (s32[384]{0:T(512)S(1)}, bf16[1024,256]{1,0:T(8,128)(2,1)S(1)}, bf16[1024,256]{1,0:T(8,128)(2,1)S(1)}) custom-call(s32[2]{0:T(128)S(1)} %pad_add_fusion.place_ref, f32[2,16,128]{2,1,0:T(8,128)S(1)} %pad_maximum_fusion.behind_ref, s32[2,2,32]{2,1,0:T(2,128)S(1)} %copy-done.3, s32[2,2,32]{2,1,0:T(2,128)S(1)} %collective-permute-done.1.refs_1_, ...), custom_call_target="tpu_custom_call" | custom-call | flops 3000000000 | bytes 10000 | tf_op jit(solution)/shard_map/pallas_call | solution.py:424
  36.1 0.1 collective-permute-start.7
  36.2 4.0 %collective-permute-start.11 = (bf16[1024,256]{1,0:T(8,128)(2,1)S(1)}, bf16[1024,256]{1,0:T(8,128)(2,1)S(1)}, u32[]{:S(2)}, u32[]{:S(2)}) collective-permute-start(bf16[1024,256]{1,0:T(8,128)(2,1)S(1)} %get-tuple-element.41.own_ref), channel_id=1, source_target_pairs={{0,124},{4,8},{8,4},{12,16},{16,12},{20,24},{24,20},{28,32},{32,28... | collective-permute-start | bytes 1572872 | tf_op jit(solution)/shard_map/ppermute | solution.py:41
  40.2 2.8 %shard_map.63 = f32[2,24,128]{2,1,0:T(8,128)S(1)} custom-call(s32[384]{0:T(512)S(1)} %get-tuple-element.27.table_ref, f32[24,128]{1,0:T(8,128)S(1)} %fusion.hh_ref, f32[1024,128]{1,0:T(8,128)S(1)} %get-tuple-element.31.kc_ref, f32[24,1024,128]{2,1,0:T(8,128)S(1)} %get-tuple-element.38.g_ref), custom_call_target="tpu_custom_call" | custom-call | flops 3000000000 | bytes 10000 | tf_op jit(solution)/shard_map/pallas_call | solution.py:413
  43.1 1.3 %collective-permute-start.8 = (f32[2,8,128]{2,1,0:T(8,128)S(1)}, f32[2,8,128]{2,1,0:T(8,128)S(1)}, u32[]{:S(2)}, u32[]{:S(2)}) collective-permute-start(f32[2,8,128]{2,1,0:T(8,128)S(1)} %get-tuple-element.56), channel_id=1, source_target_pairs={{0,4},{4,0},{8,12},{12,8},{16,20},{20,16},{24,28},{28,24},{32,36},... | collective-permute-start | bytes 24584 | tf_op jit(solution)/shard_map/ppermute | solution.py:35
  44.4 2.8 %collective-permute-start.15 = (bf16[1024,256]{1,0:T(8,128)(2,1)S(1)}, bf16[1024,256]{1,0:T(8,128)(2,1)S(1)}, u32[]{:S(2)}, u32[]{:S(2)}) collective-permute-start(bf16[1024,256]{1,0:T(8,128)(2,1)S(1)} %copy-done), channel_id=1, source_target_pairs={{0,124},{4,8},{8,4},{12,16},{16,12},{20,24},{24,20},{28,32},{32,28... | collective-permute-start | bytes 1572872 | tf_op jit(solution)/shard_map/ppermute | solution.py:41
  47.2 2.3 %collective-permute-start.9 = (f32[2,16,128]{2,1,0:T(8,128)S(1)}, f32[2,16,128]{2,1,0:T(8,128)S(1)}, u32[]{:S(2)}, u32[]{:S(2)}) collective-permute-start(f32[2,16,128]{2,1,0:T(8,128)S(1)} %pad_maximum_fusion.1.behind_ref), channel_id=1, source_target_pairs={{0,124},{4,8},{8,4},{12,16},{16,12},{20,24},{24,20},{28,32},{32,28... | collective-permute-start | bytes 49160 | tf_op jit(solution)/shard_map/ppermute | solution.py:41
  49.6 4.0 %shard_map.64.g2_ref = f32[24,1024,128]{2,1,0:T(8,128)S(1)} custom-call(f32[2,16,128]{2,1,0:T(8,128)S(1)} %pad_maximum_fusion.1.behind_ref, bf16[1024,256]{1,0:T(8,128)(2,1)S(1)} %get-tuple-element.39.source_ref, bf16[1024,256]{1,0:T(8,128)(2,1)S(1)} %get-tuple-element.41.own_ref, bf16[1024,256]{1,0:T(8,128)(2,1)S(1)} %collective-permute-done.10.sib_ref, ...), custom_call_target="tpu_custom_call" | custom-call | flops 3000000000 | bytes 10000 | tf_op jit(solution)/shard_map/pallas_call | solution.py:417
  53.6 2.9 %collective-permute-done.9 = f32[2,16,128]{2,1,0:T(8,128)S(1)} collective-permute-done((f32[2,16,128]{2,1,0:T(8,128)S(1)}, f32[2,16,128]{2,1,0:T(8,128)S(1)}, u32[]{:S(2)}, u32[]{:S(2)}) %collective-permute-start.9) | collective-permute-done | bytes 16416 | tf_op jit(solution)/shard_map/ppermute | solution.py:41
  56.6 1.2 %collective-permute-done.12 = f32[8,128]{1,0:T(8,128)S(1)} collective-permute-done((f32[8,128]{1,0:T(8,128)S(1)}, f32[8,128]{1,0:T(8,128)S(1)}, u32[]{:S(2)}, u32[]{:S(2)}) %collective-permute-start.12) | collective-permute-done | bytes 4128 | tf_op jit(solution)/shard_map/ppermute | solution.py:35
  57.8 0.7 collective-permute-start.13
  58.5 4.2 %collective-permute-done.13.hh2_ref = f32[24,128]{1,0:T(8,128)S(1)} collective-permute-done((f32[24,128]{1,0:T(8,128)S(1)}, f32[24,128]{1,0:T(8,128)S(1)}, u32[]{:S(2)}, u32[]{:S(2)}) %collective-permute-start.13) | collective-permute-done | bytes 12320 | tf_op jit(solution)/shard_map/ppermute | solution.py:46
  62.7 6.9 %shard_map.66.own_ref = bf16[1024,256]{1,0:T(8,128)(2,1)} custom-call(s32[2]{0:T(128)S(1)} %pad_add_fusion.place_ref, s32[384]{0:T(512)S(1)} %get-tuple-element.27.table_ref, f32[24,128]{1,0:T(8,128)S(1)} %fusion.1.hh_ref, f32[24,1024,128]{2,1,0:T(8,128)S(1)} %get-tuple-element.38.g_ref, s32[384]{0:T(512)S(1)} %get-tuple-element.43.table2_ref, ...), custom_call_target="tpu_custom_call" | custom-call | flops 3000000000 | bytes 10000 | tf_op jit(solution)/shard_map/pallas_call | solution.py:431
  69.6 2.7 %collective-permute-start.17 = (bf16[1024,256]{1,0:T(8,128)(2,1)}, bf16[1024,256]{1,0:T(8,128)(2,1)S(1)}, u32[]{:S(2)}, u32[]{:S(2)}) collective-permute-start(bf16[1024,256]{1,0:T(8,128)(2,1)} %shard_map.66.own_ref), channel_id=1, source_target_pairs={{0,124},{4,8},{8,4},{12,16},{16,12},{20,24},{24,20},{28,32},{32,28... | collective-permute-start | bytes 1572872 | tf_op jit(solution)/shard_map/ppermute | solution.py:41
  72.3 2.6 %shard_map.65 = (bf16[1024,3200]{1,0:T(8,128)(2,1)S(1)}, f32[1024,128]{1,0:T(8,128)S(1)}) custom-call(s32[2]{0:T(128)S(1)} %pad_add_fusion.place_ref, s32[384]{0:T(512)S(1)} %get-tuple-element.27.table_ref, f32[24,128]{1,0:T(8,128)S(1)} %fusion.1.hh_ref, f32[24,1024,128]{2,1,0:T(8,128)S(1)} %get-tuple-element.38.g_ref, s32[384]{0:T(512)S(1)} %get-tuple-element.43.table2_ref, ...), custom_call_target="tpu_custom_call" | custom-call | flops 3000000000 | bytes 10000 | tf_op jit(solution)/shard_map/pallas_call | solution.py:435
  74.9 1.8 %shard_map.67.total_ref = f32[1024,256]{1,0:T(8,128)S(1)} custom-call(bf16[1024,3200]{1,0:T(8,128)(2,1)S(1)} %get-tuple-element.45.w_ref, bf16[1024,256]{1,0:T(8,128)(2,1)S(1)} %copy-done.1, bf16[1024,256]{1,0:T(8,128)(2,1)S(1)} %collective-permute-done.16.sib_ref), custom_call_target="tpu_custom_call" | custom-call | flops 3000000000 | bytes 10000 | tf_op jit(solution)/shard_map/pallas_call | solution.py:439
  76.7 5.0 %collective-permute-done.17.out_ref = bf16[1024,256]{1,0:T(8,128)(2,1)S(1)} collective-permute-done((bf16[1024,256]{1,0:T(8,128)(2,1)}, bf16[1024,256]{1,0:T(8,128)(2,1)S(1)}, u32[]{:S(2)}, u32[]{:S(2)}) %collective-permute-start.17) | collective-permute-done | bytes 524320 | tf_op jit(solution)/shard_map/ppermute | solution.py:41
  81.7 2.0 %shard_map.68 = bf16[1024,256]{1,0:T(8,128)(2,1)} custom-call(bf16[1024,3200]{1,0:T(8,128)(2,1)S(1)} %get-tuple-element.45.w_ref, f32[1024,128]{1,0:T(8,128)S(1)} %get-tuple-element.46.sum_ref, f32[1024,256]{1,0:T(8,128)S(1)} %shard_map.67.total_ref, bf16[1024,256]{1,0:T(8,128)(2,1)S(1)} %collective-permute-done.17.out_ref), custom_call_target="tpu_custom_call" | custom-call | flops 3000000000 | bytes 10000 | tf_op jit(solution)/shard_map/pallas_call | solution.py:443
  (33 shorter events, 0.3 us)
Async XLA Ops:
  0.7 32.8 %copy-start.3 = (s32[2,2,32]{2,1,0:T(2,128)S(1)}, s32[2,2,32]{2,1,0:T(2,128)}, u32[]{:S(2)}) copy-start(s32[2,2,32]{2,1,0:T(2,128)} %refs_0_.1) | copy-start | bytes 1540
  2.7 6.8 %collective-permute-start = (bf16[1056,256]{1,0:T(8,128)(2,1)S(1)}, bf16[1056,256]{1,0:T(8,128)(2,1)S(1)}, u32[]{:S(2)}, u32[]{:S(2)}) collective-permute-start(bf16[1056,256]{1,0:T(8,128)(2,1)S(1)} %shard_map.59.refs_6_), channel_id=1, source_target_pairs={{0,4},{4,0},{8,12},{12,8},{16,20},{20,16},{24,28},{28,24},{32,36},... | collective-permute-start | bytes 1622024 | tf_op jit(solution)/shard_map/ppermute | solution.py:35
  2.8 21.1 %collective-permute-start.4 = (bf16[1056,256]{1,0:T(8,128)(2,1)S(1)}, bf16[1056,256]{1,0:T(8,128)(2,1)S(1)}, u32[]{:S(2)}, u32[]{:S(2)}) collective-permute-start(bf16[1056,256]{1,0:T(8,128)(2,1)S(1)} %shard_map.59.refs_6_), channel_id=1, source_target_pairs={{0,124},{4,8},{8,4},{12,16},{16,12},{20,24},{24,20},{28,32},{32,28... | collective-permute-start | bytes 1622024 | tf_op jit(solution)/shard_map/ppermute | solution.py:41
  9.5 4.4 %collective-permute-start.3 = (s32[2,2,32]{2,1,0:T(2,128)}, s32[2,2,32]{2,1,0:T(2,128)S(1)}, u32[]{:S(2)}, u32[]{:S(2)}) collective-permute-start(s32[2,2,32]{2,1,0:T(2,128)} %refs_0_.1), channel_id=1, source_target_pairs={{0,3},{1,0},{2,1},{3,2},{4,7},{5,4},{6,5},{7,6},{8,11},{9,8},{10,9... | collective-permute-start | bytes 1544 | tf_op jit(solution)/shard_map/ppermute | solution.py:470
  12.3 5.3 %collective-permute-start.2 = (s32[2,2,32]{2,1,0:T(2,128)}, s32[2,2,32]{2,1,0:T(2,128)S(1)}, u32[]{:S(2)}, u32[]{:S(2)}) collective-permute-start(s32[2,2,32]{2,1,0:T(2,128)} %refs_0_.1), channel_id=1, source_target_pairs={{0,2},{1,3},{2,0},{3,1},{4,6},{5,7},{6,4},{7,5},{8,10},{9,11},{10,... | collective-permute-start | bytes 1544 | tf_op jit(solution)/shard_map/ppermute | solution.py:470
  13.1 5.0 %collective-permute-start.1 = (s32[2,2,32]{2,1,0:T(2,128)}, s32[2,2,32]{2,1,0:T(2,128)S(1)}, u32[]{:S(2)}, u32[]{:S(2)}) collective-permute-start(s32[2,2,32]{2,1,0:T(2,128)} %refs_0_.1), channel_id=1, source_target_pairs={{0,1},{1,2},{2,3},{3,0},{4,5},{5,6},{6,7},{7,4},{8,9},{9,10},{10,1... | collective-permute-start | bytes 1544 | tf_op jit(solution)/shard_map/ppermute | solution.py:470
  18.1 0.7 copy-start.2
  28.1 16.3 %copy-start = (bf16[1024,256]{1,0:T(8,128)(2,1)S(1)}, bf16[1024,256]{1,0:T(8,128)(2,1)}, u32[]{:S(2)}) copy-start(bf16[1024,256]{1,0:T(8,128)(2,1)} %own_ref.1) | copy-start | bytes 1572868
  28.2 1.3 %collective-permute-start.5 = (f32[2,8,128]{2,1,0:T(8,128)S(1)}, f32[2,8,128]{2,1,0:T(8,128)S(1)}, u32[]{:S(2)}, u32[]{:S(2)}) collective-permute-start(f32[2,8,128]{2,1,0:T(8,128)S(1)} %get-tuple-element.58), channel_id=1, source_target_pairs={{0,4},{4,0},{8,12},{12,8},{16,20},{20,16},{24,28},{28,24},{32,36},... | collective-permute-start | bytes 24584 | tf_op jit(solution)/shard_map/ppermute | solution.py:35
  29.4 6.6 %collective-permute-start.6 = (f32[2,16,128]{2,1,0:T(8,128)S(1)}, f32[2,16,128]{2,1,0:T(8,128)S(1)}, u32[]{:S(2)}, u32[]{:S(2)}) collective-permute-start(f32[2,16,128]{2,1,0:T(8,128)S(1)} %pad_maximum_fusion.behind_ref), channel_id=1, source_target_pairs={{0,124},{4,8},{8,4},{12,16},{16,12},{20,24},{24,20},{28,32},{32,28... | collective-permute-start | bytes 49160 | tf_op jit(solution)/shard_map/ppermute | solution.py:41
  36.1 4.1 %collective-permute-start.7 = (f32[8,128]{1,0:T(8,128)S(1)}, f32[8,128]{1,0:T(8,128)S(1)}, u32[]{:S(2)}, u32[]{:S(2)}) collective-permute-start(f32[8,128]{1,0:T(8,128)S(1)} %get-tuple-element.54), channel_id=1, source_target_pairs={{0,4},{4,0},{8,12},{12,8},{16,20},{20,16},{24,28},{28,24},{32,36},... | collective-permute-start | bytes 12296 | tf_op jit(solution)/shard_map/ppermute | solution.py:35
  36.2 13.4 %collective-permute-start.11 = (bf16[1024,256]{1,0:T(8,128)(2,1)S(1)}, bf16[1024,256]{1,0:T(8,128)(2,1)S(1)}, u32[]{:S(2)}, u32[]{:S(2)}) collective-permute-start(bf16[1024,256]{1,0:T(8,128)(2,1)S(1)} %get-tuple-element.41.own_ref), channel_id=1, source_target_pairs={{0,124},{4,8},{8,4},{12,16},{16,12},{20,24},{24,20},{28,32},{32,28... | collective-permute-start | bytes 1572872 | tf_op jit(solution)/shard_map/ppermute | solution.py:41
  40.2 9.4 %collective-permute-start.10 = (bf16[1024,256]{1,0:T(8,128)(2,1)S(1)}, bf16[1024,256]{1,0:T(8,128)(2,1)S(1)}, u32[]{:S(2)}, u32[]{:S(2)}) collective-permute-start(bf16[1024,256]{1,0:T(8,128)(2,1)S(1)} %get-tuple-element.41.own_ref), channel_id=1, source_target_pairs={{0,4},{4,0},{8,12},{12,8},{16,20},{20,16},{24,28},{28,24},{32,36},... | collective-permute-start | bytes 1572872 | tf_op jit(solution)/shard_map/ppermute | solution.py:35
  43.1 4.2 %collective-permute-start.8 = (f32[2,8,128]{2,1,0:T(8,128)S(1)}, f32[2,8,128]{2,1,0:T(8,128)S(1)}, u32[]{:S(2)}, u32[]{:S(2)}) collective-permute-start(f32[2,8,128]{2,1,0:T(8,128)S(1)} %get-tuple-element.56), channel_id=1, source_target_pairs={{0,4},{4,0},{8,12},{12,8},{16,20},{20,16},{24,28},{28,24},{32,36},... | collective-permute-start | bytes 24584 | tf_op jit(solution)/shard_map/ppermute | solution.py:35
  44.4 14.0 %collective-permute-start.15 = (bf16[1024,256]{1,0:T(8,128)(2,1)S(1)}, bf16[1024,256]{1,0:T(8,128)(2,1)S(1)}, u32[]{:S(2)}, u32[]{:S(2)}) collective-permute-start(bf16[1024,256]{1,0:T(8,128)(2,1)S(1)} %copy-done), channel_id=1, source_target_pairs={{0,124},{4,8},{8,4},{12,16},{16,12},{20,24},{24,20},{28,32},{32,28... | collective-permute-start | bytes 1572872 | tf_op jit(solution)/shard_map/ppermute | solution.py:41
  47.2 11.2 %collective-permute-start.14 = (bf16[1024,256]{1,0:T(8,128)(2,1)S(1)}, bf16[1024,256]{1,0:T(8,128)(2,1)S(1)}, u32[]{:S(2)}, u32[]{:S(2)}) collective-permute-start(bf16[1024,256]{1,0:T(8,128)(2,1)S(1)} %copy-done), channel_id=1, source_target_pairs={{0,4},{4,0},{8,12},{12,8},{16,20},{20,16},{24,28},{28,24},{32,36},... | collective-permute-start | bytes 1572872 | tf_op jit(solution)/shard_map/ppermute | solution.py:35
  47.2 9.3 %collective-permute-start.9 = (f32[2,16,128]{2,1,0:T(8,128)S(1)}, f32[2,16,128]{2,1,0:T(8,128)S(1)}, u32[]{:S(2)}, u32[]{:S(2)}) collective-permute-start(f32[2,16,128]{2,1,0:T(8,128)S(1)} %pad_maximum_fusion.1.behind_ref), channel_id=1, source_target_pairs={{0,124},{4,8},{8,4},{12,16},{16,12},{20,24},{24,20},{28,32},{32,28... | collective-permute-start | bytes 49160 | tf_op jit(solution)/shard_map/ppermute | solution.py:41
  56.5 1.2 %collective-permute-start.12 = (f32[8,128]{1,0:T(8,128)S(1)}, f32[8,128]{1,0:T(8,128)S(1)}, u32[]{:S(2)}, u32[]{:S(2)}) collective-permute-start(f32[8,128]{1,0:T(8,128)S(1)} %get-tuple-element.52), channel_id=1, source_target_pairs={{0,4},{4,0},{8,12},{12,8},{16,20},{20,16},{24,28},{28,24},{32,36},... | collective-permute-start | bytes 12296 | tf_op jit(solution)/shard_map/ppermute | solution.py:35
  57.8 4.9 %collective-permute-start.13 = (f32[24,128]{1,0:T(8,128)S(1)}, f32[24,128]{1,0:T(8,128)S(1)}, u32[]{:S(2)}, u32[]{:S(2)}) collective-permute-start(f32[24,128]{1,0:T(8,128)S(1)} %fusion.1.hh_ref), channel_id=1, source_target_pairs={{0,3},{1,2},{2,1},{3,0},{4,7},{5,6},{6,5},{7,4},{8,11},{9,10},{10,... | collective-permute-start | bytes 36872 | tf_op jit(solution)/shard_map/ppermute | solution.py:46
  69.6 5.3 %copy-start.1 = (bf16[1024,256]{1,0:T(8,128)(2,1)S(1)}, bf16[1024,256]{1,0:T(8,128)(2,1)}, u32[]{:S(2)}) copy-start(bf16[1024,256]{1,0:T(8,128)(2,1)} %shard_map.66.own_ref) | copy-start | bytes 1572868
  69.6 5.3 %collective-permute-start.16 = (bf16[1024,256]{1,0:T(8,128)(2,1)}, bf16[1024,256]{1,0:T(8,128)(2,1)S(1)}, u32[]{:S(2)}, u32[]{:S(2)}) collective-permute-start(bf16[1024,256]{1,0:T(8,128)(2,1)} %shard_map.66.own_ref), channel_id=1, source_target_pairs={{0,4},{4,0},{8,12},{12,8},{16,20},{20,16},{24,28},{28,24},{32,36},... | collective-permute-start | bytes 1572872 | tf_op jit(solution)/shard_map/ppermute | solution.py:35
  69.6 12.1 %collective-permute-start.17 = (bf16[1024,256]{1,0:T(8,128)(2,1)}, bf16[1024,256]{1,0:T(8,128)(2,1)S(1)}, u32[]{:S(2)}, u32[]{:S(2)}) collective-permute-start(bf16[1024,256]{1,0:T(8,128)(2,1)} %shard_map.66.own_ref), channel_id=1, source_target_pairs={{0,124},{4,8},{8,4},{12,16},{16,12},{20,24},{24,20},{28,32},{32,28... | collective-permute-start | bytes 1572872 | tf_op jit(solution)/shard_map/ppermute | solution.py:41

commit v6 on v5

--- a/solution.py
+++ b/solution.py
@@ -320,8 +320,8 @@
     products(source_ref, (own_ref, sib_ref, out_ref), g_ref, 0)
 
 
-def rest_kernel(place_ref, behind_ref, *refs):
-    del behind_ref
+def rest_kernel(place_ref, behind_ref, arrived_ref, *refs):
+    del behind_ref, arrived_ref
     *slot_refs, cells_hbm, table_ref, source_ref, target_ref, sems = refs
     group = place_ref[1]
     copies = (
@@ -417,11 +417,11 @@
     return call(other_kernel, G_SHAPE, VMEM, [ANY] + [VMEM] * 4)(*args)
 
 
-def other_inputs(place, behind, slots, *args):
+def other_inputs(place, behind, arrived, slots, *args):
     outs = (TABLE_SHAPE, FATE_SHAPE, FATE_SHAPE)
-    in_specs = [SMEM, ANY] + [SMEM] * len(slots) + [HBM]
+    in_specs = [SMEM, ANY, ANY] + [SMEM] * len(slots) + [HBM]
     scratch = [pltpu.SemaphoreType.DMA((2,))]
-    return call(rest_kernel, outs, (SMEM, VMEM, VMEM), in_specs, scratch)(place, behind, *slots, *args)
+    return call(rest_kernel, outs, (SMEM, VMEM, VMEM), in_specs, scratch)(place, behind, arrived, *slots, *args)
 
 
 COUPLINGS = [SMEM, SMEM, VMEM, VMEM, SMEM, VMEM, VMEM]
@@ -480,17 +480,16 @@
     )
     target = target_message(place, cells, masses)
     target_out, target_sib = outward(target), sibling(target)
-    slots, target_sib = lax.optimization_barrier((tile_list, target_sib))
-    gathered = [slots] + [shifted(slots, k) for k in range(1, lax.axis_size("tiles"))]
+    slots, fates, target_sib = lax.optimization_barrier((tile_list, signatures, target_sib))
+    fates_out, fates_sib = outward(fates), sibling(fates)
+    gathered = [pltpu.with_memory_space_constraint(tile_list, pltpu.HBM)] + [shifted(slots, k) for k in range(1, lax.axis_size("tiles"))]
     g, kc, near, source, table = near_products(place, gathered, cells, masses, target, target_sib)
     g, window, part = far_products(table, source, target_out, g, near, kc)
 
     totals, (table_other, other_source, other) = folded(
-        part, lambda message: other_inputs(place, message, gathered, cells)
+        part, lambda message: other_inputs(place, message, fates_out, gathered, cells)
     )
     other_out, other_sib = outward(other), sibling(other)
-    fates, other = lax.optimization_barrier((signatures, other))
-    fates_out, fates_sib = outward(fates), sibling(fates)
     hh = window[1] - LAM * totals
     part = sweep(table, hh, kc, g)
     totals, g_other = folded(

time: 83.4 us -> 80 us (0.959); the launches traced: 83.8 us -> 79.1 us
  starting transfers between devices: 29.4 us -> 23.4 us
  Pallas kernels: 34 us -> 36.9 us
  waiting for transfers between devices: 18.7 us -> 17.8 us
    ppermute x6, starting transfers between devices: 22.6 us -> 18 us  [outward(): return lax.ppermute(value, 'cells', pairs)]
    pallas_call x1, Pallas kernels: 2.8 us -> 4.33 us  [sweep(): call(sweep_kernel, PART_SHAPE, VMEM, [SMEM] + [VMEM] * 3, SWEEP_SCRATCH)]
    pallas_call x1, Pallas kernels: 4.15 us -> 5.67 us  [far_products(): call(far_kernel, outs, (VMEM,) * 3, [SMEM] + [VMEM] * 5, SWEEP_SCRATCH, {...]
    ppermute x6, waiting for transfers between devices: 7.97 us -> 6.51 us  [outward(): return lax.ppermute(value, 'cells', pairs)]
    pallas_call x1, Pallas kernels: 6.88 us -> 5.64 us  [late_fates(): call(late_kernel, FATE_SHAPE, VMEM, COUPLINGS + [VMEM] * 3, HOLD + [TERMS...]
    pallas_call x1, Pallas kernels: 2.56 us -> 3.53 us  [early_weights(): call(early_weights_kernel, (W_SHAPE, COLUMN_SHAPE), (VMEM, VMEM), COUPLIN...]
  transfers between devices with their start and end apart: 18 -> 18, of which waited for: 7 -> 9; matrix products, arithmetic and copies ran while one was open for 0% -> 0% of each run, Pallas kernels for 23% -> 34%
where the time goes in v6:
time: 80 us; the launch traced here: 79.1 us
  Pallas kernels  36.9 us (46%)
  starting transfers between devices  23.4 us (29%)
  waiting for transfers between devices  17.8 us (22%)
  between operations  0.85 us (1%)
    ppermute x6, starting transfers between devices, outward(): return lax.ppermute(value, 'cells', pairs)  18 us
    ppermute x6, waiting for transfers between devices, outward(): return lax.ppermute(value, 'cells', pairs)  6.51 us
    pallas_call x1, Pallas kernels, far_products(): call(far_kernel, outs, (VMEM,) * 3, [SMEM] + [VMEM] * 5, SWEEP_SCRATCH, {...  5.67 us
    pallas_call x1, Pallas kernels, late_fates(): call(late_kernel, FATE_SHAPE, VMEM, COUPLINGS + [VMEM] * 3, HOLD + [TERMS...  5.64 us
    pallas_call x1, Pallas kernels, near_products(): call(near_kernel, outs, (VMEM,) * 4 + (SMEM,), in_specs, scratch)  5.29 us
    ppermute x1, waiting for transfers between devices, mirrored(): lax.ppermute(value, 'tiles', [(t, count - 1 - t) for t in range(count)])  4.89 us
    ppermute x3, starting transfers between devices, shifted(): lax.ppermute(value, 'tiles', [(t, (t + steps) % count) for t in range(cou...  4.44 us
    pallas_call x1, Pallas kernels, sweep(): call(sweep_kernel, PART_SHAPE, VMEM, [SMEM] + [VMEM] * 3, SWEEP_SCRATCH)  4.33 us
  transfers between devices with their start and end apart: 18, of which 9 were waited for; matrix products, arithmetic and copies ran while one was open for 0% of the time, Pallas kernels for 34%

profile of v6, /device:TPU:0, one launch (start us, length us, event | category | flops | bytes accessed | tf_op | source)
XLA Modules:
  0.0 79.1 jit_solution(3866154860319879219)
XLA Ops:
  0.7 2.0 %shard_map.59.refs_6_ = bf16[1056,256]{1,0:T(8,128)(2,1)S(1)} custom-call(s32[2]{0:T(128)S(1)} %pad_add_fusion.place_ref, bf16[3,1024,256]{2,1,0:T(8,128)(2,1)} %refs_4_.3, f32[3,1024]{1,0:T(4,128)} %refs_5_.1), custom_call_target="tpu_custom_call" | custom-call | flops 3000000000 | bytes 10000 | tf_op jit(solution)/shard_map/pallas_call | solution.py:397
  2.7 0.1 collective-permute-start
  2.8 6.7 %collective-permute-start.4 = (bf16[1056,256]{1,0:T(8,128)(2,1)S(1)}, bf16[1056,256]{1,0:T(8,128)(2,1)S(1)}, u32[]{:S(2)}, u32[]{:S(2)}) collective-permute-start(bf16[1056,256]{1,0:T(8,128)(2,1)S(1)} %shard_map.59.refs_6_), channel_id=1, source_target_pairs={{0,124},{4,8},{8,4},{12,16},{16,12},{20,24},{24,20},{28,32},{32,28... | collective-permute-start | bytes 1622024 | tf_op jit(solution)/shard_map/ppermute | solution.py:41
  9.5 2.8 %collective-permute-start.3 = (s32[2,2,32]{2,1,0:T(2,128)}, s32[2,2,32]{2,1,0:T(2,128)S(1)}, u32[]{:S(2)}, u32[]{:S(2)}) collective-permute-start(s32[2,2,32]{2,1,0:T(2,128)} %refs_0_.3), channel_id=1, source_target_pairs={{0,3},{1,0},{2,1},{3,2},{4,7},{5,4},{6,5},{7,6},{8,11},{9,8},{10,9... | collective-permute-start | bytes 1544 | tf_op jit(solution)/shard_map/ppermute | solution.py:470
  12.3 0.8 %collective-permute-start.2 = (s32[2,2,32]{2,1,0:T(2,128)}, s32[2,2,32]{2,1,0:T(2,128)S(1)}, u32[]{:S(2)}, u32[]{:S(2)}) collective-permute-start(s32[2,2,32]{2,1,0:T(2,128)} %refs_0_.3), channel_id=1, source_target_pairs={{0,2},{1,3},{2,0},{3,1},{4,6},{5,7},{6,4},{7,5},{8,10},{9,11},{10,... | collective-permute-start | bytes 1544 | tf_op jit(solution)/shard_map/ppermute | solution.py:470
  13.1 0.9 %collective-permute-start.1 = (s32[2,2,32]{2,1,0:T(2,128)}, s32[2,2,32]{2,1,0:T(2,128)S(1)}, u32[]{:S(2)}, u32[]{:S(2)}) collective-permute-start(s32[2,2,32]{2,1,0:T(2,128)} %refs_0_.3), channel_id=1, source_target_pairs={{0,1},{1,2},{2,3},{3,0},{4,5},{5,6},{6,7},{7,4},{8,9},{9,10},{10,1... | collective-permute-start | bytes 1544 | tf_op jit(solution)/shard_map/ppermute | solution.py:470
  14.0 0.7 collective-permute-start.7
  14.7 2.9 %collective-permute-done.2.refs_2_ = s32[2,2,32]{2,1,0:T(2,128)S(1)} collective-permute-done((s32[2,2,32]{2,1,0:T(2,128)}, s32[2,2,32]{2,1,0:T(2,128)S(1)}, u32[]{:S(2)}, u32[]{:S(2)}) %collective-permute-start.2) | collective-permute-done | bytes 544 | tf_op jit(solution)/shard_map/ppermute | solution.py:470
  17.6 0.5 collective-permute-done.1.refs_1_
  18.1 5.3 %shard_map.60 = (f32[24,1024,128]{2,1,0:T(8,128)S(1)}, f32[1024,128]{1,0:T(8,128)S(1)}, f32[2,16,128]{2,1,0:T(8,128)S(1)}, bf16[1024,256]{1,0:T(8,128)(2,1)S(1)}, s32[384]{0:T(512)S(1)}) custom-call(s32[2]{0:T(128)S(1)} %pad_add_fusion.place_ref, s32[2,2,32]{2,1,0:T(2,128)} %refs_0_.3, s32[2,2,32]{2,1,0:T(2,128)S(1)} %collective-permute-done.1.refs_1_, ...), custom_call_target="tpu_custom_call" | custom-call | flops 3000000000 | bytes 10000 | tf_op jit(solution)/shard_map/pallas_call | solution.py:404
  23.4 5.7 %shard_map.61 = (f32[24,1024,128]{2,1,0:T(8,128)S(1)}, f32[2,24,128]{2,1,0:T(8,128)S(1)}, f32[2,24,128]{2,1,0:T(8,128)S(1)}) custom-call(s32[384]{0:T(512)S(1)} %get-tuple-element.26.table_ref, bf16[1024,256]{1,0:T(8,128)(2,1)S(1)} %get-tuple-element.27.source_ref, ...), custom_call_target="tpu_custom_call", output_to_operand_aliasing={{0}: (3, {})} | custom-call | flops 3000000000 | bytes 10000 | tf_op jit(solution)/shard_map/pallas_call | solution.py:409
  29.1 0.1 collective-permute-start.5
  29.2 1.2 %collective-permute-done.5 = f32[2,8,128]{2,1,0:T(8,128)S(1)} collective-permute-done((f32[2,8,128]{2,1,0:T(8,128)S(1)}, f32[2,8,128]{2,1,0:T(8,128)S(1)}, u32[]{:S(2)}, u32[]{:S(2)}) %collective-permute-start.5) | collective-permute-done | bytes 8224 | tf_op jit(solution)/shard_map/ppermute | solution.py:35
  30.4 2.0 %collective-permute-start.6 = (f32[2,16,128]{2,1,0:T(8,128)S(1)}, f32[2,16,128]{2,1,0:T(8,128)S(1)}, u32[]{:S(2)}, u32[]{:S(2)}) collective-permute-start(f32[2,16,128]{2,1,0:T(8,128)S(1)} %pad_maximum_fusion.behind_ref), channel_id=1, source_target_pairs={{0,124},{4,8},{8,4},{12,16},{16,12},{20,24},{24,20},{28,32},{32,28... | collective-permute-start | bytes 49160 | tf_op jit(solution)/shard_map/ppermute | solution.py:41
  32.3 2.6 %shard_map.62 = (s32[384]{0:T(512)S(1)}, bf16[1024,256]{1,0:T(8,128)(2,1)S(1)}, bf16[1024,256]{1,0:T(8,128)(2,1)S(1)}) custom-call(s32[2]{0:T(128)S(1)} %pad_add_fusion.place_ref, f32[2,16,128]{2,1,0:T(8,128)S(1)} %pad_maximum_fusion.behind_ref, bf16[1024,256]{1,0:T(8,128)(2,1)S(1)} %collective-permute-done.7.arrived_ref.out_ref, s32[2,2,32]{2,1,0:T(2,128)} %refs_0_.3, ...), custom_call_target="tpu_custom_call" | custom-call | flops 3000000000 | bytes 10000 | tf_op jit(solution)/shard_map/pallas_call | solution.py:424
  34.9 2.0 %collective-permute-done.6 = f32[2,16,128]{2,1,0:T(8,128)S(1)} collective-permute-done((f32[2,16,128]{2,1,0:T(8,128)S(1)}, f32[2,16,128]{2,1,0:T(8,128)S(1)}, u32[]{:S(2)}, u32[]{:S(2)}) %collective-permute-start.6) | collective-permute-done | bytes 16416 | tf_op jit(solution)/shard_map/ppermute | solution.py:41
  37.0 2.0 %collective-permute-start.12 = (bf16[1024,256]{1,0:T(8,128)(2,1)S(1)}, bf16[1024,256]{1,0:T(8,128)(2,1)S(1)}, u32[]{:S(2)}, u32[]{:S(2)}) collective-permute-start(bf16[1024,256]{1,0:T(8,128)(2,1)S(1)} %get-tuple-element.40.own_ref), channel_id=1, source_target_pairs={{0,124},{4,8},{8,4},{12,16},{16,12},{20,24},{24,20},{28,32},{32,28... | collective-permute-start | bytes 1572872 | tf_op jit(solution)/shard_map/ppermute | solution.py:41
  39.0 4.3 %shard_map.63 = f32[2,24,128]{2,1,0:T(8,128)S(1)} custom-call(s32[384]{0:T(512)S(1)} %get-tuple-element.26.table_ref, f32[24,128]{1,0:T(8,128)S(1)} %fusion.hh_ref, f32[1024,128]{1,0:T(8,128)S(1)} %get-tuple-element.30.kc_ref, f32[24,1024,128]{2,1,0:T(8,128)S(1)} %get-tuple-element.38.g_ref), custom_call_target="tpu_custom_call" | custom-call | flops 3000000000 | bytes 10000 | tf_op jit(solution)/shard_map/pallas_call | solution.py:413
  43.4 0.1 collective-permute-start.9
  43.5 0.5 collective-permute-start.15
  44.0 0.7 collective-permute-done.9
  44.7 3.7 %collective-permute-start.10 = (f32[2,16,128]{2,1,0:T(8,128)S(1)}, f32[2,16,128]{2,1,0:T(8,128)S(1)}, u32[]{:S(2)}, u32[]{:S(2)}) collective-permute-start(f32[2,16,128]{2,1,0:T(8,128)S(1)} %pad_maximum_fusion.1.behind_ref), channel_id=1, source_target_pairs={{0,124},{4,8},{8,4},{12,16},{16,12},{20,24},{24,20},{28,32},{32,28... | collective-permute-start | bytes 49160 | tf_op jit(solution)/shard_map/ppermute | solution.py:41
  48.4 0.7 collective-permute-done.12.out_ref
  49.1 4.0 %shard_map.64.g2_ref = f32[24,1024,128]{2,1,0:T(8,128)S(1)} custom-call(f32[2,16,128]{2,1,0:T(8,128)S(1)} %pad_maximum_fusion.1.behind_ref, bf16[1024,256]{1,0:T(8,128)(2,1)S(1)} %get-tuple-element.39.source_ref, bf16[1024,256]{1,0:T(8,128)(2,1)S(1)} %get-tuple-element.40.own_ref, bf16[1024,256]{1,0:T(8,128)(2,1)S(1)} %collective-permute-done.11.sib_ref, ...), custom_call_target="tpu_custom_call" | custom-call | flops 3000000000 | bytes 10000 | tf_op jit(solution)/shard_map/pallas_call | solution.py:417
  53.2 1.2 %collective-permute-done.13 = f32[8,128]{1,0:T(8,128)S(1)} collective-permute-done((f32[8,128]{1,0:T(8,128)S(1)}, f32[8,128]{1,0:T(8,128)S(1)}, u32[]{:S(2)}, u32[]{:S(2)}) %collective-permute-start.13) | collective-permute-done | bytes 4128 | tf_op jit(solution)/shard_map/ppermute | solution.py:35
  54.4 4.9 %collective-permute-done.14.hh2_ref = f32[24,128]{1,0:T(8,128)S(1)} collective-permute-done((f32[24,128]{1,0:T(8,128)S(1)}, f32[24,128]{1,0:T(8,128)S(1)}, u32[]{:S(2)}, u32[]{:S(2)}) %collective-permute-start.14) | collective-permute-done | bytes 12320 | tf_op jit(solution)/shard_map/ppermute | solution.py:46
  59.2 5.6 %shard_map.66.own_ref = bf16[1024,256]{1,0:T(8,128)(2,1)} custom-call(s32[2]{0:T(128)S(1)} %pad_add_fusion.place_ref, s32[384]{0:T(512)S(1)} %get-tuple-element.26.table_ref, f32[24,128]{1,0:T(8,128)S(1)} %fusion.1.hh_ref, f32[24,1024,128]{2,1,0:T(8,128)S(1)} %get-tuple-element.38.g_ref, s32[384]{0:T(512)S(1)} %get-tuple-element.42.table2_ref, ...), custom_call_target="tpu_custom_call" | custom-call | flops 3000000000 | bytes 10000 | tf_op jit(solution)/shard_map/pallas_call | solution.py:431
  64.9 2.9 %collective-permute-start.17 = (bf16[1024,256]{1,0:T(8,128)(2,1)}, bf16[1024,256]{1,0:T(8,128)(2,1)S(1)}, u32[]{:S(2)}, u32[]{:S(2)}) collective-permute-start(bf16[1024,256]{1,0:T(8,128)(2,1)} %shard_map.66.own_ref), channel_id=1, source_target_pairs={{0,124},{4,8},{8,4},{12,16},{16,12},{20,24},{24,20},{28,32},{32,28... | collective-permute-start | bytes 1572872 | tf_op jit(solution)/shard_map/ppermute | solution.py:41
  67.8 3.5 %shard_map.65 = (bf16[1024,3200]{1,0:T(8,128)(2,1)S(1)}, f32[1024,128]{1,0:T(8,128)S(1)}) custom-call(s32[2]{0:T(128)S(1)} %pad_add_fusion.place_ref, s32[384]{0:T(512)S(1)} %get-tuple-element.26.table_ref, f32[24,128]{1,0:T(8,128)S(1)} %fusion.1.hh_ref, f32[24,1024,128]{2,1,0:T(8,128)S(1)} %get-tuple-element.38.g_ref, s32[384]{0:T(512)S(1)} %get-tuple-element.42.table2_ref, ...), custom_call_target="tpu_custom_call" | custom-call | flops 3000000000 | bytes 10000 | tf_op jit(solution)/shard_map/pallas_call | solution.py:435
  71.4 1.8 %shard_map.67.total_ref = f32[1024,256]{1,0:T(8,128)S(1)} custom-call(bf16[1024,3200]{1,0:T(8,128)(2,1)S(1)} %get-tuple-element.44.w_ref, bf16[1024,256]{1,0:T(8,128)(2,1)S(1)} %copy-done.1, bf16[1024,256]{1,0:T(8,128)(2,1)S(1)} %collective-permute-done.16.sib_ref), custom_call_target="tpu_custom_call" | custom-call | flops 3000000000 | bytes 10000 | tf_op jit(solution)/shard_map/pallas_call | solution.py:439
  73.2 3.8 %collective-permute-done.17.out_ref = bf16[1024,256]{1,0:T(8,128)(2,1)S(1)} collective-permute-done((bf16[1024,256]{1,0:T(8,128)(2,1)}, bf16[1024,256]{1,0:T(8,128)(2,1)S(1)}, u32[]{:S(2)}, u32[]{:S(2)}) %collective-permute-start.17) | collective-permute-done | bytes 524320 | tf_op jit(solution)/shard_map/ppermute | solution.py:41
  77.0 2.0 %shard_map.68 = bf16[1024,256]{1,0:T(8,128)(2,1)} custom-call(bf16[1024,3200]{1,0:T(8,128)(2,1)S(1)} %get-tuple-element.44.w_ref, f32[1024,128]{1,0:T(8,128)S(1)} %get-tuple-element.45.sum_ref, f32[1024,256]{1,0:T(8,128)S(1)} %shard_map.67.total_ref, bf16[1024,256]{1,0:T(8,128)(2,1)S(1)} %collective-permute-done.17.out_ref), custom_call_target="tpu_custom_call" | custom-call | flops 3000000000 | bytes 10000 | tf_op jit(solution)/shard_map/pallas_call | solution.py:443
  (29 shorter events, 0.4 us)
Async XLA Ops:
  2.7 6.8 %collective-permute-start = (bf16[1056,256]{1,0:T(8,128)(2,1)S(1)}, bf16[1056,256]{1,0:T(8,128)(2,1)S(1)}, u32[]{:S(2)}, u32[]{:S(2)}) collective-permute-start(bf16[1056,256]{1,0:T(8,128)(2,1)S(1)} %shard_map.59.refs_6_), channel_id=1, source_target_pairs={{0,4},{4,0},{8,12},{12,8},{16,20},{20,16},{24,28},{28,24},{32,36},... | collective-permute-start | bytes 1622024 | tf_op jit(solution)/shard_map/ppermute | solution.py:35
  2.8 20.5 %collective-permute-start.4 = (bf16[1056,256]{1,0:T(8,128)(2,1)S(1)}, bf16[1056,256]{1,0:T(8,128)(2,1)S(1)}, u32[]{:S(2)}, u32[]{:S(2)}) collective-permute-start(bf16[1056,256]{1,0:T(8,128)(2,1)S(1)} %shard_map.59.refs_6_), channel_id=1, source_target_pairs={{0,124},{4,8},{8,4},{12,16},{16,12},{20,24},{24,20},{28,32},{32,28... | collective-permute-start | bytes 1622024 | tf_op jit(solution)/shard_map/ppermute | solution.py:41
  9.5 5.2 %collective-permute-start.3 = (s32[2,2,32]{2,1,0:T(2,128)}, s32[2,2,32]{2,1,0:T(2,128)S(1)}, u32[]{:S(2)}, u32[]{:S(2)}) collective-permute-start(s32[2,2,32]{2,1,0:T(2,128)} %refs_0_.3), channel_id=1, source_target_pairs={{0,3},{1,0},{2,1},{3,2},{4,7},{5,4},{6,5},{7,6},{8,11},{9,8},{10,9... | collective-permute-start | bytes 1544 | tf_op jit(solution)/shard_map/ppermute | solution.py:470
  12.3 5.3 %collective-permute-start.2 = (s32[2,2,32]{2,1,0:T(2,128)}, s32[2,2,32]{2,1,0:T(2,128)S(1)}, u32[]{:S(2)}, u32[]{:S(2)}) collective-permute-start(s32[2,2,32]{2,1,0:T(2,128)} %refs_0_.3), channel_id=1, source_target_pairs={{0,2},{1,3},{2,0},{3,1},{4,6},{5,7},{6,4},{7,5},{8,10},{9,11},{10,... | collective-permute-start | bytes 1544 | tf_op jit(solution)/shard_map/ppermute | solution.py:470
  13.1 5.0 %collective-permute-start.1 = (s32[2,2,32]{2,1,0:T(2,128)}, s32[2,2,32]{2,1,0:T(2,128)S(1)}, u32[]{:S(2)}, u32[]{:S(2)}) collective-permute-start(s32[2,2,32]{2,1,0:T(2,128)} %refs_0_.3), channel_id=1, source_target_pairs={{0,1},{1,2},{2,3},{3,0},{4,5},{5,6},{6,7},{7,4},{8,9},{9,10},{10,1... | collective-permute-start | bytes 1544 | tf_op jit(solution)/shard_map/ppermute | solution.py:470
  14.0 18.4 %collective-permute-start.7 = (bf16[1024,256]{1,0:T(8,128)(2,1)}, bf16[1024,256]{1,0:T(8,128)(2,1)S(1)}, u32[]{:S(2)}, u32[]{:S(2)}) collective-permute-start(bf16[1024,256]{1,0:T(8,128)(2,1)} %own_ref.1), channel_id=1, source_target_pairs={{0,124},{4,8},{8,4},{12,16},{16,12},{20,24},{24,20},{28,32},{32,28... | collective-permute-start | bytes 1572872 | tf_op jit(solution)/shard_map/ppermute | solution.py:41
  29.1 14.4 %copy-start = (bf16[1024,256]{1,0:T(8,128)(2,1)S(1)}, bf16[1024,256]{1,0:T(8,128)(2,1)}, u32[]{:S(2)}) copy-start(bf16[1024,256]{1,0:T(8,128)(2,1)} %own_ref.1) | copy-start | bytes 1572868
  29.1 1.3 %collective-permute-start.5 = (f32[2,8,128]{2,1,0:T(8,128)S(1)}, f32[2,8,128]{2,1,0:T(8,128)S(1)}, u32[]{:S(2)}, u32[]{:S(2)}) collective-permute-start(f32[2,8,128]{2,1,0:T(8,128)S(1)} %get-tuple-element.56), channel_id=1, source_target_pairs={{0,4},{4,0},{8,12},{12,8},{16,20},{20,16},{24,28},{28,24},{32,36},... | collective-permute-start | bytes 24584 | tf_op jit(solution)/shard_map/ppermute | solution.py:35
  30.4 6.6 %collective-permute-start.6 = (f32[2,16,128]{2,1,0:T(8,128)S(1)}, f32[2,16,128]{2,1,0:T(8,128)S(1)}, u32[]{:S(2)}, u32[]{:S(2)}) collective-permute-start(f32[2,16,128]{2,1,0:T(8,128)S(1)} %pad_maximum_fusion.behind_ref), channel_id=1, source_target_pairs={{0,124},{4,8},{8,4},{12,16},{16,12},{20,24},{24,20},{28,32},{32,28... | collective-permute-start | bytes 49160 | tf_op jit(solution)/shard_map/ppermute | solution.py:41
  37.0 2.1 %collective-permute-start.8 = (f32[8,128]{1,0:T(8,128)S(1)}, f32[8,128]{1,0:T(8,128)S(1)}, u32[]{:S(2)}, u32[]{:S(2)}) collective-permute-start(f32[8,128]{1,0:T(8,128)S(1)} %get-tuple-element.52), channel_id=1, source_target_pairs={{0,4},{4,0},{8,12},{12,8},{16,20},{20,16},{24,28},{28,24},{32,36},... | collective-permute-start | bytes 12296 | tf_op jit(solution)/shard_map/ppermute | solution.py:35
  37.0 12.0 %collective-permute-start.12 = (bf16[1024,256]{1,0:T(8,128)(2,1)S(1)}, bf16[1024,256]{1,0:T(8,128)(2,1)S(1)}, u32[]{:S(2)}, u32[]{:S(2)}) collective-permute-start(bf16[1024,256]{1,0:T(8,128)(2,1)S(1)} %get-tuple-element.40.own_ref), channel_id=1, source_target_pairs={{0,124},{4,8},{8,4},{12,16},{16,12},{20,24},{24,20},{28,32},{32,28... | collective-permute-start | bytes 1572872 | tf_op jit(solution)/shard_map/ppermute | solution.py:41
  39.0 10.0 %collective-permute-start.11 = (bf16[1024,256]{1,0:T(8,128)(2,1)S(1)}, bf16[1024,256]{1,0:T(8,128)(2,1)S(1)}, u32[]{:S(2)}, u32[]{:S(2)}) collective-permute-start(bf16[1024,256]{1,0:T(8,128)(2,1)S(1)} %get-tuple-element.40.own_ref), channel_id=1, source_target_pairs={{0,4},{4,0},{8,12},{12,8},{16,20},{20,16},{24,28},{28,24},{32,36},... | collective-permute-start | bytes 1572872 | tf_op jit(solution)/shard_map/ppermute | solution.py:35
  43.4 1.3 %collective-permute-start.9 = (f32[2,8,128]{2,1,0:T(8,128)S(1)}, f32[2,8,128]{2,1,0:T(8,128)S(1)}, u32[]{:S(2)}, u32[]{:S(2)}) collective-permute-start(f32[2,8,128]{2,1,0:T(8,128)S(1)} %get-tuple-element.54), channel_id=1, source_target_pairs={{0,4},{4,0},{8,12},{12,8},{16,20},{20,16},{24,28},{28,24},{32,36},... | collective-permute-start | bytes 24584 | tf_op jit(solution)/shard_map/ppermute | solution.py:35
  43.5 10.9 %collective-permute-start.15 = (bf16[1024,256]{1,0:T(8,128)(2,1)S(1)}, bf16[1024,256]{1,0:T(8,128)(2,1)S(1)}, u32[]{:S(2)}, u32[]{:S(2)}) collective-permute-start(bf16[1024,256]{1,0:T(8,128)(2,1)S(1)} %copy-done), channel_id=1, source_target_pairs={{0,4},{4,0},{8,12},{12,8},{16,20},{20,16},{24,28},{28,24},{32,36},... | collective-permute-start | bytes 1572872 | tf_op jit(solution)/shard_map/ppermute | solution.py:35
  44.7 8.4 %collective-permute-start.10 = (f32[2,16,128]{2,1,0:T(8,128)S(1)}, f32[2,16,128]{2,1,0:T(8,128)S(1)}, u32[]{:S(2)}, u32[]{:S(2)}) collective-permute-start(f32[2,16,128]{2,1,0:T(8,128)S(1)} %pad_maximum_fusion.1.behind_ref), channel_id=1, source_target_pairs={{0,124},{4,8},{8,4},{12,16},{16,12},{20,24},{24,20},{28,32},{32,28... | collective-permute-start | bytes 49160 | tf_op jit(solution)/shard_map/ppermute | solution.py:41
  53.1 1.2 %collective-permute-start.13 = (f32[8,128]{1,0:T(8,128)S(1)}, f32[8,128]{1,0:T(8,128)S(1)}, u32[]{:S(2)}, u32[]{:S(2)}) collective-permute-start(f32[8,128]{1,0:T(8,128)S(1)} %get-tuple-element.50), channel_id=1, source_target_pairs={{0,4},{4,0},{8,12},{12,8},{16,20},{20,16},{24,28},{28,24},{32,36},... | collective-permute-start | bytes 12296 | tf_op jit(solution)/shard_map/ppermute | solution.py:35
  54.3 4.9 %collective-permute-start.14 = (f32[24,128]{1,0:T(8,128)S(1)}, f32[24,128]{1,0:T(8,128)S(1)}, u32[]{:S(2)}, u32[]{:S(2)}) collective-permute-start(f32[24,128]{1,0:T(8,128)S(1)} %fusion.1.hh_ref), channel_id=1, source_target_pairs={{0,3},{1,2},{2,1},{3,0},{4,7},{5,6},{6,5},{7,4},{8,11},{9,10},{10,... | collective-permute-start | bytes 36872 | tf_op jit(solution)/shard_map/ppermute | solution.py:46
  64.9 6.5 %copy-start.1 = (bf16[1024,256]{1,0:T(8,128)(2,1)S(1)}, bf16[1024,256]{1,0:T(8,128)(2,1)}, u32[]{:S(2)}) copy-start(bf16[1024,256]{1,0:T(8,128)(2,1)} %shard_map.66.own_ref) | copy-start | bytes 1572868
  64.9 6.5 %collective-permute-start.16 = (bf16[1024,256]{1,0:T(8,128)(2,1)}, bf16[1024,256]{1,0:T(8,128)(2,1)S(1)}, u32[]{:S(2)}, u32[]{:S(2)}) collective-permute-start(bf16[1024,256]{1,0:T(8,128)(2,1)} %shard_map.66.own_ref), channel_id=1, source_target_pairs={{0,4},{4,0},{8,12},{12,8},{16,20},{20,16},{24,28},{28,24},{32,36},... | collective-permute-start | bytes 1572872 | tf_op jit(solution)/shard_map/ppermute | solution.py:35
  64.9 12.1 %collective-permute-start.17 = (bf16[1024,256]{1,0:T(8,128)(2,1)}, bf16[1024,256]{1,0:T(8,128)(2,1)S(1)}, u32[]{:S(2)}, u32[]{:S(2)}) collective-permute-start(bf16[1024,256]{1,0:T(8,128)(2,1)} %shard_map.66.own_ref), channel_id=1, source_target_pairs={{0,124},{4,8},{8,4},{12,16},{16,12},{20,24},{24,20},{28,32},{32,28... | collective-permute-start | bytes 1572872 | tf_op jit(solution)/shard_map/ppermute | solution.py:41

commit v7 on v6

--- a/solution.py
+++ b/solution.py
@@ -59,30 +59,28 @@
     )
 
 
-def build_table(place_ref, coupling, slot_refs, table_ref):
+def enter_slots(place_ref, coupling, slot_refs, table_ref, quarter, counts):
+    low, high = counts
     owner = place_ref[0]
-    unroll = 4
-
-    def step(index, counts):
-        low, high = counts
-        for inner in range(unroll):
-            for slot_ref in slot_refs:
-                source = slot_ref[coupling, 0, index * unroll + inner]
-                target = slot_ref[coupling, 1, index * unroll + inner]
-                away = target >> 3
-                region = jnp.where(away == owner, 0, jnp.where(away == (owner ^ 1), NBLK, 2 * NBLK))
-                empty = source < 0
-                s = source & 7
-                shift = (s & 3) << 3
-                lower = s < 4
-                count = (jnp.where(lower, low, high) >> shift) & 255
-                table_ref[jnp.where(empty, UNREAD, s * STRIDE + count)] = region + (target & 7)
-                one = jnp.where(empty, 0, 1 << shift)
-                low, high = low + jnp.where(lower, one, 0), high + jnp.where(lower, 0, one)
-        return low, high
-
-    zero = jnp.int32(0)
-    counts = lax.fori_loop(0, slot_refs[0].shape[2] // unroll, step, (zero, zero))
+    share = slot_refs[0].shape[2] // 4
+    for index in range(share):
+        for slot_ref in slot_refs:
+            source = slot_ref[coupling, 0, quarter * share + index]
+            target = slot_ref[coupling, 1, quarter * share + index]
+            away = target >> 3
+            region = jnp.where(away == owner, 0, jnp.where(away == (owner ^ 1), NBLK, 2 * NBLK))
+            empty = source < 0
+            s = source & 7
+            shift = (s & 3) << 3
+            lower = s < 4
+            count = (jnp.where(lower, low, high) >> shift) & 255
+            table_ref[jnp.where(empty, UNREAD, s * STRIDE + count)] = region + (target & 7)
+            one = jnp.where(empty, 0, 1 << shift)
+            low, high = low + jnp.where(lower, one, 0), high + jnp.where(lower, 0, one)
+    return low, high
+
+
+def close_table(table_ref, counts):
     for s in range(NBLK):
         count = (counts[s // 4] >> (8 * (s % 4))) & 255
         for extra in range(QUAD - 1):
@@ -90,17 +88,21 @@
         table_ref[GROUPS + s] = (count + QUAD - 1) >> 2
 
 
+def product_pair(source_ref, target_ref, g_ref, region, pair):
+    rows = target_ref[pl.ds(pl.multiple_of(pair * 256, 256), 256), :]
+    g = lax.dot_general(
+        source_ref[...], rows, (((1,), (1,)), ((), ())), preferred_element_type=jnp.float32
+    ) * (2.0 * SCALE)
+    g_ref[region * NBLK + 2 * pair] = g[:, :BLOCK]
+    g_ref[region * NBLK + 2 * pair + 1] = g[:, BLOCK:]
+
+
 def products(source_ref, target_refs, g_ref, first):
     for region, target_ref in enumerate(target_refs, first):
 
         @pl.loop(0, NBLK // 2)
         def _(pair):
-            rows = target_ref[pl.ds(pl.multiple_of(pair * 256, 256), 256), :]
-            g = lax.dot_general(
-                source_ref[...], rows, (((1,), (1,)), ((), ())), preferred_element_type=jnp.float32
-            ) * (2.0 * SCALE)
-            g_ref[region * NBLK + 2 * pair] = g[:, :BLOCK]
-            g_ref[region * NBLK + 2 * pair + 1] = g[:, BLOCK:]
+            product_pair(source_ref, target_ref, g_ref, region, pair)
 
 
 def block_masses(mass_ref, group, first):
@@ -192,33 +194,34 @@
     extended(hh_ref, terms_ref)
     top_ref[...] = jnp.full(top_ref.shape, -BIG, jnp.float32)
     mass_ref[...] = jnp.zeros(mass_ref.shape, jnp.float32)
-    row_maxima(table_ref, terms_ref, g_ref, m_ref)
 
     @pl.loop(0, NBLK)
     def _(s):
-        m = m_ref[source_rows(s), :].reshape(STRIPS, 8, BLOCK)
-
-        def step(q, acc):
-            v = [
-                jnp.exp2(strips(g_ref, t, s) + terms_ref[t] - m)
-                for t in group_targets(table_ref, s, q)
-            ]
-            return acc + ((v[0] + v[1]) + (v[2] + v[3]))
-
-        start = jnp.zeros((STRIPS, 8, BLOCK), jnp.float32)
-        acc = lax.fori_loop(0, table_ref[GROUPS + s], step, start)
+        def step(q, carried):
+            top, acc = carried
+            v = [strips(g_ref, t, s) + terms_ref[t] for t in group_targets(table_ref, s, q)]
+            high = jnp.maximum(jnp.maximum(v[0], v[1]), jnp.maximum(v[2], v[3]))
+            high = jnp.maximum(top, high)
+            e = [jnp.exp2(part - high) for part in v]
+            return high, acc * jnp.exp2(top - high) + ((e[0] + e[1]) + (e[2] + e[3]))
+
+        shape = (STRIPS, 8, BLOCK)
+        start = jnp.full(shape, -BIG, jnp.float32), jnp.zeros(shape, jnp.float32)
+        top, acc = lax.fori_loop(0, table_ref[GROUPS + s], step, start)
+        m_ref[source_rows(s), :] = top.reshape(BLOCK, BLOCK)
         acc_ref[source_rows(s), :] = acc.reshape(BLOCK, BLOCK)
 
-    sums = jnp.broadcast_to(jnp.sum(acc_ref[...], axis=1, keepdims=True), acc_ref.shape)
-    acc_ref[...] = kc_ref[...] - LAM * (m_ref[...] + LOG2E * jnp.log(sums))
+    tops = m_ref[...]
+    high = jnp.max(tops, axis=1, keepdims=True)
+    sums = jnp.sum(acc_ref[...] * jnp.exp2(tops - high), axis=1, keepdims=True)
+    acc_ref[...] = kc_ref[...] - LAM * (high + LOG2E * jnp.log(sums))
 
     @pl.loop(0, NBLK)
     def _(s):
         uu = acc_ref[source_rows(s), :].reshape(STRIPS, 8, BLOCK)
-
-        @pl.loop(0, table_ref[GROUPS + s])
-        def _(q):
-            ts = group_targets(table_ref, s, q)
+        groups = table_ref[GROUPS + s]
+
+        def columns(ts):
             tops = [top_ref[t] for t in ts]
             masses = [mass_ref[t] for t in ts]
             made = []
@@ -230,6 +233,14 @@
                 top_ref[t] = high
                 mass_ref[t] = mass
 
+        @pl.loop(0, groups // 2)
+        def _(double):
+            columns(group_targets(table_ref, s, 2 * double) + group_targets(table_ref, s, 2 * double + 1))
+
+        @pl.when(groups % 2 == 1)
+        def _():
+            columns(group_targets(table_ref, s, groups - 1))
+
     top = top_ref[:WIN]
     high = jnp.max(top, axis=1, keepdims=True)
     part_ref[0] = high[:, 0, :]
@@ -244,7 +255,6 @@
     def _(s):
         rows = source_rows(s)
         m = m_ref[rows, :].reshape(STRIPS, 8, BLOCK)
-        w_ref[rows, :] = jnp.zeros((BLOCK, (WIN + 1) * BLOCK), jnp.bfloat16)
 
         def step(q, acc):
             ts = group_targets(table_ref, s, q)
@@ -295,9 +305,15 @@
         copy.start()
     unpack(own_ref, window_ref, 0)
     unpack(sib_ref, window_ref, 1)
-    build_table(place_ref, place_ref[1], slot_refs, table_ref)
     copies[0].wait()
-    products(source_ref, (own_ref, sib_ref), g_ref, 0)
+
+    def step(pair, counts):
+        product_pair(source_ref, own_ref, g_ref, 0, pair)
+        return enter_slots(place_ref, group, slot_refs, table_ref, pair, counts)
+
+    zero = jnp.int32(0)
+    close_table(table_ref, lax.fori_loop(0, NBLK // 2, step, (zero, zero)))
+    products(source_ref, (sib_ref,), g_ref, 1)
     copies[1].wait()
     masses = block_masses(mass_ref, group, 0)
     for s in range(NBLK):
@@ -330,7 +346,12 @@
     )
     for copy in copies:
         copy.start()
-    build_table(place_ref, 1 - group, slot_refs, table_ref)
+
+    def step(quarter, counts):
+        return enter_slots(place_ref, 1 - group, slot_refs, table_ref, quarter, counts)
+
+    zero = jnp.int32(0)
+    close_table(table_ref, lax.fori_loop(0, 4, step, (zero, zero)))
     for copy in copies:
         copy.wait()
 
@@ -345,7 +366,16 @@
         weigh(*others, *outs)
 
 
-def late_kernel(place_ref, table_ref, hh_ref, g_ref, table2_ref, hh2_ref, g2_ref, own_ref, sib_ref, out_ref, late_ref, w_ref, sum_ref, terms_ref, m_ref):
+def blank_kernel(behind_ref, w_ref):
+    del behind_ref
+
+    @pl.loop(0, NBLK)
+    def _(s):
+        w_ref[source_rows(s), :] = jnp.zeros((BLOCK, (WIN + 1) * BLOCK), jnp.bfloat16)
+
+
+def late_kernel(place_ref, table_ref, hh_ref, g_ref, table2_ref, hh2_ref, g2_ref, own_ref, sib_ref, out_ref, blank_ref, late_ref, w_ref, sum_ref, terms_ref, m_ref):
+    del blank_ref
     weigh_one(1, place_ref, (table_ref, hh_ref, g_ref), (table2_ref, hh2_ref, g2_ref), w_ref, sum_ref, terms_ref, m_ref)
     fates = (own_ref, sib_ref, out_ref)
 
@@ -355,6 +385,7 @@
 
 
 def early_weights_kernel(place_ref, table_ref, hh_ref, g_ref, table2_ref, hh2_ref, g2_ref, w_ref, sum_ref, terms_ref, m_ref):
+    blank_kernel(None, w_ref)
     weigh_one(0, place_ref, (table_ref, hh_ref, g_ref), (table2_ref, hh2_ref, g2_ref), w_ref, sum_ref, terms_ref, m_ref)
 
 
@@ -380,7 +411,6 @@
 TERMS = pltpu.VMEM((WIN + 1, 8, BLOCK), jnp.float32)
 COLUMN = pltpu.VMEM(COLUMN_SHAPE.shape, COLUMN_SHAPE.dtype)
 SWEEP_SCRATCH = [TERMS] * 3 + [COLUMN] * 2
-HOLD = [pltpu.VMEM(W_SHAPE.shape, W_SHAPE.dtype), COLUMN]
 
 
 WINDOW_SHAPE = jax.ShapeDtypeStruct((2, WIN, BLOCK), jnp.float32)
@@ -427,8 +457,13 @@
 COUPLINGS = [SMEM, SMEM, VMEM, VMEM, SMEM, VMEM, VMEM]
 
 
+def blank_weights(behind):
+    return call(blank_kernel, W_SHAPE, VMEM, [ANY])(behind)
+
+
 def late_fates(*args):
-    return call(late_kernel, FATE_SHAPE, VMEM, COUPLINGS + [VMEM] * 3, HOLD + [TERMS, COLUMN], mib=9)(*args)
+    outs, in_specs = (FATE_SHAPE, W_SHAPE), COUPLINGS + [VMEM] * 4
+    return call(late_kernel, outs, (VMEM, VMEM), in_specs, [COLUMN, TERMS, COLUMN], {10: 1})(*args)[0]
 
 
 def early_weights(*args):
@@ -497,7 +532,7 @@
     )
     hh = window[1] - LAM * totals
     couplings = (place, table, hh, g, table_other, mirrored(hh), g_other)
-    late = late_fates(*couplings, signatures, fates_sib, fates_out)
+    late = late_fates(*couplings, signatures, fates_sib, fates_out, blank_weights(hh))
     late_out, late_sib = outward(late), sibling(late)
     weights, sums = early_weights(*couplings)
     total = early_near(weights, late, late_sib)

time: 80 us -> 79.5 us (level); the launches traced: 79.1 us -> 79.7 us
  Pallas kernels: 36.9 us -> 37.8 us
    ppermute x6, starting transfers between devices: 18 us -> 15.8 us  [outward(): return lax.ppermute(value, 'cells', pairs)]
    ppermute x8, starting transfers between devices: 0.92 us -> 2.41 us  [sibling(): lax.ppermute(value, 'cells', [(c, c ^ 1) for c in range(lax.axis_size('ce...]
    ppermute x6, waiting for transfers between devices: 6.51 us -> 7.5 us  [outward(): return lax.ppermute(value, 'cells', pairs)]
    pallas_call x1 -> x2, Pallas kernels: 5.64 us -> 5.88 us  [the longest x1 5.42 us: late_fates(): call(late_kernel, outs, (VMEM, VMEM), in_specs, [COLUMN, TERMS, COLUMN],...]
  transfers between devices with their start and end apart: 18 -> 18, of which waited for: 9 -> 9; matrix products, arithmetic and copies ran while one was open for 0% -> 0% of each run, Pallas kernels for 34% -> 36%
where the time goes in v7:
time: 79.5 us; the launch traced here: 79.7 us
  Pallas kernels  37.8 us (48%)
  starting transfers between devices  22.7 us (29%)
  waiting for transfers between devices  18.2 us (23%)
  between operations  0.85 us (1%)
    ppermute x6, starting transfers between devices, outward(): return lax.ppermute(value, 'cells', pairs)  15.8 us
    ppermute x6, waiting for transfers between devices, outward(): return lax.ppermute(value, 'cells', pairs)  7.5 us
    pallas_call x1, Pallas kernels, near_products(): call(near_kernel, outs, (VMEM,) * 4 + (SMEM,), in_specs, scratch)  5.88 us
    pallas_call x1, Pallas kernels, far_products(): call(far_kernel, outs, (VMEM,) * 3, [SMEM] + [VMEM] * 5, SWEEP_SCRATCH, {...  5.66 us
    pallas_call x1, Pallas kernels, late_fates(): call(late_kernel, outs, (VMEM, VMEM), in_specs, [COLUMN, TERMS, COLUMN],...  5.42 us
    ppermute x3, starting transfers between devices, shifted(): lax.ppermute(value, 'tiles', [(t, (t + steps) % count) for t in range(cou...  4.45 us
    ppermute x1, waiting for transfers between devices, mirrored(): lax.ppermute(value, 'tiles', [(t, count - 1 - t) for t in range(count)])  4.42 us
    pallas_call x1, Pallas kernels, sweep(): call(sweep_kernel, PART_SHAPE, VMEM, [SMEM] + [VMEM] * 3, SWEEP_SCRATCH)  4.33 us
  transfers between devices with their start and end apart: 18, of which 9 were waited for; matrix products, arithmetic and copies ran while one was open for 0% of the time, Pallas kernels for 36%

profile of v7, /device:TPU:0, one launch (start us, length us, event | category | flops | bytes accessed | tf_op | source)
XLA Modules:
  0.0 79.7 jit_solution(3453200417465887014)
XLA Ops:
  0.7 2.0 %shard_map.59.refs_6_ = bf16[1056,256]{1,0:T(8,128)(2,1)S(1)} custom-call(s32[2]{0:T(128)S(1)} %pad_add_fusion.place_ref, bf16[3,1024,256]{2,1,0:T(8,128)(2,1)} %refs_4_.3, f32[3,1024]{1,0:T(4,128)} %refs_5_.1), custom_call_target="tpu_custom_call" | custom-call | flops 3000000000 | bytes 10000 | tf_op jit(solution)/shard_map/pallas_call | solution.py:427
  2.9 6.7 %collective-permute-start.4 = (bf16[1056,256]{1,0:T(8,128)(2,1)S(1)}, bf16[1056,256]{1,0:T(8,128)(2,1)S(1)}, u32[]{:S(2)}, u32[]{:S(2)}) collective-permute-start(bf16[1056,256]{1,0:T(8,128)(2,1)S(1)} %shard_map.59.refs_6_), channel_id=1, source_target_pairs={{0,124},{4,8},{8,4},{12,16},{16,12},{20,24},{24,20},{28,32},{32,28... | collective-permute-start | bytes 1622024 | tf_op jit(solution)/shard_map/ppermute | solution.py:41
  9.5 2.8 %collective-permute-start.3 = (s32[2,2,32]{2,1,0:T(2,128)S(1)}, s32[2,2,32]{2,1,0:T(2,128)S(1)}, u32[]{:S(2)}, u32[]{:S(2)}) collective-permute-start(s32[2,2,32]{2,1,0:T(2,128)S(1)} %copy-done.2), channel_id=1, source_target_pairs={{0,3},{1,0},{2,1},{3,2},{4,7},{5,4},{6,5},{7,6},{8,11},{9,8},{10,9... | collective-permute-start | bytes 1544 | tf_op jit(solution)/shard_map/ppermute | solution.py:505
  12.3 0.8 %collective-permute-start.2 = (s32[2,2,32]{2,1,0:T(2,128)S(1)}, s32[2,2,32]{2,1,0:T(2,128)S(1)}, u32[]{:S(2)}, u32[]{:S(2)}) collective-permute-start(s32[2,2,32]{2,1,0:T(2,128)S(1)} %copy-done.2), channel_id=1, source_target_pairs={{0,2},{1,3},{2,0},{3,1},{4,6},{5,7},{6,4},{7,5},{8,10},{9,11},{10,... | collective-permute-start | bytes 1544 | tf_op jit(solution)/shard_map/ppermute | solution.py:505
  13.1 0.9 %collective-permute-start.1 = (s32[2,2,32]{2,1,0:T(2,128)S(1)}, s32[2,2,32]{2,1,0:T(2,128)S(1)}, u32[]{:S(2)}, u32[]{:S(2)}) collective-permute-start(s32[2,2,32]{2,1,0:T(2,128)S(1)} %copy-done.2), channel_id=1, source_target_pairs={{0,1},{1,2},{2,3},{3,0},{4,5},{5,6},{6,7},{7,4},{8,9},{9,10},{10,1... | collective-permute-start | bytes 1544 | tf_op jit(solution)/shard_map/ppermute | solution.py:505
  14.0 0.7 collective-permute-start.7
  14.7 2.7 %collective-permute-done.2.refs_2_ = s32[2,2,32]{2,1,0:T(2,128)S(1)} collective-permute-done((s32[2,2,32]{2,1,0:T(2,128)S(1)}, s32[2,2,32]{2,1,0:T(2,128)S(1)}, u32[]{:S(2)}, u32[]{:S(2)}) %collective-permute-start.2) | collective-permute-done | bytes 544 | tf_op jit(solution)/shard_map/ppermute | solution.py:505
  17.4 0.5 collective-permute-done.1.refs_1_
  17.9 5.9 %shard_map.60 = (f32[24,1024,128]{2,1,0:T(8,128)S(1)}, f32[1024,128]{1,0:T(8,128)S(1)}, f32[2,16,128]{2,1,0:T(8,128)S(1)}, bf16[1024,256]{1,0:T(8,128)(2,1)S(1)}, s32[384]{0:T(512)S(1)}) custom-call(s32[2]{0:T(128)S(1)} %pad_add_fusion.place_ref, s32[2,2,32]{2,1,0:T(2,128)} %refs_0_.3, s32[2,2,32]{2,1,0:T(2,128)S(1)} %collective-permute-done.1.refs_1_, ...), custom_call_target="tpu_custom_call" | custom-call | flops 3000000000 | bytes 10000 | tf_op jit(solution)/shard_map/pallas_call | solution.py:434
  23.8 5.7 %shard_map.61 = (f32[24,1024,128]{2,1,0:T(8,128)S(1)}, f32[2,24,128]{2,1,0:T(8,128)S(1)}, f32[2,24,128]{2,1,0:T(8,128)S(1)}) custom-call(s32[384]{0:T(512)S(1)} %get-tuple-element.27.table_ref, bf16[1024,256]{1,0:T(8,128)(2,1)S(1)} %get-tuple-element.28.source_ref, ...), custom_call_target="tpu_custom_call", output_to_operand_aliasing={{0}: (3, {})} | custom-call | flops 3000000000 | bytes 10000 | tf_op jit(solution)/shard_map/pallas_call | solution.py:439
  29.6 1.2 %collective-permute-done.5 = f32[2,8,128]{2,1,0:T(8,128)S(1)} collective-permute-done((f32[2,8,128]{2,1,0:T(8,128)S(1)}, f32[2,8,128]{2,1,0:T(8,128)S(1)}, u32[]{:S(2)}, u32[]{:S(2)}) %collective-permute-start.5) | collective-permute-done | bytes 8224 | tf_op jit(solution)/shard_map/ppermute | solution.py:35
  30.7 1.6 %collective-permute-start.6 = (f32[2,16,128]{2,1,0:T(8,128)S(1)}, f32[2,16,128]{2,1,0:T(8,128)S(1)}, u32[]{:S(2)}, u32[]{:S(2)}) collective-permute-start(f32[2,16,128]{2,1,0:T(8,128)S(1)} %pad_maximum_fusion.behind_ref), channel_id=1, source_target_pairs={{0,124},{4,8},{8,4},{12,16},{16,12},{20,24},{24,20},{28,32},{32,28... | collective-permute-start | bytes 49160 | tf_op jit(solution)/shard_map/ppermute | solution.py:41
  32.3 2.6 %shard_map.62 = (s32[384]{0:T(512)S(1)}, bf16[1024,256]{1,0:T(8,128)(2,1)S(1)}, bf16[1024,256]{1,0:T(8,128)(2,1)S(1)}) custom-call(s32[2]{0:T(128)S(1)} %pad_add_fusion.place_ref, f32[2,16,128]{2,1,0:T(8,128)S(1)} %pad_maximum_fusion.behind_ref, bf16[1024,256]{1,0:T(8,128)(2,1)S(1)} %collective-permute-done.7.arrived_ref.out_ref, s32[2,2,32]{2,1,0:T(2,128)} %refs_0_.3, ...), custom_call_target="tpu_custom_call" | custom-call | flops 3000000000 | bytes 10000 | tf_op jit(solution)/shard_map/pallas_call | solution.py:454
  34.9 2.4 %collective-permute-done.6 = f32[2,16,128]{2,1,0:T(8,128)S(1)} collective-permute-done((f32[2,16,128]{2,1,0:T(8,128)S(1)}, f32[2,16,128]{2,1,0:T(8,128)S(1)}, u32[]{:S(2)}, u32[]{:S(2)}) %collective-permute-start.6) | collective-permute-done | bytes 16416 | tf_op jit(solution)/shard_map/ppermute | solution.py:41
  37.4 1.6 %collective-permute-start.12 = (bf16[1024,256]{1,0:T(8,128)(2,1)S(1)}, bf16[1024,256]{1,0:T(8,128)(2,1)S(1)}, u32[]{:S(2)}, u32[]{:S(2)}) collective-permute-start(bf16[1024,256]{1,0:T(8,128)(2,1)S(1)} %get-tuple-element.41.own_ref), channel_id=1, source_target_pairs={{0,124},{4,8},{8,4},{12,16},{16,12},{20,24},{24,20},{28,32},{32,28... | collective-permute-start | bytes 1572872 | tf_op jit(solution)/shard_map/ppermute | solution.py:41
  39.0 4.3 %shard_map.63 = f32[2,24,128]{2,1,0:T(8,128)S(1)} custom-call(s32[384]{0:T(512)S(1)} %get-tuple-element.27.table_ref, f32[24,128]{1,0:T(8,128)S(1)} %fusion.hh_ref, f32[1024,128]{1,0:T(8,128)S(1)} %get-tuple-element.31.kc_ref, f32[24,1024,128]{2,1,0:T(8,128)S(1)} %get-tuple-element.39.g_ref), custom_call_target="tpu_custom_call" | custom-call | flops 3000000000 | bytes 10000 | tf_op jit(solution)/shard_map/pallas_call | solution.py:443
  43.4 1.5 %collective-permute-start.9 = (f32[2,8,128]{2,1,0:T(8,128)S(1)}, f32[2,8,128]{2,1,0:T(8,128)S(1)}, u32[]{:S(2)}, u32[]{:S(2)}) collective-permute-start(f32[2,8,128]{2,1,0:T(8,128)S(1)} %get-tuple-element.56), channel_id=1, source_target_pairs={{0,4},{4,0},{8,12},{12,8},{16,20},{20,16},{24,28},{28,24},{32,36},... | collective-permute-start | bytes 24584 | tf_op jit(solution)/shard_map/ppermute | solution.py:35
  44.8 0.1 collective-permute-start.15
  44.9 0.7 collective-permute-done.9
  45.7 2.9 %collective-permute-start.10 = (f32[2,16,128]{2,1,0:T(8,128)S(1)}, f32[2,16,128]{2,1,0:T(8,128)S(1)}, u32[]{:S(2)}, u32[]{:S(2)}) collective-permute-start(f32[2,16,128]{2,1,0:T(8,128)S(1)} %pad_maximum_fusion.1.behind_ref), channel_id=1, source_target_pairs={{0,124},{4,8},{8,4},{12,16},{16,12},{20,24},{24,20},{28,32},{32,28... | collective-permute-start | bytes 49160 | tf_op jit(solution)/shard_map/ppermute | solution.py:41
  48.6 0.8 %collective-permute-done.12.out_ref = bf16[1024,256]{1,0:T(8,128)(2,1)S(1)} collective-permute-done((bf16[1024,256]{1,0:T(8,128)(2,1)S(1)}, bf16[1024,256]{1,0:T(8,128)(2,1)S(1)}, u32[]{:S(2)}, u32[]{:S(2)}) %collective-permute-start.12) | collective-permute-done | bytes 524320 | tf_op jit(solution)/shard_map/ppermute | solution.py:41
  49.4 4.0 %shard_map.64.g2_ref = f32[24,1024,128]{2,1,0:T(8,128)S(1)} custom-call(f32[2,16,128]{2,1,0:T(8,128)S(1)} %pad_maximum_fusion.1.behind_ref, bf16[1024,256]{1,0:T(8,128)(2,1)S(1)} %get-tuple-element.40.source_ref, bf16[1024,256]{1,0:T(8,128)(2,1)S(1)} %get-tuple-element.41.own_ref, bf16[1024,256]{1,0:T(8,128)(2,1)S(1)} %collective-permute-done.11.sib_ref, ...), custom_call_target="tpu_custom_call" | custom-call | flops 3000000000 | bytes 10000 | tf_op jit(solution)/shard_map/pallas_call | solution.py:447
  53.6 1.2 %collective-permute-done.13 = f32[8,128]{1,0:T(8,128)S(1)} collective-permute-done((f32[8,128]{1,0:T(8,128)S(1)}, f32[8,128]{1,0:T(8,128)S(1)}, u32[]{:S(2)}, u32[]{:S(2)}) %collective-permute-start.13) | collective-permute-done | bytes 4128 | tf_op jit(solution)/shard_map/ppermute | solution.py:35
  54.7 0.5 shard_map.66.blank_ref
  55.2 4.4 %collective-permute-done.14.hh2_ref = f32[24,128]{1,0:T(8,128)S(1)} collective-permute-done((f32[24,128]{1,0:T(8,128)S(1)}, f32[24,128]{1,0:T(8,128)S(1)}, u32[]{:S(2)}, u32[]{:S(2)}) %collective-permute-start.14) | collective-permute-done | bytes 12320 | tf_op jit(solution)/shard_map/ppermute | solution.py:46
  59.6 5.4 %shard_map.67 = (bf16[1024,256]{1,0:T(8,128)(2,1)}, bf16[1024,3200]{1,0:T(8,128)(2,1)S(1)}) custom-call(s32[2]{0:T(128)S(1)} %pad_add_fusion.place_ref, s32[384]{0:T(512)S(1)} %get-tuple-element.27.table_ref, f32[24,128]{1,0:T(8,128)S(1)} %fusion.1.hh_ref.behind_ref, f32[24,1024,128]{2,1,0:T(8,128)S(1)} %get-tuple-element.39.g_ref, ...), custom_call_target="tpu_custom_call", output_to_operand_aliasing={{1}: (10, {})} | custom-call | flops 3000000000 | bytes 10000 | tf_op jit(solution)/shard_map/pallas_call | solution.py:466
  65.0 0.5 collective-permute-start.16
  65.5 2.4 %collective-permute-start.17 = (bf16[1024,256]{1,0:T(8,128)(2,1)}, bf16[1024,256]{1,0:T(8,128)(2,1)S(1)}, u32[]{:S(2)}, u32[]{:S(2)}) collective-permute-start(bf16[1024,256]{1,0:T(8,128)(2,1)} %get-tuple-element.24.own_ref), channel_id=1, source_target_pairs={{0,124},{4,8},{8,4},{12,16},{16,12},{20,24},{24,20},{28,32},{32,28... | collective-permute-start | bytes 1572872 | tf_op jit(solution)/shard_map/ppermute | solution.py:41
  67.9 3.7 %shard_map.65 = (bf16[1024,3200]{1,0:T(8,128)(2,1)S(1)}, f32[1024,128]{1,0:T(8,128)S(1)}) custom-call(s32[2]{0:T(128)S(1)} %pad_add_fusion.place_ref, s32[384]{0:T(512)S(1)} %get-tuple-element.27.table_ref, f32[24,128]{1,0:T(8,128)S(1)} %fusion.1.hh_ref.behind_ref, f32[24,1024,128]{2,1,0:T(8,128)S(1)} %get-tuple-element.39.g_ref, ...), custom_call_target="tpu_custom_call" | custom-call | flops 3000000000 | bytes 10000 | tf_op jit(solution)/shard_map/pallas_call | solution.py:470
  71.6 1.8 %shard_map.68.total_ref = f32[1024,256]{1,0:T(8,128)S(1)} custom-call(bf16[1024,3200]{1,0:T(8,128)(2,1)S(1)} %get-tuple-element.45.w_ref, bf16[1024,256]{1,0:T(8,128)(2,1)S(1)} %copy-done.1, bf16[1024,256]{1,0:T(8,128)(2,1)S(1)} %collective-permute-done.16.sib_ref), custom_call_target="tpu_custom_call" | custom-call | flops 3000000000 | bytes 10000 | tf_op jit(solution)/shard_map/pallas_call | solution.py:474
  73.4 4.2 %collective-permute-done.17.out_ref = bf16[1024,256]{1,0:T(8,128)(2,1)S(1)} collective-permute-done((bf16[1024,256]{1,0:T(8,128)(2,1)}, bf16[1024,256]{1,0:T(8,128)(2,1)S(1)}, u32[]{:S(2)}, u32[]{:S(2)}) %collective-permute-start.17) | collective-permute-done | bytes 524320 | tf_op jit(solution)/shard_map/ppermute | solution.py:41
  77.7 2.0 %shard_map.69 = bf16[1024,256]{1,0:T(8,128)(2,1)} custom-call(bf16[1024,3200]{1,0:T(8,128)(2,1)S(1)} %get-tuple-element.45.w_ref, f32[1024,128]{1,0:T(8,128)S(1)} %get-tuple-element.46.sum_ref, f32[1024,256]{1,0:T(8,128)S(1)} %shard_map.68.total_ref, bf16[1024,256]{1,0:T(8,128)(2,1)S(1)} %collective-permute-done.17.out_ref), custom_call_target="tpu_custom_call" | custom-call | flops 3000000000 | bytes 10000 | tf_op jit(solution)/shard_map/pallas_call | solution.py:478
  (32 shorter events, 0.6 us)
Async XLA Ops:
  0.6 8.9 %copy-start.2 = (s32[2,2,32]{2,1,0:T(2,128)S(1)}, s32[2,2,32]{2,1,0:T(2,128)}, u32[]{:S(2)}) copy-start(s32[2,2,32]{2,1,0:T(2,128)} %refs_0_.3) | copy-start | bytes 1540
  0.6 13.3 %copy-start = (bf16[1024,256]{1,0:T(8,128)(2,1)S(1)}, bf16[1024,256]{1,0:T(8,128)(2,1)}, u32[]{:S(2)}) copy-start(bf16[1024,256]{1,0:T(8,128)(2,1)} %own_ref.1) | copy-start | bytes 1572868
  2.8 6.8 %collective-permute-start = (bf16[1056,256]{1,0:T(8,128)(2,1)S(1)}, bf16[1056,256]{1,0:T(8,128)(2,1)S(1)}, u32[]{:S(2)}, u32[]{:S(2)}) collective-permute-start(bf16[1056,256]{1,0:T(8,128)(2,1)S(1)} %shard_map.59.refs_6_), channel_id=1, source_target_pairs={{0,4},{4,0},{8,12},{12,8},{16,20},{20,16},{24,28},{28,24},{32,36},... | collective-permute-start | bytes 1622024 | tf_op jit(solution)/shard_map/ppermute | solution.py:35
  2.9 20.9 %collective-permute-start.4 = (bf16[1056,256]{1,0:T(8,128)(2,1)S(1)}, bf16[1056,256]{1,0:T(8,128)(2,1)S(1)}, u32[]{:S(2)}, u32[]{:S(2)}) collective-permute-start(bf16[1056,256]{1,0:T(8,128)(2,1)S(1)} %shard_map.59.refs_6_), channel_id=1, source_target_pairs={{0,124},{4,8},{8,4},{12,16},{16,12},{20,24},{24,20},{28,32},{32,28... | collective-permute-start | bytes 1622024 | tf_op jit(solution)/shard_map/ppermute | solution.py:41
  9.5 5.2 %collective-permute-start.3 = (s32[2,2,32]{2,1,0:T(2,128)S(1)}, s32[2,2,32]{2,1,0:T(2,128)S(1)}, u32[]{:S(2)}, u32[]{:S(2)}) collective-permute-start(s32[2,2,32]{2,1,0:T(2,128)S(1)} %copy-done.2), channel_id=1, source_target_pairs={{0,3},{1,0},{2,1},{3,2},{4,7},{5,4},{6,5},{7,6},{8,11},{9,8},{10,9... | collective-permute-start | bytes 1544 | tf_op jit(solution)/shard_map/ppermute | solution.py:505
  12.3 5.1 %collective-permute-start.2 = (s32[2,2,32]{2,1,0:T(2,128)S(1)}, s32[2,2,32]{2,1,0:T(2,128)S(1)}, u32[]{:S(2)}, u32[]{:S(2)}) collective-permute-start(s32[2,2,32]{2,1,0:T(2,128)S(1)} %copy-done.2), channel_id=1, source_target_pairs={{0,2},{1,3},{2,0},{3,1},{4,6},{5,7},{6,4},{7,5},{8,10},{9,11},{10,... | collective-permute-start | bytes 1544 | tf_op jit(solution)/shard_map/ppermute | solution.py:505
  13.1 4.8 %collective-permute-start.1 = (s32[2,2,32]{2,1,0:T(2,128)S(1)}, s32[2,2,32]{2,1,0:T(2,128)S(1)}, u32[]{:S(2)}, u32[]{:S(2)}) collective-permute-start(s32[2,2,32]{2,1,0:T(2,128)S(1)} %copy-done.2), channel_id=1, source_target_pairs={{0,1},{1,2},{2,3},{3,0},{4,5},{5,6},{6,7},{7,4},{8,9},{9,10},{10,1... | collective-permute-start | bytes 1544 | tf_op jit(solution)/shard_map/ppermute | solution.py:505
  14.0 18.3 %collective-permute-start.7 = (bf16[1024,256]{1,0:T(8,128)(2,1)S(1)}, bf16[1024,256]{1,0:T(8,128)(2,1)S(1)}, u32[]{:S(2)}, u32[]{:S(2)}) collective-permute-start(bf16[1024,256]{1,0:T(8,128)(2,1)S(1)} %copy-done), channel_id=1, source_target_pairs={{0,124},{4,8},{8,4},{12,16},{16,12},{20,24},{24,20},{28,32},{32,28... | collective-permute-start | bytes 1572872 | tf_op jit(solution)/shard_map/ppermute | solution.py:41
  29.5 1.3 %collective-permute-start.5 = (f32[2,8,128]{2,1,0:T(8,128)S(1)}, f32[2,8,128]{2,1,0:T(8,128)S(1)}, u32[]{:S(2)}, u32[]{:S(2)}) collective-permute-start(f32[2,8,128]{2,1,0:T(8,128)S(1)} %get-tuple-element.58), channel_id=1, source_target_pairs={{0,4},{4,0},{8,12},{12,8},{16,20},{20,16},{24,28},{28,24},{32,36},... | collective-permute-start | bytes 24584 | tf_op jit(solution)/shard_map/ppermute | solution.py:35
  30.7 6.6 %collective-permute-start.6 = (f32[2,16,128]{2,1,0:T(8,128)S(1)}, f32[2,16,128]{2,1,0:T(8,128)S(1)}, u32[]{:S(2)}, u32[]{:S(2)}) collective-permute-start(f32[2,16,128]{2,1,0:T(8,128)S(1)} %pad_maximum_fusion.behind_ref), channel_id=1, source_target_pairs={{0,124},{4,8},{8,4},{12,16},{16,12},{20,24},{24,20},{28,32},{32,28... | collective-permute-start | bytes 49160 | tf_op jit(solution)/shard_map/ppermute | solution.py:41
  37.3 1.7 %collective-permute-start.8 = (f32[8,128]{1,0:T(8,128)S(1)}, f32[8,128]{1,0:T(8,128)S(1)}, u32[]{:S(2)}, u32[]{:S(2)}) collective-permute-start(f32[8,128]{1,0:T(8,128)S(1)} %get-tuple-element.54), channel_id=1, source_target_pairs={{0,4},{4,0},{8,12},{12,8},{16,20},{20,16},{24,28},{28,24},{32,36},... | collective-permute-start | bytes 12296 | tf_op jit(solution)/shard_map/ppermute | solution.py:35
  37.4 12.0 %collective-permute-start.12 = (bf16[1024,256]{1,0:T(8,128)(2,1)S(1)}, bf16[1024,256]{1,0:T(8,128)(2,1)S(1)}, u32[]{:S(2)}, u32[]{:S(2)}) collective-permute-start(bf16[1024,256]{1,0:T(8,128)(2,1)S(1)} %get-tuple-element.41.own_ref), channel_id=1, source_target_pairs={{0,124},{4,8},{8,4},{12,16},{16,12},{20,24},{24,20},{28,32},{32,28... | collective-permute-start | bytes 1572872 | tf_op jit(solution)/shard_map/ppermute | solution.py:41
  39.0 10.4 %collective-permute-start.11 = (bf16[1024,256]{1,0:T(8,128)(2,1)S(1)}, bf16[1024,256]{1,0:T(8,128)(2,1)S(1)}, u32[]{:S(2)}, u32[]{:S(2)}) collective-permute-start(bf16[1024,256]{1,0:T(8,128)(2,1)S(1)} %get-tuple-element.41.own_ref), channel_id=1, source_target_pairs={{0,4},{4,0},{8,12},{12,8},{16,20},{20,16},{24,28},{28,24},{32,36},... | collective-permute-start | bytes 1572872 | tf_op jit(solution)/shard_map/ppermute | solution.py:35
  43.4 2.3 %collective-permute-start.9 = (f32[2,8,128]{2,1,0:T(8,128)S(1)}, f32[2,8,128]{2,1,0:T(8,128)S(1)}, u32[]{:S(2)}, u32[]{:S(2)}) collective-permute-start(f32[2,8,128]{2,1,0:T(8,128)S(1)} %get-tuple-element.56), channel_id=1, source_target_pairs={{0,4},{4,0},{8,12},{12,8},{16,20},{20,16},{24,28},{28,24},{32,36},... | collective-permute-start | bytes 24584 | tf_op jit(solution)/shard_map/ppermute | solution.py:35
  44.8 10.4 %collective-permute-start.15 = (bf16[1024,256]{1,0:T(8,128)(2,1)S(1)}, bf16[1024,256]{1,0:T(8,128)(2,1)S(1)}, u32[]{:S(2)}, u32[]{:S(2)}) collective-permute-start(bf16[1024,256]{1,0:T(8,128)(2,1)S(1)} %copy-done), channel_id=1, source_target_pairs={{0,4},{4,0},{8,12},{12,8},{16,20},{20,16},{24,28},{28,24},{32,36},... | collective-permute-start | bytes 1572872 | tf_op jit(solution)/shard_map/ppermute | solution.py:35
  45.7 7.7 %collective-permute-start.10 = (f32[2,16,128]{2,1,0:T(8,128)S(1)}, f32[2,16,128]{2,1,0:T(8,128)S(1)}, u32[]{:S(2)}, u32[]{:S(2)}) collective-permute-start(f32[2,16,128]{2,1,0:T(8,128)S(1)} %pad_maximum_fusion.1.behind_ref), channel_id=1, source_target_pairs={{0,124},{4,8},{8,4},{12,16},{16,12},{20,24},{24,20},{28,32},{32,28... | collective-permute-start | bytes 49160 | tf_op jit(solution)/shard_map/ppermute | solution.py:41
  53.5 1.2 %collective-permute-start.13 = (f32[8,128]{1,0:T(8,128)S(1)}, f32[8,128]{1,0:T(8,128)S(1)}, u32[]{:S(2)}, u32[]{:S(2)}) collective-permute-start(f32[8,128]{1,0:T(8,128)S(1)} %get-tuple-element.52), channel_id=1, source_target_pairs={{0,4},{4,0},{8,12},{12,8},{16,20},{20,16},{24,28},{28,24},{32,36},... | collective-permute-start | bytes 12296 | tf_op jit(solution)/shard_map/ppermute | solution.py:35
  54.7 4.9 %collective-permute-start.14 = (f32[24,128]{1,0:T(8,128)S(1)}, f32[24,128]{1,0:T(8,128)S(1)}, u32[]{:S(2)}, u32[]{:S(2)}) collective-permute-start(f32[24,128]{1,0:T(8,128)S(1)} %fusion.1.hh_ref.behind_ref), channel_id=1, source_target_pairs={{0,3},{1,2},{2,1},{3,0},{4,7},{5,6},{6,5},{7,4},{8,11},{9,10},{10,... | collective-permute-start | bytes 36872 | tf_op jit(solution)/shard_map/ppermute | solution.py:46
  65.0 6.6 %copy-start.1 = (bf16[1024,256]{1,0:T(8,128)(2,1)S(1)}, bf16[1024,256]{1,0:T(8,128)(2,1)}, u32[]{:S(2)}) copy-start(bf16[1024,256]{1,0:T(8,128)(2,1)} %get-tuple-element.24.own_ref) | copy-start | bytes 1572868
  65.0 6.5 %collective-permute-start.16 = (bf16[1024,256]{1,0:T(8,128)(2,1)}, bf16[1024,256]{1,0:T(8,128)(2,1)S(1)}, u32[]{:S(2)}, u32[]{:S(2)}) collective-permute-start(bf16[1024,256]{1,0:T(8,128)(2,1)} %get-tuple-element.24.own_ref), channel_id=1, source_target_pairs={{0,4},{4,0},{8,12},{12,8},{16,20},{20,16},{24,28},{28,24},{32,36},... | collective-permute-start | bytes 1572872 | tf_op jit(solution)/shard_map/ppermute | solution.py:35
  65.5 12.1 %collective-permute-start.17 = (bf16[1024,256]{1,0:T(8,128)(2,1)}, bf16[1024,256]{1,0:T(8,128)(2,1)S(1)}, u32[]{:S(2)}, u32[]{:S(2)}) collective-permute-start(bf16[1024,256]{1,0:T(8,128)(2,1)} %get-tuple-element.24.own_ref), channel_id=1, source_target_pairs={{0,124},{4,8},{8,4},{12,16},{16,12},{20,24},{24,20},{28,32},{32,28... | collective-permute-start | bytes 1572872 | tf_op jit(solution)/shard_map/ppermute | solution.py:41

commit v8 on v7

--- a/solution.py
+++ b/solution.py
@@ -88,21 +88,16 @@
         table_ref[GROUPS + s] = (count + QUAD - 1) >> 2
 
 
-def product_pair(source_ref, target_ref, g_ref, region, pair):
-    rows = target_ref[pl.ds(pl.multiple_of(pair * 256, 256), 256), :]
-    g = lax.dot_general(
-        source_ref[...], rows, (((1,), (1,)), ((), ())), preferred_element_type=jnp.float32
-    ) * (2.0 * SCALE)
-    g_ref[region * NBLK + 2 * pair] = g[:, :BLOCK]
-    g_ref[region * NBLK + 2 * pair + 1] = g[:, BLOCK:]
-
-
 def products(source_ref, target_refs, g_ref, first):
     for region, target_ref in enumerate(target_refs, first):
-
-        @pl.loop(0, NBLK // 2)
-        def _(pair):
-            product_pair(source_ref, target_ref, g_ref, region, pair)
+        g = lax.dot_general(
+            source_ref[...],
+            target_ref[:CELLS, :],
+            (((1,), (1,)), ((), ())),
+            preferred_element_type=jnp.float32,
+        ) * (2.0 * SCALE)
+        for block in range(NBLK):
+            g_ref[region * NBLK + block] = g[:, block * BLOCK : (block + 1) * BLOCK]
 
 
 def block_masses(mass_ref, group, first):
@@ -114,12 +109,14 @@
     return jnp.concatenate(rows, axis=0)
 
 
-def pack_kernel(place_ref, cells_hbm, mass_hbm, message_ref, mass_ref, sems):
+def pack_kernel(place_ref, cells_hbm, mass_hbm, message_ref, source_ref, mass_ref, sems):
     group = place_ref[1]
     cells = pltpu.make_async_copy(cells_hbm.at[group + 1], message_ref.at[:CELLS], sems.at[0])
     fetched = pltpu.make_async_copy(mass_hbm, mass_ref, sems.at[1])
+    source = pltpu.make_async_copy(cells_hbm.at[group], source_ref, sems.at[2])
+    fetched.start()
     cells.start()
-    fetched.start()
+    source.start()
     fetched.wait()
     masses = block_masses(mass_ref, group, 1) * LOG2E
     cells.wait()
@@ -145,6 +142,7 @@
         parts.append(jnp.zeros_like(left))
         packed = jnp.concatenate(parts, axis=0).astype(jnp.bfloat16)
         message_ref[CELLS:, half * BLOCK : (half + 1) * BLOCK] = packed
+    source.wait()
 
 
 def unpack(message_ref, window_ref, region):
@@ -288,33 +286,29 @@
 
 
 def chunks(body):
-    @pl.loop(0, 4)
-    def _(chunk):
-        body(pl.ds(pl.multiple_of(chunk * 256, 256), 256))
+    for chunk in range(2):
+        body(slice(chunk * 512, (chunk + 1) * 512))
 
 
 def near_kernel(place_ref, *refs):
-    *slot_refs, cells_hbm, mass_hbm, own_ref, sib_ref = refs[: len(refs) - 7]
-    g_ref, kc_ref, window_ref, source_ref, table_ref, mass_ref, sems = refs[len(refs) - 7 :]
+    *slot_refs, mass_hbm, source_ref, own_ref, sib_ref = refs[: len(refs) - 6]
+    g_ref, kc_ref, window_ref, table_ref, mass_ref, sem = refs[len(refs) - 6 :]
     group = place_ref[1]
-    copies = (
-        pltpu.make_async_copy(cells_hbm.at[group], source_ref, sems.at[0]),
-        pltpu.make_async_copy(mass_hbm, mass_ref, sems.at[1]),
-    )
-    for copy in copies:
-        copy.start()
+    fetched = pltpu.make_async_copy(mass_hbm, mass_ref, sem)
+    fetched.start()
     unpack(own_ref, window_ref, 0)
     unpack(sib_ref, window_ref, 1)
-    copies[0].wait()
-
-    def step(pair, counts):
-        product_pair(source_ref, own_ref, g_ref, 0, pair)
-        return enter_slots(place_ref, group, slot_refs, table_ref, pair, counts)
+
+    def step(quarter, counts):
+        return enter_slots(place_ref, group, slot_refs, table_ref, quarter, counts)
 
     zero = jnp.int32(0)
-    close_table(table_ref, lax.fori_loop(0, NBLK // 2, step, (zero, zero)))
-    products(source_ref, (sib_ref,), g_ref, 1)
-    copies[1].wait()
+    counts = (zero, zero)
+    for quarter in range(4):
+        counts = step(quarter, counts)
+    products(source_ref, (own_ref, sib_ref), g_ref, 0)
+    close_table(table_ref, counts)
+    fetched.wait()
     masses = block_masses(mass_ref, group, 0)
     for s in range(NBLK):
         x = source_ref[s * BLOCK : (s + 1) * BLOCK, :].astype(jnp.float32)
@@ -423,15 +417,15 @@
 
 
 def target_message(*args):
-    scratch = [MASSES, pltpu.SemaphoreType.DMA((2,))]
-    return call(pack_kernel, MESSAGE_SHAPE, VMEM, [SMEM, HBM, HBM], scratch)(*args)
+    scratch = [MASSES, pltpu.SemaphoreType.DMA((3,))]
+    return call(pack_kernel, (MESSAGE_SHAPE, FATE_SHAPE), (VMEM, VMEM), [SMEM, HBM, HBM], scratch)(*args)
 
 
 def near_products(place, slots, *args):
-    outs = (G_SHAPE, COLUMN_SHAPE, NEAR_SHAPE, FATE_SHAPE, TABLE_SHAPE)
-    in_specs = [SMEM] * (1 + len(slots)) + [HBM, HBM, VMEM, VMEM]
-    scratch = [MASSES, pltpu.SemaphoreType.DMA((2,))]
-    return call(near_kernel, outs, (VMEM,) * 4 + (SMEM,), in_specs, scratch)(place, *slots, *args)
+    outs = (G_SHAPE, COLUMN_SHAPE, NEAR_SHAPE, TABLE_SHAPE)
+    in_specs = [SMEM] * (1 + len(slots)) + [HBM, VMEM, VMEM, VMEM]
+    scratch = [MASSES, pltpu.SemaphoreType.DMA]
+    return call(near_kernel, outs, (VMEM,) * 3 + (SMEM,), in_specs, scratch)(place, *slots, *args)
 
 
 def far_products(*args):
@@ -513,12 +507,12 @@
     cells, masses = (
         pltpu.with_memory_space_constraint(array, pltpu.HBM) for array in (embeddings, log_mass)
     )
-    target = target_message(place, cells, masses)
+    target, source = target_message(place, cells, masses)
     target_out, target_sib = outward(target), sibling(target)
     slots, fates, target_sib = lax.optimization_barrier((tile_list, signatures, target_sib))
     fates_out, fates_sib = outward(fates), sibling(fates)
     gathered = [pltpu.with_memory_space_constraint(tile_list, pltpu.HBM)] + [shifted(slots, k) for k in range(1, lax.axis_size("tiles"))]
-    g, kc, near, source, table = near_products(place, gathered, cells, masses, target, target_sib)
+    g, kc, near, table = near_products(place, gathered, masses, source, target, target_sib)
     g, window, part = far_products(table, source, target_out, g, near, kc)
 
     totals, (table_other, other_source, other) = folded(

time: 79.5 us -> 75.8 us (0.953)
  Pallas kernels: 37.8 us -> 33.3 us
  starting transfers between devices: 22.7 us -> 23.9 us
  waiting for transfers between devices: 18.2 us -> 17.3 us
    ppermute x1, starting transfers between devices: 0.01 us -> 3.47 us  [mirrored(): lax.ppermute(value, 'tiles', [(t, count - 1 - t) for t in range(count)])]
    ppermute x1, waiting for transfers between devices: 4.42 us -> 1.2 us  [mirrored(): lax.ppermute(value, 'tiles', [(t, count - 1 - t) for t in range(count)])]
    ppermute x6, waiting for transfers between devices: 7.5 us -> 9.89 us  [outward(): return lax.ppermute(value, 'cells', pairs)]
    pallas_call x2, Pallas kernels: 7.91 us -> 5.66 us  [the longest x1 3.61 us: near_products(): call(near_kernel, outs, (VMEM,) * 3 + (SMEM,), in_specs, scratch)]
    pallas_call x1, Pallas kernels: 3.98 us -> 1.83 us  [other_products(): return call(other_kernel, G_SHAPE, VMEM, [ANY] + [VMEM] * 4)(*args)]
    pallas_call x1, Pallas kernels: 5.42 us -> 6.97 us  [late_fates(): call(late_kernel, outs, (VMEM, VMEM), in_specs, [COLUMN, TERMS, COLUMN],...]
    ppermute x8, starting transfers between devices: 2.41 us -> 0.93 us  [sibling(): lax.ppermute(value, 'cells', [(c, c ^ 1) for c in range(lax.axis_size('ce...]
  transfers between devices with their start and end apart: 18 -> 18, of which waited for: 9 -> 9; matrix products, arithmetic and copies ran while one was open for 0% -> 0% of each run, Pallas kernels for 36% -> 30%
where the time goes in v8:
time: 75.8 us; the launch traced here: 75.5 us
  Pallas kernels  33.3 us (44%)
  starting transfers between devices  23.9 us (32%)
  waiting for transfers between devices  17.3 us (23%)
  between operations  0.86 us (1%)
    ppermute x6, starting transfers between devices, outward(): return lax.ppermute(value, 'cells', pairs)  15 us
    ppermute x6, waiting for transfers between devices, outward(): return lax.ppermute(value, 'cells', pairs)  9.89 us
    pallas_call x1, Pallas kernels, late_fates(): call(late_kernel, outs, (VMEM, VMEM), in_specs, [COLUMN, TERMS, COLUMN],...  6.97 us
    pallas_call x1, Pallas kernels, far_products(): call(far_kernel, outs, (VMEM,) * 3, [SMEM] + [VMEM] * 5, SWEEP_SCRATCH, {...  5.06 us
    ppermute x3, starting transfers between devices, shifted(): lax.ppermute(value, 'tiles', [(t, (t + steps) % count) for t in range(cou...  4.45 us
    pallas_call x1, Pallas kernels, sweep(): call(sweep_kernel, PART_SHAPE, VMEM, [SMEM] + [VMEM] * 3, SWEEP_SCRATCH)  4.33 us
    pallas_call x1, Pallas kernels, early_weights(): call(early_weights_kernel, (W_SHAPE, COLUMN_SHAPE), (VMEM, VMEM), COUPLIN...  3.66 us
    pallas_call x1, Pallas kernels, near_products(): call(near_kernel, outs, (VMEM,) * 3 + (SMEM,), in_specs, scratch)  3.61 us
  transfers between devices with their start and end apart: 18, of which 9 were waited for; matrix products, arithmetic and copies ran while one was open for 0% of the time, Pallas kernels for 30%

profile of v8, /device:TPU:0, one launch (start us, length us, event | category | flops | bytes accessed | tf_op | source)
XLA Modules:
  0.0 75.5 jit_solution(7080750609486863566)
XLA Ops:
  0.7 2.0 %shard_map.59 = (bf16[1056,256]{1,0:T(8,128)(2,1)S(1)}, bf16[1024,256]{1,0:T(8,128)(2,1)S(1)}) custom-call(s32[2]{0:T(128)S(1)} %pad_add_fusion.place_ref, bf16[3,1024,256]{2,1,0:T(8,128)(2,1)} %refs_4_.3, f32[3,1024]{1,0:T(4,128)} %refs_4_.2), custom_call_target="tpu_custom_call" | custom-call | flops 3000000000 | bytes 10000 | tf_op jit(solution)/shard_map/pallas_call | solution.py:421
  2.8 0.1 collective-permute-start
  2.9 6.7 %collective-permute-start.4 = (bf16[1056,256]{1,0:T(8,128)(2,1)S(1)}, bf16[1056,256]{1,0:T(8,128)(2,1)S(1)}, u32[]{:S(2)}, u32[]{:S(2)}) collective-permute-start(bf16[1056,256]{1,0:T(8,128)(2,1)S(1)} %get-tuple-element.26.refs_6_), channel_id=1, source_target_pairs={{0,124},{4,8},{8,4},{12,16},{16,12},{20,24},{24,20},{28,32},{32,28... | collective-permute-start | bytes 1622024 | tf_op jit(solution)/shard_map/ppermute | solution.py:41
  9.6 2.8 %collective-permute-start.3 = (s32[2,2,32]{2,1,0:T(2,128)S(1)}, s32[2,2,32]{2,1,0:T(2,128)S(1)}, u32[]{:S(2)}, u32[]{:S(2)}) collective-permute-start(s32[2,2,32]{2,1,0:T(2,128)S(1)} %copy-done.2), channel_id=1, source_target_pairs={{0,3},{1,0},{2,1},{3,2},{4,7},{5,4},{6,5},{7,6},{8,11},{9,8},{10,9... | collective-permute-start | bytes 1544 | tf_op jit(solution)/shard_map/ppermute | solution.py:499
  12.3 0.8 %collective-permute-start.2 = (s32[2,2,32]{2,1,0:T(2,128)S(1)}, s32[2,2,32]{2,1,0:T(2,128)S(1)}, u32[]{:S(2)}, u32[]{:S(2)}) collective-permute-start(s32[2,2,32]{2,1,0:T(2,128)S(1)} %copy-done.2), channel_id=1, source_target_pairs={{0,2},{1,3},{2,0},{3,1},{4,6},{5,7},{6,4},{7,5},{8,10},{9,11},{10,... | collective-permute-start | bytes 1544 | tf_op jit(solution)/shard_map/ppermute | solution.py:499
  13.1 0.9 %collective-permute-start.1 = (s32[2,2,32]{2,1,0:T(2,128)S(1)}, s32[2,2,32]{2,1,0:T(2,128)S(1)}, u32[]{:S(2)}, u32[]{:S(2)}) collective-permute-start(s32[2,2,32]{2,1,0:T(2,128)S(1)} %copy-done.2), channel_id=1, source_target_pairs={{0,1},{1,2},{2,3},{3,0},{4,5},{5,6},{6,7},{7,4},{8,9},{9,10},{10,1... | collective-permute-start | bytes 1544 | tf_op jit(solution)/shard_map/ppermute | solution.py:499
  14.0 0.7 collective-permute-start.7
  14.7 2.7 %collective-permute-done.2.refs_2_ = s32[2,2,32]{2,1,0:T(2,128)S(1)} collective-permute-done((s32[2,2,32]{2,1,0:T(2,128)S(1)}, s32[2,2,32]{2,1,0:T(2,128)S(1)}, u32[]{:S(2)}, u32[]{:S(2)}) %collective-permute-start.2) | collective-permute-done | bytes 544 | tf_op jit(solution)/shard_map/ppermute | solution.py:499
  17.4 0.5 collective-permute-done.1.refs_1_
  17.9 3.6 %shard_map.60 = (f32[24,1024,128]{2,1,0:T(8,128)S(1)}, f32[1024,128]{1,0:T(8,128)S(1)}, f32[2,16,128]{2,1,0:T(8,128)S(1)}, s32[384]{0:T(512)S(1)}) custom-call(s32[2]{0:T(128)S(1)} %pad_add_fusion.place_ref, s32[2,2,32]{2,1,0:T(2,128)} %refs_0_.3, s32[2,2,32]{2,1,0:T(2,128)S(1)} %collective-permute-done.1.refs_1_, ...), custom_call_target="tpu_custom_call" | custom-call | flops 3000000000 | bytes 10000 | tf_op jit(solution)/shard_map/pallas_call | solution.py:428
  21.5 5.1 %shard_map.61 = (f32[24,1024,128]{2,1,0:T(8,128)S(1)}, f32[2,24,128]{2,1,0:T(8,128)S(1)}, f32[2,24,128]{2,1,0:T(8,128)S(1)}) custom-call(s32[384]{0:T(512)S(1)} %get-tuple-element.30.table_ref, bf16[1024,256]{1,0:T(8,128)(2,1)S(1)} %get-tuple-element.28.refs_5_.source_ref, ...), custom_call_target="tpu_custom_call", output_to_operand_aliasing={{0}: (3, {})} | custom-call | flops 3000000000 | bytes 10000 | tf_op jit(solution)/shard_map/pallas_call | solution.py:433
  26.7 1.2 %collective-permute-done.5 = f32[2,8,128]{2,1,0:T(8,128)S(1)} collective-permute-done((f32[2,8,128]{2,1,0:T(8,128)S(1)}, f32[2,8,128]{2,1,0:T(8,128)S(1)}, u32[]{:S(2)}, u32[]{:S(2)}) %collective-permute-start.5) | collective-permute-done | bytes 8224 | tf_op jit(solution)/shard_map/ppermute | solution.py:35
  27.9 1.1 %collective-permute-start.6 = (f32[2,16,128]{2,1,0:T(8,128)S(1)}, f32[2,16,128]{2,1,0:T(8,128)S(1)}, u32[]{:S(2)}, u32[]{:S(2)}) collective-permute-start(f32[2,16,128]{2,1,0:T(8,128)S(1)} %pad_maximum_fusion.behind_ref), channel_id=1, source_target_pairs={{0,124},{4,8},{8,4},{12,16},{16,12},{20,24},{24,20},{28,32},{32,28... | collective-permute-start | bytes 49160 | tf_op jit(solution)/shard_map/ppermute | solution.py:41
  29.0 2.6 %shard_map.62 = (s32[384]{0:T(512)S(1)}, bf16[1024,256]{1,0:T(8,128)(2,1)S(1)}, bf16[1024,256]{1,0:T(8,128)(2,1)S(1)}) custom-call(s32[2]{0:T(128)S(1)} %pad_add_fusion.place_ref, f32[2,16,128]{2,1,0:T(8,128)S(1)} %pad_maximum_fusion.behind_ref, bf16[1024,256]{1,0:T(8,128)(2,1)S(1)} %collective-permute-done.7.arrived_ref.out_ref, s32[2,2,32]{2,1,0:T(2,128)} %refs_0_.3, ...), custom_call_target="tpu_custom_call" | custom-call | flops 3000000000 | bytes 10000 | tf_op jit(solution)/shard_map/pallas_call | solution.py:448
  31.6 2.9 %collective-permute-done.6 = f32[2,16,128]{2,1,0:T(8,128)S(1)} collective-permute-done((f32[2,16,128]{2,1,0:T(8,128)S(1)}, f32[2,16,128]{2,1,0:T(8,128)S(1)}, u32[]{:S(2)}, u32[]{:S(2)}) %collective-permute-start.6) | collective-permute-done | bytes 16416 | tf_op jit(solution)/shard_map/ppermute | solution.py:41
  34.6 1.3 %collective-permute-start.12 = (bf16[1024,256]{1,0:T(8,128)(2,1)S(1)}, bf16[1024,256]{1,0:T(8,128)(2,1)S(1)}, u32[]{:S(2)}, u32[]{:S(2)}) collective-permute-start(bf16[1024,256]{1,0:T(8,128)(2,1)S(1)} %get-tuple-element.43.own_ref), channel_id=1, source_target_pairs={{0,124},{4,8},{8,4},{12,16},{16,12},{20,24},{24,20},{28,32},{32,28... | collective-permute-start | bytes 1572872 | tf_op jit(solution)/shard_map/ppermute | solution.py:41
  35.9 4.3 %shard_map.63 = f32[2,24,128]{2,1,0:T(8,128)S(1)} custom-call(s32[384]{0:T(512)S(1)} %get-tuple-element.30.table_ref, f32[24,128]{1,0:T(8,128)S(1)} %fusion.hh_ref, f32[1024,128]{1,0:T(8,128)S(1)} %get-tuple-element.33.kc_ref, f32[24,1024,128]{2,1,0:T(8,128)S(1)} %get-tuple-element.41.g_ref), custom_call_target="tpu_custom_call" | custom-call | flops 3000000000 | bytes 10000 | tf_op jit(solution)/shard_map/pallas_call | solution.py:437
  40.3 0.5 collective-permute-start.15
  40.8 0.7 collective-permute-done.9
  41.5 3.5 %collective-permute-start.10 = (f32[2,16,128]{2,1,0:T(8,128)S(1)}, f32[2,16,128]{2,1,0:T(8,128)S(1)}, u32[]{:S(2)}, u32[]{:S(2)}) collective-permute-start(f32[2,16,128]{2,1,0:T(8,128)S(1)} %pad_maximum_fusion.1.behind_ref), channel_id=1, source_target_pairs={{0,124},{4,8},{8,4},{12,16},{16,12},{20,24},{24,20},{28,32},{32,28... | collective-permute-start | bytes 49160 | tf_op jit(solution)/shard_map/ppermute | solution.py:41
  45.0 1.6 %collective-permute-done.12.out_ref = bf16[1024,256]{1,0:T(8,128)(2,1)S(1)} collective-permute-done((bf16[1024,256]{1,0:T(8,128)(2,1)S(1)}, bf16[1024,256]{1,0:T(8,128)(2,1)S(1)}, u32[]{:S(2)}, u32[]{:S(2)}) %collective-permute-start.12) | collective-permute-done | bytes 524320 | tf_op jit(solution)/shard_map/ppermute | solution.py:41
  46.6 1.8 %shard_map.64.g2_ref = f32[24,1024,128]{2,1,0:T(8,128)S(1)} custom-call(f32[2,16,128]{2,1,0:T(8,128)S(1)} %pad_maximum_fusion.1.behind_ref, bf16[1024,256]{1,0:T(8,128)(2,1)S(1)} %get-tuple-element.42.source_ref, bf16[1024,256]{1,0:T(8,128)(2,1)S(1)} %get-tuple-element.43.own_ref, bf16[1024,256]{1,0:T(8,128)(2,1)S(1)} %collective-permute-done.11.sib_ref, ...), custom_call_target="tpu_custom_call" | custom-call | flops 3000000000 | bytes 10000 | tf_op jit(solution)/shard_map/pallas_call | solution.py:441
  48.6 1.2 %collective-permute-done.13 = f32[8,128]{1,0:T(8,128)S(1)} collective-permute-done((f32[8,128]{1,0:T(8,128)S(1)}, f32[8,128]{1,0:T(8,128)S(1)}, u32[]{:S(2)}, u32[]{:S(2)}) %collective-permute-start.13) | collective-permute-done | bytes 4128 | tf_op jit(solution)/shard_map/ppermute | solution.py:35
  49.7 3.5 %collective-permute-start.14 = (f32[24,128]{1,0:T(8,128)S(1)}, f32[24,128]{1,0:T(8,128)S(1)}, u32[]{:S(2)}, u32[]{:S(2)}) collective-permute-start(f32[24,128]{1,0:T(8,128)S(1)} %fusion.1.hh_ref.behind_ref), channel_id=1, source_target_pairs={{0,3},{1,2},{2,1},{3,0},{4,7},{5,6},{6,5},{7,4},{8,11},{9,10},{10,... | collective-permute-start | bytes 36872 | tf_op jit(solution)/shard_map/ppermute | solution.py:46
  53.2 0.5 shard_map.66.blank_ref
  53.7 1.2 %collective-permute-done.14.hh2_ref = f32[24,128]{1,0:T(8,128)S(1)} collective-permute-done((f32[24,128]{1,0:T(8,128)S(1)}, f32[24,128]{1,0:T(8,128)S(1)}, u32[]{:S(2)}, u32[]{:S(2)}) %collective-permute-start.14) | collective-permute-done | bytes 12320 | tf_op jit(solution)/shard_map/ppermute | solution.py:46
  54.9 7.0 %shard_map.67 = (bf16[1024,256]{1,0:T(8,128)(2,1)}, bf16[1024,3200]{1,0:T(8,128)(2,1)S(1)}) custom-call(s32[2]{0:T(128)S(1)} %pad_add_fusion.place_ref, s32[384]{0:T(512)S(1)} %get-tuple-element.30.table_ref, f32[24,128]{1,0:T(8,128)S(1)} %fusion.1.hh_ref.behind_ref, f32[24,1024,128]{2,1,0:T(8,128)S(1)} %get-tuple-element.41.g_ref, ...), custom_call_target="tpu_custom_call", output_to_operand_aliasing={{1}: (10, {})} | custom-call | flops 3000000000 | bytes 10000 | tf_op jit(solution)/shard_map/pallas_call | solution.py:460
  61.8 1.8 %collective-permute-start.17 = (bf16[1024,256]{1,0:T(8,128)(2,1)}, bf16[1024,256]{1,0:T(8,128)(2,1)S(1)}, u32[]{:S(2)}, u32[]{:S(2)}) collective-permute-start(bf16[1024,256]{1,0:T(8,128)(2,1)} %get-tuple-element.25.own_ref), channel_id=1, source_target_pairs={{0,124},{4,8},{8,4},{12,16},{16,12},{20,24},{24,20},{28,32},{32,28... | collective-permute-start | bytes 1572872 | tf_op jit(solution)/shard_map/ppermute | solution.py:41
  63.7 3.7 %shard_map.65 = (bf16[1024,3200]{1,0:T(8,128)(2,1)S(1)}, f32[1024,128]{1,0:T(8,128)S(1)}) custom-call(s32[2]{0:T(128)S(1)} %pad_add_fusion.place_ref, s32[384]{0:T(512)S(1)} %get-tuple-element.30.table_ref, f32[24,128]{1,0:T(8,128)S(1)} %fusion.1.hh_ref.behind_ref, f32[24,1024,128]{2,1,0:T(8,128)S(1)} %get-tuple-element.41.g_ref, ...), custom_call_target="tpu_custom_call" | custom-call | flops 3000000000 | bytes 10000 | tf_op jit(solution)/shard_map/pallas_call | solution.py:464
  67.3 1.2 %shard_map.68.total_ref = f32[1024,256]{1,0:T(8,128)S(1)} custom-call(bf16[1024,3200]{1,0:T(8,128)(2,1)S(1)} %get-tuple-element.47.w_ref, bf16[1024,256]{1,0:T(8,128)(2,1)S(1)} %copy-done.1, bf16[1024,256]{1,0:T(8,128)(2,1)S(1)} %collective-permute-done.16.sib_ref), custom_call_target="tpu_custom_call" | custom-call | flops 3000000000 | bytes 10000 | tf_op jit(solution)/shard_map/pallas_call | solution.py:468
  68.6 5.4 %collective-permute-done.17.out_ref = bf16[1024,256]{1,0:T(8,128)(2,1)S(1)} collective-permute-done((bf16[1024,256]{1,0:T(8,128)(2,1)}, bf16[1024,256]{1,0:T(8,128)(2,1)S(1)}, u32[]{:S(2)}, u32[]{:S(2)}) %collective-permute-start.17) | collective-permute-done | bytes 524320 | tf_op jit(solution)/shard_map/ppermute | solution.py:41
  74.0 1.5 %shard_map.69 = bf16[1024,256]{1,0:T(8,128)(2,1)} custom-call(bf16[1024,3200]{1,0:T(8,128)(2,1)S(1)} %get-tuple-element.47.w_ref, f32[1024,128]{1,0:T(8,128)S(1)} %get-tuple-element.48.sum_ref, f32[1024,256]{1,0:T(8,128)S(1)} %shard_map.68.total_ref, bf16[1024,256]{1,0:T(8,128)(2,1)S(1)} %collective-permute-done.17.out_ref), custom_call_target="tpu_custom_call" | custom-call | flops 3000000000 | bytes 10000 | tf_op jit(solution)/shard_map/pallas_call | solution.py:472
  (32 shorter events, 0.6 us)
Async XLA Ops:
  0.6 8.9 %copy-start.2 = (s32[2,2,32]{2,1,0:T(2,128)S(1)}, s32[2,2,32]{2,1,0:T(2,128)}, u32[]{:S(2)}) copy-start(s32[2,2,32]{2,1,0:T(2,128)} %refs_0_.3) | copy-start | bytes 1540
  0.6 13.4 %copy-start = (bf16[1024,256]{1,0:T(8,128)(2,1)S(1)}, bf16[1024,256]{1,0:T(8,128)(2,1)}, u32[]{:S(2)}) copy-start(bf16[1024,256]{1,0:T(8,128)(2,1)} %own_ref.1) | copy-start | bytes 1572868
  2.8 6.8 %collective-permute-start = (bf16[1056,256]{1,0:T(8,128)(2,1)S(1)}, bf16[1056,256]{1,0:T(8,128)(2,1)S(1)}, u32[]{:S(2)}, u32[]{:S(2)}) collective-permute-start(bf16[1056,256]{1,0:T(8,128)(2,1)S(1)} %get-tuple-element.26.refs_6_), channel_id=1, source_target_pairs={{0,4},{4,0},{8,12},{12,8},{16,20},{20,16},{24,28},{28,24},{32,36},... | collective-permute-start | bytes 1622024 | tf_op jit(solution)/shard_map/ppermute | solution.py:35
  2.9 18.7 %collective-permute-start.4 = (bf16[1056,256]{1,0:T(8,128)(2,1)S(1)}, bf16[1056,256]{1,0:T(8,128)(2,1)S(1)}, u32[]{:S(2)}, u32[]{:S(2)}) collective-permute-start(bf16[1056,256]{1,0:T(8,128)(2,1)S(1)} %get-tuple-element.26.refs_6_), channel_id=1, source_target_pairs={{0,124},{4,8},{8,4},{12,16},{16,12},{20,24},{24,20},{28,32},{32,28... | collective-permute-start | bytes 1622024 | tf_op jit(solution)/shard_map/ppermute | solution.py:41
  9.6 5.2 %collective-permute-start.3 = (s32[2,2,32]{2,1,0:T(2,128)S(1)}, s32[2,2,32]{2,1,0:T(2,128)S(1)}, u32[]{:S(2)}, u32[]{:S(2)}) collective-permute-start(s32[2,2,32]{2,1,0:T(2,128)S(1)} %copy-done.2), channel_id=1, source_target_pairs={{0,3},{1,0},{2,1},{3,2},{4,7},{5,4},{6,5},{7,6},{8,11},{9,8},{10,9... | collective-permute-start | bytes 1544 | tf_op jit(solution)/shard_map/ppermute | solution.py:499
  12.3 5.1 %collective-permute-start.2 = (s32[2,2,32]{2,1,0:T(2,128)S(1)}, s32[2,2,32]{2,1,0:T(2,128)S(1)}, u32[]{:S(2)}, u32[]{:S(2)}) collective-permute-start(s32[2,2,32]{2,1,0:T(2,128)S(1)} %copy-done.2), channel_id=1, source_target_pairs={{0,2},{1,3},{2,0},{3,1},{4,6},{5,7},{6,4},{7,5},{8,10},{9,11},{10,... | collective-permute-start | bytes 1544 | tf_op jit(solution)/shard_map/ppermute | solution.py:499
  13.1 4.8 %collective-permute-start.1 = (s32[2,2,32]{2,1,0:T(2,128)S(1)}, s32[2,2,32]{2,1,0:T(2,128)S(1)}, u32[]{:S(2)}, u32[]{:S(2)}) collective-permute-start(s32[2,2,32]{2,1,0:T(2,128)S(1)} %copy-done.2), channel_id=1, source_target_pairs={{0,1},{1,2},{2,3},{3,0},{4,5},{5,6},{6,7},{7,4},{8,9},{9,10},{10,1... | collective-permute-start | bytes 1544 | tf_op jit(solution)/shard_map/ppermute | solution.py:499
  14.0 15.0 %collective-permute-start.7 = (bf16[1024,256]{1,0:T(8,128)(2,1)S(1)}, bf16[1024,256]{1,0:T(8,128)(2,1)S(1)}, u32[]{:S(2)}, u32[]{:S(2)}) collective-permute-start(bf16[1024,256]{1,0:T(8,128)(2,1)S(1)} %copy-done), channel_id=1, source_target_pairs={{0,124},{4,8},{8,4},{12,16},{16,12},{20,24},{24,20},{28,32},{32,28... | collective-permute-start | bytes 1572872 | tf_op jit(solution)/shard_map/ppermute | solution.py:41
  26.6 1.3 %collective-permute-start.5 = (f32[2,8,128]{2,1,0:T(8,128)S(1)}, f32[2,8,128]{2,1,0:T(8,128)S(1)}, u32[]{:S(2)}, u32[]{:S(2)}) collective-permute-start(f32[2,8,128]{2,1,0:T(8,128)S(1)} %get-tuple-element.60), channel_id=1, source_target_pairs={{0,4},{4,0},{8,12},{12,8},{16,20},{20,16},{24,28},{28,24},{32,36},... | collective-permute-start | bytes 24584 | tf_op jit(solution)/shard_map/ppermute | solution.py:35
  27.9 6.6 %collective-permute-start.6 = (f32[2,16,128]{2,1,0:T(8,128)S(1)}, f32[2,16,128]{2,1,0:T(8,128)S(1)}, u32[]{:S(2)}, u32[]{:S(2)}) collective-permute-start(f32[2,16,128]{2,1,0:T(8,128)S(1)} %pad_maximum_fusion.behind_ref), channel_id=1, source_target_pairs={{0,124},{4,8},{8,4},{12,16},{16,12},{20,24},{24,20},{28,32},{32,28... | collective-permute-start | bytes 49160 | tf_op jit(solution)/shard_map/ppermute | solution.py:41
  34.5 1.4 %collective-permute-start.8 = (f32[8,128]{1,0:T(8,128)S(1)}, f32[8,128]{1,0:T(8,128)S(1)}, u32[]{:S(2)}, u32[]{:S(2)}) collective-permute-start(f32[8,128]{1,0:T(8,128)S(1)} %get-tuple-element.56), channel_id=1, source_target_pairs={{0,4},{4,0},{8,12},{12,8},{16,20},{20,16},{24,28},{28,24},{32,36},... | collective-permute-start | bytes 12296 | tf_op jit(solution)/shard_map/ppermute | solution.py:35
  34.6 12.0 %collective-permute-start.12 = (bf16[1024,256]{1,0:T(8,128)(2,1)S(1)}, bf16[1024,256]{1,0:T(8,128)(2,1)S(1)}, u32[]{:S(2)}, u32[]{:S(2)}) collective-permute-start(bf16[1024,256]{1,0:T(8,128)(2,1)S(1)} %get-tuple-element.43.own_ref), channel_id=1, source_target_pairs={{0,124},{4,8},{8,4},{12,16},{16,12},{20,24},{24,20},{28,32},{32,28... | collective-permute-start | bytes 1572872 | tf_op jit(solution)/shard_map/ppermute | solution.py:41
  35.8 10.7 %collective-permute-start.11 = (bf16[1024,256]{1,0:T(8,128)(2,1)S(1)}, bf16[1024,256]{1,0:T(8,128)(2,1)S(1)}, u32[]{:S(2)}, u32[]{:S(2)}) collective-permute-start(bf16[1024,256]{1,0:T(8,128)(2,1)S(1)} %get-tuple-element.43.own_ref), channel_id=1, source_target_pairs={{0,4},{4,0},{8,12},{12,8},{16,20},{20,16},{24,28},{28,24},{32,36},... | collective-permute-start | bytes 1572872 | tf_op jit(solution)/shard_map/ppermute | solution.py:35
  40.2 1.3 %collective-permute-start.9 = (f32[2,8,128]{2,1,0:T(8,128)S(1)}, f32[2,8,128]{2,1,0:T(8,128)S(1)}, u32[]{:S(2)}, u32[]{:S(2)}) collective-permute-start(f32[2,8,128]{2,1,0:T(8,128)S(1)} %get-tuple-element.58), channel_id=1, source_target_pairs={{0,4},{4,0},{8,12},{12,8},{16,20},{20,16},{24,28},{28,24},{32,36},... | collective-permute-start | bytes 24584 | tf_op jit(solution)/shard_map/ppermute | solution.py:35
  40.3 13.4 %collective-permute-start.15 = (bf16[1024,256]{1,0:T(8,128)(2,1)S(1)}, bf16[1024,256]{1,0:T(8,128)(2,1)S(1)}, u32[]{:S(2)}, u32[]{:S(2)}) collective-permute-start(bf16[1024,256]{1,0:T(8,128)(2,1)S(1)} %copy-done), channel_id=1, source_target_pairs={{0,4},{4,0},{8,12},{12,8},{16,20},{20,16},{24,28},{28,24},{32,36},... | collective-permute-start | bytes 1572872 | tf_op jit(solution)/shard_map/ppermute | solution.py:35
  41.5 6.9 %collective-permute-start.10 = (f32[2,16,128]{2,1,0:T(8,128)S(1)}, f32[2,16,128]{2,1,0:T(8,128)S(1)}, u32[]{:S(2)}, u32[]{:S(2)}) collective-permute-start(f32[2,16,128]{2,1,0:T(8,128)S(1)} %pad_maximum_fusion.1.behind_ref), channel_id=1, source_target_pairs={{0,124},{4,8},{8,4},{12,16},{16,12},{20,24},{24,20},{28,32},{32,28... | collective-permute-start | bytes 49160 | tf_op jit(solution)/shard_map/ppermute | solution.py:41
  48.5 1.2 %collective-permute-start.13 = (f32[8,128]{1,0:T(8,128)S(1)}, f32[8,128]{1,0:T(8,128)S(1)}, u32[]{:S(2)}, u32[]{:S(2)}) collective-permute-start(f32[8,128]{1,0:T(8,128)S(1)} %get-tuple-element.54), channel_id=1, source_target_pairs={{0,4},{4,0},{8,12},{12,8},{16,20},{20,16},{24,28},{28,24},{32,36},... | collective-permute-start | bytes 12296 | tf_op jit(solution)/shard_map/ppermute | solution.py:35
  49.7 5.1 %collective-permute-start.14 = (f32[24,128]{1,0:T(8,128)S(1)}, f32[24,128]{1,0:T(8,128)S(1)}, u32[]{:S(2)}, u32[]{:S(2)}) collective-permute-start(f32[24,128]{1,0:T(8,128)S(1)} %fusion.1.hh_ref.behind_ref), channel_id=1, source_target_pairs={{0,3},{1,2},{2,1},{3,0},{4,7},{5,6},{6,5},{7,4},{8,11},{9,10},{10,... | collective-permute-start | bytes 36872 | tf_op jit(solution)/shard_map/ppermute | solution.py:46
  61.8 5.5 %copy-start.1 = (bf16[1024,256]{1,0:T(8,128)(2,1)S(1)}, bf16[1024,256]{1,0:T(8,128)(2,1)}, u32[]{:S(2)}) copy-start(bf16[1024,256]{1,0:T(8,128)(2,1)} %get-tuple-element.25.own_ref) | copy-start | bytes 1572868
  61.8 5.5 %collective-permute-start.16 = (bf16[1024,256]{1,0:T(8,128)(2,1)}, bf16[1024,256]{1,0:T(8,128)(2,1)S(1)}, u32[]{:S(2)}, u32[]{:S(2)}) collective-permute-start(bf16[1024,256]{1,0:T(8,128)(2,1)} %get-tuple-element.25.own_ref), channel_id=1, source_target_pairs={{0,4},{4,0},{8,12},{12,8},{16,20},{20,16},{24,28},{28,24},{32,36},... | collective-permute-start | bytes 1572872 | tf_op jit(solution)/shard_map/ppermute | solution.py:35
  61.8 12.1 %collective-permute-start.17 = (bf16[1024,256]{1,0:T(8,128)(2,1)}, bf16[1024,256]{1,0:T(8,128)(2,1)S(1)}, u32[]{:S(2)}, u32[]{:S(2)}) collective-permute-start(bf16[1024,256]{1,0:T(8,128)(2,1)} %get-tuple-element.25.own_ref), channel_id=1, source_target_pairs={{0,124},{4,8},{8,4},{12,16},{16,12},{20,24},{24,20},{28,32},{32,28... | collective-permute-start | bytes 1572872 | tf_op jit(solution)/shard_map/ppermute | solution.py:41
